TPU v7x, 32 devices: a whole 2x2x4 slice. The times are simulated.
32 devices in a mesh: fsdp: 8 (over y, x, core), sp: 4 (over z).
Axes of the slice: x: 2, y: 2, z: 4, core: 2. Of those that a mesh axis runs over, the one named last changes fastest.
Arguments:
- inputs: bfloat16 [32, 1024, 768], P('fsdp', 'sp'), may hold values from -6 to 6
- global_pos: int32 [32, 4], P('fsdp'), may hold values from 0 to 1023, as said below
- w_local: bfloat16 [3, 768, 768], P(None, 'fsdp'), may hold values from -0.21875 to 0.21875
- w_global: bfloat16 [3, 768, 768], P(None, 'fsdp'), may hold values from -0.3125 to 0.3125
- w_out: bfloat16 [768, 768], P('fsdp'), may hold values from -2.5 to 2.5
- b_proj: bfloat16 [6, 768], P(None, 'fsdp'), may hold values from -3 to 3
- gains: bfloat16 [2, 768], P(None, 'fsdp'), may hold values from 0.5 to 1.5
- shifts: bfloat16 [2, 768], P(None, 'fsdp'), may hold values from -3 to 3
- w_in: bfloat16 [768, 3072], P('fsdp'), may hold values from -0.21875 to 0.21875
- c_in: bfloat16 [3072], P('fsdp'), may hold values from -3 to 3
- w_back: bfloat16 [3072, 768], P('fsdp'), may hold values from -0.109375 to 0.109375
- cotangent: bfloat16 [32, 1024, 768], P('fsdp', 'sp'), may hold values from -6 to 6
Outputs:
- output: bfloat16 [32, 1024, 768], P('fsdp', 'sp')
- grad_inputs: bfloat16 [32, 1024, 768], P('fsdp', 'sp')
- grad_w_local: float32 [3, 768, 768], P(None, 'fsdp')
- grad_w_global: float32 [3, 768, 768], P(None, 'fsdp')
- grad_w_out: float32 [768, 768], P('fsdp')
- grad_b_proj: float32 [6, 768], P(None, 'fsdp')
- grad_gains: float32 [2, 768], P(None, 'fsdp')
- grad_shifts: float32 [2, 768], P(None, 'fsdp')
- grad_w_in: float32 [768, 3072], P('fsdp')
- grad_c_in: float32 [3072], P('fsdp')
- grad_w_back: float32 [3072, 768], P('fsdp')
Inputs may be any that keep to these rules, and one draw needn't show every extreme that they name: `global_pos`: in each sequence the 4 global positions are different; the first is 0 and the second is 1023.
All inputs are finite; a program needn't handle non-finite values.
Results may differ from a plain program's by a relative error of at most 0.017.
Values may be sent and summed in bfloat16 or wider, within the bound.
No kernel may reach another device: no remote copies, remote signals or barrier semaphores. Data moves between devices by JAX's collectives and lax.ppermute only.
A program may use at most 256 MiB of HBM per device.

v0:
```python
import jax
import jax.numpy as jnp
from jax import lax
from jax.sharding import PartitionSpec as P

HEADS = 12
HEAD_DIM = 64
WIN = 256
MICRO = 2


HIGHEST = lax.Precision.HIGHEST
MASKED_SCORE = -1000000000.0
NORM_EPS = 1e-05


def exact_gelu(values):
    return jax.nn.gelu(values, approximate=False)


def normalize(summed):
    center = summed - jnp.mean(summed, axis=-1, keepdims=True)
    inverse = lax.rsqrt(jnp.mean(center * center, axis=-1, keepdims=True) + NORM_EPS)
    return (center * inverse, inverse)


def norm_back(scaled, normed, inverse):
    return inverse * (
        scaled
        - jnp.mean(scaled, axis=-1, keepdims=True)
        - normed * jnp.mean(scaled * normed, axis=-1, keepdims=True)
    )


def project(tokens, matrix):
    return jnp.einsum("srd,de->sre", tokens, matrix, preferred_element_type=jnp.float32)


def back_project(gradient, matrix):
    return jnp.einsum("sre,de->srd", gradient, matrix, preferred_element_type=jnp.float32)


def outer_sum(tokens, gradient):
    return jnp.einsum("srd,sre->de", tokens, gradient, preferred_element_type=jnp.float32)


def row_total(values):
    return jnp.sum(values.astype(jnp.float32), axis=(0, 1))


def micro_step(tokens, positions, upstream_low, weights, sp_index, sp_count):
    w_local, w_global, w_out, b_proj, gains, shifts, w_in, c_in, w_back = weights
    batch_seqs, local_rows, model_width = tokens.shape
    glob_count = positions.shape[1]
    length = local_rows * sp_count
    local_heads = HEADS // sp_count
    head_cols = local_heads * HEAD_DIM
    score_scale = HEAD_DIM ** (-0.5)
    biases = b_proj.astype(jnp.float32)
    gain_rows = gains.astype(jnp.float32)
    shift_rows = shifts.astype(jnp.float32)
    queries = ((project(tokens, w_local[0]) + biases[0]) * score_scale).astype(jnp.bfloat16)
    key_loc = project(tokens, w_local[1]).astype(jnp.bfloat16)
    value_loc = (project(tokens, w_local[2]) + biases[1]).astype(jnp.bfloat16)
    key_glob = project(tokens, w_global[1]).astype(jnp.bfloat16)
    value_glob = (project(tokens, w_global[2]) + biases[3]).astype(jnp.bfloat16)
    stacked = jnp.stack([queries, key_loc, value_loc, key_glob, value_glob])
    spread = lax.all_to_all(stacked, "sp", split_axis=3, concat_axis=2, tiled=True)
    shaped = spread.reshape(5, batch_seqs, length, local_heads, HEAD_DIM)
    query_heads = shaped[0]
    key_heads = shaped[1]
    value_heads = shaped[2]
    key_glob_heads = shaped[3]
    value_glob_heads = shaped[4]
    own_places = sp_index * local_rows + jnp.arange(local_rows, dtype=jnp.int32)
    pick_rows = (positions[:, :, None] == own_places[None, None, :]).astype(jnp.bfloat16)
    rows_part = jnp.einsum("sgr,srd->sgd", pick_rows, tokens, preferred_element_type=jnp.float32)
    rows_glob = lax.psum(rows_part.astype(jnp.bfloat16), "sp")
    query_cols = lax.dynamic_slice_in_dim(w_global[0], sp_index * head_cols, head_cols, 1)
    query_bias = lax.dynamic_slice_in_dim(biases[2], sp_index * head_cols, head_cols, 0)
    query_glob = (
        (
            jnp.einsum("sgd,dc->sgc", rows_glob, query_cols, preferred_element_type=jnp.float32)
            + query_bias
        )
        * score_scale
    ).astype(jnp.bfloat16)
    query_glob_heads = query_glob.reshape(batch_seqs, glob_count, local_heads, HEAD_DIM)
    places = jnp.arange(length, dtype=jnp.int32)
    select = positions[:, :, None] == places[None, None, :]
    select_low = select.astype(jnp.bfloat16)
    select_full = select.astype(jnp.float32)
    is_glob = jnp.sum(select_full, axis=1)
    keep_local = 1.0 - is_glob
    block_rows = min(512, length)
    offsets = list(range(0, length, block_rows))

    def block_scores(offset):
        query_block = query_heads[:, offset : offset + block_rows]
        row_places = offset + jnp.arange(block_rows, dtype=jnp.int32)
        in_band = jnp.abs(row_places[:, None] - places[None, :]) <= WIN
        allowed = in_band[None, None, :, :] | (is_glob[:, None, None, :] > 0.5)
        raw_scores = jnp.einsum(
            "sihe,sjhe->shij", query_block, key_heads, preferred_element_type=jnp.float32
        )
        return (query_block, jnp.where(allowed, raw_scores, MASKED_SCORE))

    kept_tops = []
    kept_sums = []
    contexts = []
    for offset in offsets:
        query_block, masked = block_scores(offset)
        row_top = jnp.max(masked, axis=-1, keepdims=True)
        powers = jnp.exp(masked - row_top)
        row_sum = jnp.sum(powers, axis=-1, keepdims=True)
        probs_low = (powers / row_sum).astype(jnp.bfloat16)
        contexts.append(
            jnp.einsum(
                "shij,sjhe->sihe", probs_low, value_heads, preferred_element_type=jnp.float32
            )
        )
        kept_tops.append(row_top)
        kept_sums.append(row_sum)
    context_loc = jnp.concatenate(contexts, axis=1)
    glob_scores = jnp.einsum(
        "sghe,sjhe->shgj", query_glob_heads, key_glob_heads, preferred_element_type=jnp.float32
    )
    glob_powers = jnp.exp(glob_scores - jnp.max(glob_scores, axis=-1, keepdims=True))
    glob_probs = glob_powers / jnp.sum(glob_powers, axis=-1, keepdims=True)
    glob_low = glob_probs.astype(jnp.bfloat16)
    context_glob = jnp.einsum(
        "shgj,sjhe->sghe", glob_low, value_glob_heads, preferred_element_type=jnp.float32
    )
    context = context_loc * keep_local[:, :, None, None] + jnp.einsum(
        "sgl,sghe->slhe", select_full, context_glob, precision=HIGHEST
    )
    merged = context.astype(jnp.bfloat16).reshape(batch_seqs, length, head_cols)
    ctx_tokens = lax.all_to_all(merged, "sp", split_axis=1, concat_axis=2, tiled=True)
    attended = project(ctx_tokens, w_out) + biases[4]
    normed_one, inverse_one = normalize(tokens.astype(jnp.float32) + attended)
    first_norm = normed_one * gain_rows[0] + shift_rows[0]
    first_low = first_norm.astype(jnp.bfloat16)
    ffn_inner = project(first_low, w_in) + c_in.astype(jnp.float32)
    active = exact_gelu(ffn_inner).astype(jnp.bfloat16)
    branch = project(active, w_back) + biases[5]
    normed_two, inverse_two = normalize(first_norm + branch)
    result = normed_two * gain_rows[1] + shift_rows[1]
    upstream = upstream_low.astype(jnp.float32)
    grad_gain_two = jnp.sum(upstream * normed_two, axis=(0, 1))
    grad_shift_two = jnp.sum(upstream, axis=(0, 1))
    grad_second = norm_back(upstream * gain_rows[1], normed_two, inverse_two)
    branch_grad = grad_second.astype(jnp.bfloat16)
    grad_back_w = outer_sum(active, branch_grad)
    grad_out_bias = row_total(branch_grad)
    grad_active = back_project(branch_grad, w_back)
    unused, gelu_pull = jax.vjp(exact_gelu, ffn_inner)
    inner_grad = gelu_pull(grad_active)[0].astype(jnp.bfloat16)
    grad_in_w = outer_sum(first_low, inner_grad)
    grad_in_bias = row_total(inner_grad)
    grad_first = grad_second + back_project(inner_grad, w_in)
    grad_gain_one = jnp.sum(grad_first * normed_one, axis=(0, 1))
    grad_shift_one = jnp.sum(grad_first, axis=(0, 1))
    grad_sum_one = norm_back(grad_first * gain_rows[0], normed_one, inverse_one)
    attn_grad = grad_sum_one.astype(jnp.bfloat16)
    grad_out_w = outer_sum(ctx_tokens, attn_grad)
    grad_att_bias = row_total(attn_grad)
    merged_grad = back_project(attn_grad, w_out).astype(jnp.bfloat16)
    ctx_grad = lax.all_to_all(merged_grad, "sp", split_axis=2, concat_axis=1, tiled=True).reshape(
        batch_seqs, length, local_heads, HEAD_DIM
    )
    local_grad = (ctx_grad.astype(jnp.float32) * keep_local[:, :, None, None]).astype(jnp.bfloat16)
    glob_ctx_grad = jnp.einsum(
        "sgl,slhe->sghe", select_low, ctx_grad, preferred_element_type=jnp.float32
    ).astype(jnp.bfloat16)
    key_grad = jnp.zeros(key_heads.shape, jnp.float32)
    value_grad = jnp.zeros(value_heads.shape, jnp.float32)
    query_parts = []
    for block_index, offset in enumerate(offsets):
        query_block, masked = block_scores(offset)
        probs_full = jnp.exp(masked - kept_tops[block_index]) / kept_sums[block_index]
        probs_low = probs_full.astype(jnp.bfloat16)
        grad_block = local_grad[:, offset : offset + block_rows]
        grad_probs = jnp.einsum(
            "sihe,sjhe->shij", grad_block, value_heads, preferred_element_type=jnp.float32
        )
        inner_dot = jnp.sum(probs_full * grad_probs, axis=-1, keepdims=True)
        score_grad = (probs_full * (grad_probs - inner_dot)).astype(jnp.bfloat16)
        query_parts.append(
            jnp.einsum("shij,sjhe->sihe", score_grad, key_heads, preferred_element_type=jnp.float32)
        )
        key_grad = key_grad + jnp.einsum(
            "shij,sihe->sjhe", score_grad, query_block, preferred_element_type=jnp.float32
        )
        value_grad = value_grad + jnp.einsum(
            "shij,sihe->sjhe", probs_low, grad_block, preferred_element_type=jnp.float32
        )
    query_grad = jnp.concatenate(query_parts, axis=1).astype(jnp.bfloat16)
    glob_grad_probs = jnp.einsum(
        "sghe,sjhe->shgj", glob_ctx_grad, value_glob_heads, preferred_element_type=jnp.float32
    )
    glob_inner = jnp.sum(glob_probs * glob_grad_probs, axis=-1, keepdims=True)
    glob_score_grad = (glob_probs * (glob_grad_probs - glob_inner)).astype(jnp.bfloat16)
    query_glob_grad = jnp.einsum(
        "shgj,sjhe->sghe", glob_score_grad, key_glob_heads, preferred_element_type=jnp.float32
    ).astype(jnp.bfloat16)
    key_glob_grad = jnp.einsum(
        "shgj,sghe->sjhe", glob_score_grad, query_glob_heads, preferred_element_type=jnp.float32
    ).astype(jnp.bfloat16)
    value_glob_grad = jnp.einsum(
        "shgj,sghe->sjhe", glob_low, glob_ctx_grad, preferred_element_type=jnp.float32
    ).astype(jnp.bfloat16)
    heads_grad = jnp.stack(
        [
            query_grad,
            key_grad.astype(jnp.bfloat16),
            value_grad.astype(jnp.bfloat16),
            key_glob_grad,
            value_glob_grad,
        ]
    ).reshape(5, batch_seqs, length, head_cols)
    token_side = lax.all_to_all(heads_grad, "sp", split_axis=2, concat_axis=3, tiled=True)
    pre_query = token_side[0] * score_scale
    glob_pre = query_glob_grad.reshape(batch_seqs, glob_count, head_cols) * score_scale
    rows_grad_part = jnp.einsum(
        "sgc,dc->sgd", glob_pre, query_cols, preferred_element_type=jnp.float32
    )
    rows_grad = lax.psum(rows_grad_part, "sp")
    token_grad = (
        grad_sum_one + back_project(pre_query, w_local[0]) + back_project(token_side[1], w_local[1])
    )
    token_grad = (
        token_grad
        + back_project(token_side[2], w_local[2])
        + back_project(token_side[3], w_global[1])
    )
    token_grad = token_grad + back_project(token_side[4], w_global[2])
    token_grad = token_grad + jnp.einsum(
        "sgr,sgd->srd", pick_rows.astype(jnp.float32), rows_grad, precision=HIGHEST
    )
    grad_local = jnp.stack(
        [
            outer_sum(tokens, pre_query),
            outer_sum(tokens, token_side[1]),
            outer_sum(tokens, token_side[2]),
        ]
    )
    glob_cols_grad = jnp.einsum(
        "sgd,sgc->dc", rows_glob, glob_pre, preferred_element_type=jnp.float32
    )
    glob_weight_grad = lax.dynamic_update_slice_in_dim(
        jnp.zeros((model_width, model_width), jnp.float32), glob_cols_grad, sp_index * head_cols, 1
    )
    grad_global = jnp.stack(
        [glob_weight_grad, outer_sum(tokens, token_side[3]), outer_sum(tokens, token_side[4])]
    )
    glob_bias_grad = lax.dynamic_update_slice_in_dim(
        jnp.zeros((model_width,), jnp.float32), row_total(glob_pre), sp_index * head_cols, 0
    )
    grad_bias = jnp.stack(
        [
            row_total(pre_query),
            row_total(token_side[2]),
            glob_bias_grad,
            row_total(token_side[4]),
            grad_att_bias,
            grad_out_bias,
        ]
    )
    grad_gain = jnp.stack([grad_gain_one, grad_gain_two])
    grad_shift = jnp.stack([grad_shift_one, grad_shift_two])
    gradients = (
        grad_local,
        grad_global,
        grad_out_w,
        grad_bias,
        grad_gain,
        grad_shift,
        grad_in_w,
        grad_in_bias,
        grad_back_w,
    )
    return (result.astype(jnp.bfloat16), token_grad.astype(jnp.bfloat16), gradients)


def per_device(
    inputs,
    global_pos,
    w_local,
    w_global,
    w_out,
    b_proj,
    gains,
    shifts,
    w_in,
    c_in,
    w_back,
    cotangent,
):
    sp_count = lax.axis_size("sp")
    sp_index = lax.axis_index("sp")
    batch_seqs = inputs.shape[0] // MICRO
    outputs = []
    input_grads = []
    totals = None
    for micro_index in range(MICRO):
        weights = (
            lax.all_gather(w_local, "fsdp", axis=1, tiled=True),
            lax.all_gather(w_global, "fsdp", axis=1, tiled=True),
            lax.all_gather(w_out, "fsdp", axis=0, tiled=True),
            lax.all_gather(b_proj, "fsdp", axis=1, tiled=True),
            lax.all_gather(gains, "fsdp", axis=1, tiled=True),
            lax.all_gather(shifts, "fsdp", axis=1, tiled=True),
            lax.all_gather(w_in, "fsdp", axis=0, tiled=True),
            lax.all_gather(c_in, "fsdp", axis=0, tiled=True),
            lax.all_gather(w_back, "fsdp", axis=0, tiled=True),
        )
        first_seq = micro_index * batch_seqs
        end_seq = first_seq + batch_seqs
        result, token_grads, gradients = micro_step(
            inputs[first_seq:end_seq],
            global_pos[first_seq:end_seq],
            cotangent[first_seq:end_seq],
            weights,
            sp_index,
            sp_count,
        )
        if totals is None:
            totals = tuple(gradients)
        else:
            totals = tuple((earlier + later for earlier, later in zip(totals, gradients)))
        outputs.append(result)
        input_grads.append(token_grads)
    totals = (
        lax.psum_scatter(totals[0], "fsdp", scatter_dimension=1, tiled=True),
        lax.psum_scatter(totals[1], "fsdp", scatter_dimension=1, tiled=True),
        lax.psum_scatter(totals[2], "fsdp", scatter_dimension=0, tiled=True),
        lax.psum_scatter(totals[3], "fsdp", scatter_dimension=1, tiled=True),
        lax.psum_scatter(totals[4], "fsdp", scatter_dimension=1, tiled=True),
        lax.psum_scatter(totals[5], "fsdp", scatter_dimension=1, tiled=True),
        lax.psum_scatter(totals[6], "fsdp", scatter_dimension=0, tiled=True),
        lax.psum_scatter(totals[7], "fsdp", scatter_dimension=0, tiled=True),
        lax.psum_scatter(totals[8], "fsdp", scatter_dimension=0, tiled=True),
    )
    summed = (
        lax.psum(totals[0].astype(jnp.bfloat16), "sp").astype(jnp.float32),
        lax.psum(totals[1].astype(jnp.bfloat16), "sp").astype(jnp.float32),
        lax.psum(totals[2].astype(jnp.bfloat16), "sp").astype(jnp.float32),
        lax.psum(totals[3].astype(jnp.bfloat16), "sp").astype(jnp.float32),
        lax.psum(totals[4].astype(jnp.bfloat16), "sp").astype(jnp.float32),
        lax.psum(totals[5].astype(jnp.bfloat16), "sp").astype(jnp.float32),
        lax.psum(totals[6].astype(jnp.bfloat16), "sp").astype(jnp.float32),
        lax.psum(totals[7].astype(jnp.bfloat16), "sp").astype(jnp.float32),
        lax.psum(totals[8].astype(jnp.bfloat16), "sp").astype(jnp.float32),
    )
    return (
        jnp.concatenate(outputs, axis=0),
        jnp.concatenate(input_grads, axis=0),
        summed[0],
        summed[1],
        summed[2],
        summed[3],
        summed[4],
        summed[5],
        summed[6],
        summed[7],
        summed[8],
    )


def solution(mesh):
    placed = (
        P("fsdp", "sp", None),
        P("fsdp", None),
        P(None, "fsdp", None),
        P(None, "fsdp", None),
        P("fsdp", None),
        P(None, "fsdp"),
        P(None, "fsdp"),
        P(None, "fsdp"),
        P("fsdp", None),
        P("fsdp"),
        P("fsdp", None),
        P("fsdp", "sp", None),
    )
    return jax.shard_map(
        per_device,
        mesh=mesh,
        in_specs=placed,
        out_specs=(
            P("fsdp", "sp", None),
            P("fsdp", "sp", None),
            P(None, "fsdp", None),
            P(None, "fsdp", None),
            P("fsdp", None),
            P(None, "fsdp"),
            P(None, "fsdp"),
            P(None, "fsdp"),
            P("fsdp", None),
            P("fsdp"),
            P("fsdp", None),
        ),
        check_vma=False,
    )
```

profile of v0, /device:TPU:0, one launch (start us, length us, event | category | flops | bytes accessed | tf_op | source)
XLA Modules:
  0.0 1283.1 jit_solution(14808843915681914736)
XLA Ops:
  10.0 10.5 all-gather
  20.6 8.6 all-gather.1
  29.9 16.7 %all-gather.10.cloned.1.call-done = bf16[3,768,768]{2,1,0:T(8,128)(2,1)} async-done(((bf16[3,96,768]{2,1,0:T(8,128)(2,1)}), bf16[3,768,768]{2,1,0:T(8,128)(2,1)}) %all-gather.10.cloned.1.call-update) | async-done | bytes 3538960 | tf_op jit(solution)/shard_map/all_gather | solution.py:307
  53.4 29.2 %all-gather.12.cloned.1.call-done = bf16[3,768,768]{2,1,0:T(8,128)(2,1)} async-done(((bf16[3,96,768]{2,1,0:T(8,128)(2,1)}), bf16[3,768,768]{2,1,0:T(8,128)(2,1)}) %all-gather.12.cloned.1.call-update) | async-done | bytes 3538960 | tf_op jit(solution)/shard_map/all_gather | solution.py:308
  88.4 10.6 copy.324
  99.0 5.0 all-to-all-start
  104.7 8.7 all-gather.2
  114.0 87.2 %all-reduce.3 = (bf16[2,4,768]{2,1,0:T(4,128)(2,1)S(1)}, bf16[2,4,768]{2,1,0:T(4,128)(2,1)S(1)}) all-reduce(bf16[2,4,768]{2,1,0:T(4,128)(2,1)S(1)} %convolution_convert_fusion.15, bf16[2,4,768]{2,1,0:T(4,128)(2,1)S(1)} %convolution_convert_fusion.14), channel_id=1, replica_groups=mesh['fsdp'=8,'sp'=4] {'sp'}, use_global_device_ids=true, to_apply=%region_5.6 | all-reduce | flops 12288 | bytes 49152 | tf_op jit(solution)/shard_map/psum | solution.py:78
  217.6 10.6 copy.339
  228.6 5.1 all-to-all-start.2
  263.4 8.2 fusion.311
  271.6 8.5 fusion.306
  280.2 6.1 fusion.124
  294.4 23.9 %all-to-all-done.2 = bf16[5,2,256,768]{2,1,0,3:T(2,128)(2,1)} async-done(((bf16[5,2,256,768]{2,1,0,3:T(2,128)(2,1)}), bf16[5,2,256,768]{2,1,0,3:T(2,128)(2,1)}, u32[]{:S(2)}, u32[]{:S(2)}) %all-to-all-start.2) | async-done | bytes 3932192 | tf_op jit(solution)/shard_map/all_to_all | solution.py:68
  338.4 10.6 fusion.323
  348.9 10.1 fusion.318
  371.8 6.3 fusion.130
  378.1 5.8 fusion.133
  386.9 5.1 all-to-all-start.3
  392.0 8.9 all-gather.3
  407.0 9.7 all-to-all-done.3
  422.7 5.1 fusion.50
  427.9 13.3 %fusion.94 = (u8[256,3072]{1,0:T(8,128)(4,1)}, u8[256,3072]{1,0:T(8,128)(4,1)}, u8[256,3072]{1,0:T(8,128)(4,1)}, u8[256,3072]{1,0:T(8,128)(4,1)}, f32[2,256,3072]{2,1,0:T(8,128)S(1)}) fusion(f32[3072]{0:T(1024)S(1)} %bitcast.566, f32[2,256,3072]{2,1,0:T(8,128)S(1)} %fusion.50, bf16[768,3072]{1,0:T(8,128)(2,1)} %all-gather.16.cloned.1.call-done, ...), kind=kOutput, calls=%fused_computation.206 | convolution fusion | flops 2458779648 | bytes 22042624 | tf_op jit(solution)/shard_map/srd,de->sre/dot_general | solution.py:36
  443.8 32.6 %multiply_convert_fusion.5 = (bf16[2,256,3072]{2,1,0:T(8,128)(2,1)}, f32[2,256,3072]{2,1,0:T(8,128)}, bf16[2,256,3072]{2,1,0:T(8,128)(2,1)}, f32[2,256,3072]{2,1,0:T(8,128)}) fusion(f32[2,256,3072]{2,1,0:T(8,128)S(1)} %get-tuple-element.203, f32[3072]{0:T(1024)S(1)} %bitcast.567, u8[256,3072]{1,0:T(8,128)(4,1)} %get-tuple-element.78, ...), kind=kLoop, calls=%fused_computation.62 | loop fusion | flops 221773824 | bytes 34615296 | tf_op jit(solution)/shard_map/convert_element_type | solution.py:144
  476.5 6.2 fusion.331
  491.2 13.0 %convert_reduce_fusion.1 = (f32[3072]{0:T(1024)}, bf16[2,256,3072]{2,1,0:T(8,128)(2,1)}) fusion(f32[2,256,3072]{2,1,0:T(8,128)} %get-tuple-element.144, bf16[2,256,768]{2,1,0:T(8,128)(2,1)} %get-tuple-element.171, bf16[3072,768]{1,0:T(8,128)(2,1)} %all-gather.18.cloned.1.call-done, f32[2,256,3072]{2,1,0:T(8,128)} %copy-done.18, f32[3072]{0:T(1024)S(1)} %bitcast.568), kind=kOutput, calls=%fused_computation.44 | convolution fusion | flops 2442654720 | bytes 21258240 | tf_op jit(solution)/shard_map/sre,de->srd/dot_general | solution.py:40
  504.3 7.8 multiply_reduce_fusion.5
  512.2 9.5 convert_reduce_fusion
  521.7 8.9 convert_reduce_fusion.10
  542.2 5.0 fusion.333
  547.2 5.3 bitcast_add_fusion
  563.1 7.3 fusion.268
  573.0 8.8 bitcast_add_fusion.1
  590.4 6.9 fusion.54
  597.3 9.2 multiply_reduce_fusion.1
  606.6 7.2 multiply_convert_fusion.1
  617.9 6.4 multiply_reduce_fusion
  629.7 7.0 fusion.62
  636.8 9.4 multiply_reduce_fusion.3
  657.4 10.4 add_convert_fusion.3
  671.4 9.8 multiply_convert_fusion
  703.2 5.8 all-to-all-start.7
  710.7 6.2 add_convert_fusion.6
  717.8 9.4 multiply_convert_fusion.3
  731.3 12.0 multiply_reduce_fusion.2
  744.6 6.7 multiply_convert_fusion.2
  757.9 5.6 convolution_convert_fusion.13
  764.9 5.9 convolution_convert_fusion.12
  787.6 35.4 %all-to-all-done.7 = bf16[5,2,1024,192]{3,1,0,2:T(2,128)(2,1)} async-done(((bf16[5,2,1024,192]{3,1,0,2:T(2,128)(2,1)}), bf16[5,2,1024,192]{3,1,0,2:T(2,128)(2,1)}, u32[]{:S(2)}, u32[]{:S(2)}) %all-to-all-start.7) | async-done | bytes 3932192 | tf_op jit(solution)/shard_map/all_to_all | solution.py:221
  823.1 5.1 all-to-all-start.5
  834.5 14.5 %copy.428 = bf16[5,2,4,256,192]{3,2,4,1,0:T(4,128)(2,1)} copy(bf16[5,2,4,256,192]{4,1,0,3,2:T(2,128)(2,1)} %bitcast.98) | data formatting | bytes 7864320 | tf_op jit(solution)/shard_map/all_to_all | solution.py:221
  849.0 94.3 %all-to-all-done.5 = bf16[5,2,1024,192]{3,1,0,2:T(2,128)(2,1)} async-done(((bf16[5,2,1024,192]{3,1,0,2:T(2,128)(2,1)}), bf16[5,2,1024,192]{3,1,0,2:T(2,128)(2,1)}, u32[]{:S(2)}, u32[]{:S(2)}) %all-to-all-start.5) | async-done | bytes 3932192 | tf_op jit(solution)/shard_map/all_to_all | solution.py:221
  943.3 14.3 %copy.427 = bf16[5,2,4,256,192]{3,2,4,1,0:T(4,128)(2,1)} copy(bf16[5,2,4,256,192]{4,1,0,3,2:T(2,128)(2,1)} %bitcast.75) | data formatting | bytes 7864320 | tf_op jit(solution)/shard_map/all_to_all | solution.py:221
  968.7 4.9 maximum_add_fusion.1
  973.6 11.0 copy.431
  984.6 8.2 copy.440
  1005.3 11.1 copy.429
  1016.4 8.2 copy.439
  1026.6 23.4 %all-reduce = bf16[3072]{0:T(1024)(128)(2,1)S(1)} all-reduce(f32[3072]{0:T(1024)S(1)} %add.429), channel_id=9, replica_groups=mesh['fsdp'=8,'sp'=4] {'fsdp'}, use_global_device_ids=true, to_apply=%region_76.77.clone | all-reduce | flops 3072 | bytes 18432
  1055.6 18.4 %all-reduce.1 = (f32[2,4,768]{2,1,0:T(4,128)S(1)}, f32[2,4,768]{2,1,0:T(4,128)S(1)}) all-reduce(f32[2,4,768]{2,1,0:T(4,128)S(1)} %fusion.182, f32[2,4,768]{2,1,0:T(4,128)S(1)} %fusion.184), channel_id=1, replica_groups=mesh['fsdp'=8,'sp'=4] {'sp'}, use_global_device_ids=true, to_apply=%region_39.40 | all-reduce | flops 12288 | bytes 98304 | tf_op jit(solution)/shard_map/psum | solution.py:227
  1108.6 16.8 %reduce-scatter.25.cloned.1.call-done = f32[96,2304]{1,0:T(8,128)} async-done(((f32[768,2304]{1,0:T(8,128)}), f32[96,2304]{1,0:T(8,128)}) %reduce-scatter.25.cloned.1.call-update) | async-done | bytes 884752
  1141.2 21.4 %reduce-scatter.29.cloned.1.call-done = f32[96,6]{1,0:T(8,128)} async-done(((f32[768,6]{1,0:T(8,128)}), f32[96,6]{1,0:T(8,128)}) %reduce-scatter.29.cloned.1.call-update) | async-done | bytes 2320
  1163.5 11.8 all-reduce.2
  1177.6 91.1 %all-reduce.7.cloned.1.call-done = (bf16[3,96,768]{1,2,0:T(8,128)(2,1)}, bf16[3,96,768]{1,2,0:T(8,128)(2,1)}, bf16[96,768]{1,0:T(8,128)(2,1)}, bf16[96,3072]{1,0:T(8,128)(2,1)}, bf16[384,768]{1,0:T(8,128)(2,1)}) async-done(((bf16[3,96,768]{1,2,0:T(8,128)(2,1)}, bf16[3,96,768]{1,2,0:T(8,128)(2,1)}, bf16[96,768]{1,0:T(8,128)(2,1)}, bf16[96,3072]{1,0:T(8,128)(2,1)}, bf16[384,768]{1,0:T(8,128)(2,1)}), ...) | async-done | bytes 2211856 | tf_op jit(solution)/shard_map/psum | solution.py:345
  (669 shorter events, 339.4 us)
Async XLA Ops:
  7.2 39.4 %all-gather.10.cloned.1.call-start = ((), (), s32[]{:S(2)}) async-start(), calls=%async_computation.16 | async-start | bytes 3981312 | tf_op jit(solution)/shard_map/all_gather | solution.py:307
  7.9 74.6 %all-gather.12.cloned.1.call-start = ((), (), s32[]{:S(2)}) async-start(), calls=%async_computation.17 | async-start | bytes 3981312 | tf_op jit(solution)/shard_map/all_gather | solution.py:308
  8.7 41.3 %copy-start.2 = (bf16[4,256,768]{2,1,0:T(8,128)(2,1)S(1)}, bf16[4,256,768]{2,1,0:T(8,128)(2,1)}, u32[]{:S(2)}) copy-start(bf16[4,256,768]{2,1,0:T(8,128)(2,1)} %param.12) | copy-start | bytes 4718596
  8.7 394.4 %all-gather.14.cloned.1.call-start = ((), (), s32[]{:S(2)}) async-start(), calls=%async_computation.18 | async-start | bytes 1327104 | tf_op jit(solution)/shard_map/all_gather | solution.py:309
  9.4 413.3 %all-gather.16.cloned.1.call-start = ((), (), s32[]{:S(2)}) async-start(), calls=%async_computation.19 | async-start | bytes 5308416 | tf_op jit(solution)/shard_map/all_gather | solution.py:313
  29.9 543.1 %copy-start.89 = (f32[768]{0:T(1024)}, f32[768]{0:T(1024)S(1)}, u32[]{:S(2)}) copy-start(f32[768]{0:T(1024)S(1)} %get-tuple-element.119) | copy-start | bytes 9220
  99.0 14.4 %copy-start.152 = (s32[4,4]{1,0:T(4,128)S(1)}, s32[4,4]{1,0:T(4,128)}, u32[]{:S(2)}) copy-start(s32[4,4]{1,0:T(4,128)} %param.13) | copy-start | bytes 196
  99.0 129.6 %all-to-all-start = ((bf16[5,2,256,768]{2,1,0,3:T(2,128)(2,1)}), bf16[5,2,256,768]{2,1,0,3:T(2,128)(2,1)}, u32[]{:S(2)}, u32[]{:S(2)}) async-start(bf16[5,2,256,768]{2,1,0,3:T(2,128)(2,1)} %copy.324), calls=%async_computation | async-start | bytes 7864320 | tf_op jit(solution)/shard_map/all_to_all | solution.py:68
  104.1 372.4 %all-gather.18.cloned.1.call-start = ((), (), s32[]{:S(2)}) async-start(), calls=%async_computation.20 | async-start | bytes 5308416 | tf_op jit(solution)/shard_map/all_gather | solution.py:315
  113.4 88.0 %copy-start.131 = (s32[256]{0:T(256)}, s32[256]{0:T(256)S(1)}, u32[]{:S(2)}) copy-start(s32[256]{0:T(256)S(1)} %iota_add_fusion.1) | copy-start | bytes 3076
  113.4 178.1 %copy-start.108 = (s32[2,4]{1,0:T(2,128)}, s32[2,4]{1,0:T(2,128)S(1)}, u32[]{:S(2)}) copy-start(s32[2,4]{1,0:T(2,128)S(1)} %get-tuple-element.185) | copy-start | bytes 100
  113.4 476.2 %copy-start.106 = (s32[2,4]{1,0:T(2,128)}, s32[2,4]{1,0:T(2,128)S(1)}, u32[]{:S(2)}) copy-start(s32[2,4]{1,0:T(2,128)S(1)} %get-tuple-element.186) | copy-start | bytes 100
  201.2 27.0 %copy-start.102 = (bf16[2,4,768]{2,1,0:T(4,128)(2,1)}, bf16[2,4,768]{2,1,0:T(4,128)(2,1)S(1)}, u32[]{:S(2)}) copy-start(bf16[2,4,768]{2,1,0:T(4,128)(2,1)S(1)} %get-tuple-element.129) | copy-start | bytes 36868
  201.4 90.0 %copy-start.98 = (f32[2,1024]{1,0:T(2,128)}, f32[2,1024]{1,0:T(2,128)S(1)}, u32[]{:S(2)}) copy-start(f32[2,1024]{1,0:T(2,128)S(1)} %broadcast_subtract_fusion.1) | copy-start | bytes 24580
  206.8 21.5 %copy-start.15 = (bf16[1,768,768]{2,1,0:T(8,128)(2,1)}, bf16[1,768,768]{2,1,0:T(8,128)(2,1)S(1)}, u32[]{:S(2)}) copy-start(bf16[1,768,768]{2,1,0:T(8,128)(2,1)S(1)} %slice.280) | copy-start | bytes 3538948
  207.2 52.6 %copy-start.112 = (bf16[2,4,3,64]{3,2,1,0:T(4,128)(2,1)}, bf16[2,4,3,64]{3,2,1,0:T(4,128)(2,1)S(1)}, u32[]{:S(2)}) copy-start(bf16[2,4,3,64]{3,2,1,0:T(4,128)(2,1)S(1)} %reshape.401) | copy-start | bytes 9220
  228.6 134.9 %copy-start.114 = (bf16[2,4,3,64]{3,2,1,0:T(4,128)(2,1)}, bf16[2,4,3,64]{3,2,1,0:T(4,128)(2,1)S(1)}, u32[]{:S(2)}) copy-start(bf16[2,4,3,64]{3,2,1,0:T(4,128)(2,1)S(1)} %reshape.403) | copy-start | bytes 9220
  228.6 89.7 %all-to-all-start.2 = ((bf16[5,2,256,768]{2,1,0,3:T(2,128)(2,1)}), bf16[5,2,256,768]{2,1,0,3:T(2,128)(2,1)}, u32[]{:S(2)}, u32[]{:S(2)}) async-start(bf16[5,2,256,768]{2,1,0,3:T(2,128)(2,1)} %copy.339), calls=%async_computation.2 | async-start | bytes 7864320 | tf_op jit(solution)/shard_map/all_to_all | solution.py:68
  239.3 32.3 %copy-start.28 = (bf16[2,1024,3,64]{1,3,2,0:T(8,128)(2,1)}, bf16[2,1024,3,64]{1,3,2,0:T(8,128)(2,1)S(1)}, u32[]{:S(2)}) copy-start(bf16[2,1024,3,64]{1,3,2,0:T(8,128)(2,1)S(1)} %squeeze.52) | copy-start | bytes 2359300
  244.1 27.6 %copy-start.11 = (bf16[2,1024,3,64]{1,3,2,0:T(8,128)(2,1)}, bf16[2,1024,3,64]{1,3,2,0:T(8,128)(2,1)S(1)}, u32[]{:S(2)}) copy-start(bf16[2,1024,3,64]{1,3,2,0:T(8,128)(2,1)S(1)} %squeeze.53) | copy-start | bytes 2359300
  318.3 68.5 %all-to-all-start.1 = ((bf16[2,1024,192]{2,0,1:T(2,128)(2,1)}), bf16[2,1024,192]{2,0,1:T(2,128)(2,1)S(1)}, u32[]{:S(2)}, u32[]{:S(2)}) async-start(bf16[2,1024,192]{2,0,1:T(2,128)(2,1)} %copy.333), calls=%async_computation.1 | async-start | bytes 2097152 | tf_op jit(solution)/shard_map/all_to_all | solution.py:138
  332.8 16.2 %copy-start.13 = (bf16[2,1024,3,64]{1,3,2,0:T(8,128)(2,1)}, bf16[2,1024,3,64]{1,3,2,0:T(8,128)(2,1)S(1)}, u32[]{:S(2)}) copy-start(bf16[2,1024,3,64]{1,3,2,0:T(8,128)(2,1)S(1)} %squeeze.114) | copy-start | bytes 2359300
  359.1 258.8 %copy-start.126 = (f32[2,3,512]{2,1,0:T(4,128)}, f32[2,3,512]{2,1,0:T(4,128)S(1)}, u32[]{:S(2)}) copy-start(f32[2,3,512]{2,1,0:T(4,128)S(1)} %get-tuple-element.195) | copy-start | bytes 36868
  363.5 14.5 %copy-start.35 = (bf16[2,1024,3,64]{1,3,2,0:T(8,128)(2,1)}, bf16[2,1024,3,64]{1,3,2,0:T(8,128)(2,1)S(1)}, u32[]{:S(2)}) copy-start(bf16[2,1024,3,64]{1,3,2,0:T(8,128)(2,1)S(1)} %squeeze.116) | copy-start | bytes 2359300
  363.8 14.3 %copy-start.85 = (f32[2,3,4,1024]{3,2,1,0:T(4,128)}, f32[2,3,4,1024]{3,2,1,0:T(4,128)S(1)}, u32[]{:S(2)}) copy-start(f32[2,3,4,1024]{3,2,1,0:T(4,128)S(1)} %fusion.284) | copy-start | bytes 294916
  364.5 13.6 %copy-start.147 = (f32[2,3,4]{2,1,0:T(4,128)}, f32[2,3,4]{2,1,0:T(4,128)S(1)}, u32[]{:S(2)}) copy-start(f32[2,3,4]{2,1,0:T(4,128)S(1)} %get-tuple-element.199) | copy-start | bytes 292
  386.9 29.8 %all-to-all-start.3 = ((bf16[2,1024,192]{2,0,1:T(2,128)(2,1)}), bf16[2,1024,192]{2,0,1:T(2,128)(2,1)}, u32[]{:S(2)}, u32[]{:S(2)}) async-start(bf16[2,1024,192]{2,0,1:T(2,128)(2,1)} %copy.347), calls=%async_computation.3 | async-start | bytes 2097152 | tf_op jit(solution)/shard_map/all_to_all | solution.py:138
  391.9 660.8 %reduce-scatter.33.cloned.1.call-start = ((), (), s32[]{:S(2)}) async-start(), calls=%async_computation.28 | async-start | bytes 442368
  405.6 157.5 %copy-start.116 = (f32[2,256]{1,0:T(2,128)}, f32[2,256]{1,0:T(2,128)S(1)}, u32[]{:S(2)}) copy-start(f32[2,256]{1,0:T(2,128)S(1)} %broadcast_multiply_fusion.11) | copy-start | bytes 6148
  407.0 156.0 %copy-start.139 = (f32[2,256]{1,0:T(2,128)}, f32[2,256]{1,0:T(2,128)S(1)}, u32[]{:S(2)}) copy-start(f32[2,256]{1,0:T(2,128)S(1)} %add_rsqrt_fusion.3) | copy-start | bytes 6148
  422.3 150.7 %copy-start.4 = (f32[2,256,768]{2,1,0:T(8,128)}, f32[2,256,768]{2,1,0:T(8,128)S(1)}, u32[]{:S(2)}) copy-start(f32[2,256,768]{2,1,0:T(8,128)S(1)} %get-tuple-element.202) | copy-start | bytes 4718596
  422.3 150.7 %copy-start.96 = (f32[2,256]{1,0:T(2,128)}, f32[2,256]{1,0:T(2,128)S(1)}, u32[]{:S(2)}) copy-start(f32[2,256]{1,0:T(2,128)S(1)} %broadcast_multiply_fusion.9) | copy-start | bytes 6148
  422.7 150.3 %copy-start.100 = (f32[2,256]{1,0:T(2,128)}, f32[2,256]{1,0:T(2,128)S(1)}, u32[]{:S(2)}) copy-start(f32[2,256]{1,0:T(2,128)S(1)} %add_rsqrt_fusion.1) | copy-start | bytes 6148
  443.8 32.7 %copy-start.150 = (f32[768]{0:T(1024)S(1)}, f32[768]{0:T(1024)}, u32[]{:S(2)}) copy-start(f32[768]{0:T(1024)} %get-tuple-element.239) | copy-start | bytes 9220
  487.8 24.3 %slice-start.9 = ((s8[6291456]{0:T(1024)(128)(4,1)}), s8[4194304]{0:T(1024)(128)(4,1)S(1)}, s32[]{:S(2)}) async-start(s8[6291456]{0:T(1024)(128)(4,1)} %bitcast.513), calls=%async_computation.39 | async-start | bytes 8388608
  487.8 24.3 %slice-start.11 = ((s8[6291456]{0:T(1024)(128)(4,1)}), s8[4194304]{0:T(1024)(128)(4,1)S(1)}, s32[]{:S(2)}) async-start(s8[6291456]{0:T(1024)(128)(4,1)} %bitcast.515), calls=%async_computation.41 | async-start | bytes 8388608
  491.2 20.9 %slice-start.10 = ((s8[6291456]{0:T(1024)(128)(4,1)}), s8[2097152]{0:T(1024)(128)(4,1)S(1)}, s32[]{:S(2)}) async-start(s8[6291456]{0:T(1024)(128)(4,1)} %bitcast.513), calls=%async_computation.40 | async-start | bytes 4194304
  491.2 20.9 %slice-start.12 = ((s8[6291456]{0:T(1024)(128)(4,1)}), s8[2097152]{0:T(1024)(128)(4,1)S(1)}, s32[]{:S(2)}) async-start(s8[6291456]{0:T(1024)(128)(4,1)} %bitcast.515), calls=%async_computation.42 | async-start | bytes 4194304
  531.6 522.1 %reduce-scatter.31.cloned.1.call-start = ((), (), s32[]{:S(2)}) async-start(), calls=%async_computation.27 | async-start | bytes 442368
  536.3 537.8 %reduce-scatter.19.cloned.1.call-start = ((), (), s32[]{:S(2)}) async-start(), calls=%async_computation.21 | async-start | bytes 2654208 | tf_op jit(solution)/shard_map/reduce_scatter | solution.py:336
  542.1 559.1 %reduce-scatter.23.cloned.1.call-start = ((), (), s32[]{:S(2)}) async-start(), calls=%async_computation.23 | async-start | bytes 10616832 | tf_op jit(solution)/shard_map/reduce_scatter | solution.py:342
  558.8 23.8 %all-to-all-start.6 = ((bf16[2,256,768]{1,0,2:T(2,128)(2,1)}), bf16[2,256,768]{1,0,2:T(2,128)(2,1)}, u32[]{:S(2)}, u32[]{:S(2)}) async-start(bf16[2,256,768]{1,0,2:T(2,128)(2,1)} %copy.373), calls=%async_computation.6 | async-start | bytes 1572864 | tf_op jit(solution)/shard_map/all_to_all | solution.py:168
  563.0 540.4 %reduce-scatter.21.cloned.1.call-start = ((), (), s32[]{:S(2)}) async-start(), calls=%async_computation.22 | async-start | bytes 10616832 | tf_op jit(solution)/shard_map/reduce_scatter | solution.py:340
  582.6 41.7 %all-to-all-start.4 = ((bf16[2,256,768]{1,0,2:T(2,128)(2,1)}), bf16[2,256,768]{1,0,2:T(2,128)(2,1)}, u32[]{:S(2)}, u32[]{:S(2)}) async-start(bf16[2,256,768]{1,0,2:T(2,128)(2,1)} %copy.351), calls=%async_computation.4 | async-start | bytes 1572864 | tf_op jit(solution)/shard_map/all_to_all | solution.py:168
  590.3 16.2 %slice-start.6 = ((s8[12582912]{0:T(1024)(128)(4,1)}), s8[4194304]{0:T(1024)(128)(4,1)S(1)}, s32[]{:S(2)}) async-start(s8[12582912]{0:T(1024)(128)(4,1)} %bitcast.511), calls=%async_computation.36 | async-start | bytes 8388608
  590.4 16.2 %slice-start.7 = ((s8[12582912]{0:T(1024)(128)(4,1)}), s8[4194304]{0:T(1024)(128)(4,1)S(1)}, s32[]{:S(2)}) async-start(s8[12582912]{0:T(1024)(128)(4,1)} %bitcast.511), calls=%async_computation.37 | async-start | bytes 8388608
  657.4 14.0 %copy-start.127 = (f32[2,3,512]{2,1,0:T(4,128)S(1)}, f32[2,3,512]{2,1,0:T(4,128)}, u32[]{:S(2)}) copy-start(f32[2,3,512]{2,1,0:T(4,128)} %copy-done.126) | copy-start | bytes 36868
  657.4 14.0 %copy-start.130 = (f32[2,3,512]{2,1,0:T(4,128)S(1)}, f32[2,3,512]{2,1,0:T(4,128)}, u32[]{:S(2)}) copy-start(f32[2,3,512]{2,1,0:T(4,128)} %get-tuple-element.210) | copy-start | bytes 36868
  703.2 119.9 %all-to-all-start.7 = ((bf16[5,2,1024,192]{3,1,0,2:T(2,128)(2,1)}), bf16[5,2,1024,192]{3,1,0,2:T(2,128)(2,1)}, u32[]{:S(2)}, u32[]{:S(2)}) async-start(bf16[5,2,1024,192]{3,1,0,2:T(2,128)(2,1)} %constant_dynamic-update-slice_fusion.4), calls=%async_computation.7 | async-start | bytes 10485760 | tf_op jit(solution)/shard_map/all_to_all | solution.py:221
  787.6 40.6 %copy-start.34 = (bf16[2,1024,3,64]{1,3,2,0:T(8,128)(2,1)S(1)}, bf16[2,1024,3,64]{1,3,2,0:T(8,128)(2,1)}, u32[]{:S(2)}) copy-start(bf16[2,1024,3,64]{1,3,2,0:T(8,128)(2,1)} %squeeze.55) | copy-start | bytes 2359300
  787.6 40.6 %copy-start.93 = (f32[2,3,4,1024]{3,2,1,0:T(4,128)S(1)}, f32[2,3,4,1024]{3,2,1,0:T(4,128)}, u32[]{:S(2)}) copy-start(f32[2,3,4,1024]{3,2,1,0:T(4,128)} %get-tuple-element.192) | copy-start | bytes 294916
  787.6 40.6 %copy-start.163 = (f32[2,3,4,1024]{3,2,1,0:T(4,128)S(1)}, f32[2,3,4,1024]{3,2,1,0:T(4,128)}, u32[]{:S(2)}) copy-start(f32[2,3,4,1024]{3,2,1,0:T(4,128)} %copy-done.162) | copy-start | bytes 294916
  787.6 41.1 %copy-start.36 = (bf16[2,1024,3,64]{1,3,2,0:T(8,128)(2,1)S(1)}, bf16[2,1024,3,64]{1,3,2,0:T(8,128)(2,1)}, u32[]{:S(2)}) copy-start(bf16[2,1024,3,64]{1,3,2,0:T(8,128)(2,1)} %copy-done.35) | copy-start | bytes 2359300
  787.6 41.1 %copy-start.95 = (f32[2,3,4,1024]{3,2,1,0:T(4,128)S(1)}, f32[2,3,4,1024]{3,2,1,0:T(4,128)}, u32[]{:S(2)}) copy-start(f32[2,3,4,1024]{3,2,1,0:T(4,128)} %get-tuple-element.200) | copy-start | bytes 294916
  787.6 41.1 %copy-start.149 = (f32[2,3,4]{2,1,0:T(4,128)S(1)}, f32[2,3,4]{2,1,0:T(4,128)}, u32[]{:S(2)}) copy-start(f32[2,3,4]{2,1,0:T(4,128)} %copy-done.147) | copy-start | bytes 292
  787.6 41.1 %copy-start.161 = (f32[2,3,4,1024]{3,2,1,0:T(4,128)S(1)}, f32[2,3,4,1024]{3,2,1,0:T(4,128)}, u32[]{:S(2)}) copy-start(f32[2,3,4,1024]{3,2,1,0:T(4,128)} %get-tuple-element.215) | copy-start | bytes 294916
  787.6 41.1 %copy-start.164 = (f32[2,3,4]{2,1,0:T(4,128)S(1)}, f32[2,3,4]{2,1,0:T(4,128)}, u32[]{:S(2)}) copy-start(f32[2,3,4]{2,1,0:T(4,128)} %get-tuple-element.214) | copy-start | bytes 292
  823.1 120.2 %all-to-all-start.5 = ((bf16[5,2,1024,192]{3,1,0,2:T(2,128)(2,1)}), bf16[5,2,1024,192]{3,1,0,2:T(2,128)(2,1)}, u32[]{:S(2)}, u32[]{:S(2)}) async-start(bf16[5,2,1024,192]{3,1,0,2:T(2,128)(2,1)} %constant_dynamic-update-slice_fusion), calls=%async_computation.5 | async-start | bytes 10485760 | tf_op jit(solution)/shard_map/all_to_all | solution.py:221
  828.1 277.4 %reduce-scatter.27.cloned.1.call-start = ((), (), s32[]{:S(2)}) async-start(), calls=%async_computation.25 | async-start | bytes 7962624
  992.8 132.6 %reduce-scatter.25.cloned.1.call-start = ((), (), s32[]{:S(2)}) async-start(), calls=%async_computation.24 | async-start | bytes 7962624
  1024.7 30.3 %copy-start.16 = (bf16[1,768,768]{2,1,0:T(8,128)(2,1)S(1)}, bf16[1,768,768]{2,1,0:T(8,128)(2,1)}, u32[]{:S(2)}) copy-start(bf16[1,768,768]{2,1,0:T(8,128)(2,1)} %copy-done.15) | copy-start | bytes 3538948
  1024.7 137.9 %reduce-scatter.29.cloned.1.call-start = ((), (), s32[]{:S(2)}) async-start(), calls=%async_computation.26 | async-start | bytes 442368
  1083.5 185.2 %all-reduce.7.cloned.1.call-start = ((), (), s32[]{:S(2)}) async-start(), calls=%async_computation.29 | async-start | bytes 5013504 | tf_op jit(solution)/shard_map/psum | solution.py:345
  1107.3 20.9 %copy-start.39 = (bf16[1,2,256,4,192]{2,4,3,1,0:T(8,128)(2,1)S(1)}, bf16[1,2,256,4,192]{2,4,3,1,0:T(8,128)(2,1)}, u32[]{:S(2)}) copy-start(bf16[1,2,256,4,192]{2,4,3,1,0:T(8,128)(2,1)} %copy-done.38) | copy-start | bytes 2359300
  (136 other events, 720.2 us)
Sparse Core Ops, SparseCore 0:
  9.9 36.6 all-gather.9
  48.5 33.9 all-gather.11
  84.4 24.0 all-gather.13
  110.2 38.9 all-gather.15
  150.9 38.9 all-gather.17
  531.7 32.0 reduce-scatter.32
  566.8 33.8 reduce-scatter.30
  604.0 42.4 reduce-scatter.18
  650.5 76.4 reduce-scatter.22
  730.7 76.5 reduce-scatter.20
  992.9 63.5 reduce-scatter.26
  1059.9 65.4 reduce-scatter.24
  1128.7 33.8 reduce-scatter.28
  1166.6 101.9 all-reduce.6
where the time goes:
time: 1300 us; the launch traced here: 1280 us
  waiting for transfers between devices  343 us (26%)
  matrix products  335 us (26%)
  local copies, waits for them, and re-layouts  246 us (19%)
  blocking collectives  178 us (14%)
  other arithmetic  125 us (10%)
  starting transfers between devices  38.8 us (3%)
  between operations  17.8 us (1%)
    all_to_all x2, waiting for transfers between devices, micro_step(): lax.all_to_all(heads_grad, 'sp', split_axis=2, concat_axis=3, tiled=True)  130 us
    psum x1, waiting for transfers between devices, per_device(): lax.psum(totals[0].astype(jnp.bfloat16), 'sp').astype(jnp.float32)  91.1 us
    psum x1, blocking collectives, micro_step(): rows_glob = lax.psum(rows_part.astype(jnp.bfloat16), 'sp')  87.2 us
    unnamed x381, local copies, waits for them, and re-layouts  80.1 us
    dot_general x16, matrix products, back_project(): jnp.einsum('sre,de->srd', gradient, matrix, preferred_element_type=jnp.fl...  67.4 us
    dot_general x16, matrix products, project(): jnp.einsum('srd,de->sre', tokens, matrix, preferred_element_type=jnp.floa...  54.8 us
    unnamed x19, waiting for transfers between devices  41.5 us
    dot_general x16, matrix products, outer_sum(): jnp.einsum('srd,sre->de', tokens, gradient, preferred_element_type=jnp.fl...  39.8 us
  transfers between devices with their start and end apart: 22, of which 10 were waited for; matrix products, arithmetic and copies ran while one was open for 49% of the time, Pallas kernels for 0%

commit v1 on v0

v1 whole, which is shorter than its diff:
```python
import jax
import jax.numpy as jnp
from jax import lax
from jax.sharding import PartitionSpec as P

HEADS = 12
HEAD_DIM = 64
WIN = 256

HIGHEST = lax.Precision.HIGHEST
MASKED_SCORE = -1000000000.0
NORM_EPS = 1e-05
BF = jnp.bfloat16
F32 = jnp.float32


def normalize(summed):
    center = summed - jnp.mean(summed, axis=-1, keepdims=True)
    inverse = lax.rsqrt(jnp.mean(center * center, axis=-1, keepdims=True) + NORM_EPS)
    return (center * inverse, inverse)


def norm_back(scaled, normed, inverse):
    return inverse * (
        scaled
        - jnp.mean(scaled, axis=-1, keepdims=True)
        - normed * jnp.mean(scaled * normed, axis=-1, keepdims=True)
    )


def mm(a, b):
    return jnp.dot(a, b, preferred_element_type=F32)


def mm_nt(a, b):
    return lax.dot_general(a, b, (((1,), (1,)), ((), ())), preferred_element_type=F32)


def mm_tn(a, b):
    return lax.dot_general(a, b, (((0,), (0,)), ((), ())), preferred_element_type=F32)


def gelu_pair(inner):
    cdf = 0.5 * (1.0 + lax.erf(inner * (0.5**0.5)))
    pdf = jnp.exp(-0.5 * inner * inner) * 0.3989422804014327
    return (inner * cdf, cdf + inner * pdf)


def sequence_step(x, positions, upstream_low, weights):
    w_local, w_global, w_out, b_proj, gains, shifts, w_in, c_in, w_back = weights
    length, width = x.shape
    scale = HEAD_DIM ** (-0.5)
    bias = b_proj.astype(F32)
    gain = gains.astype(F32)
    shift = shifts.astype(F32)

    def heads(value):
        return value.reshape(value.shape[0], HEADS, HEAD_DIM)

    q = heads(((mm(x, w_local[0]) + bias[0]) * scale).astype(BF))
    k = heads(mm(x, w_local[1]).astype(BF))
    v = heads((mm(x, w_local[2]) + bias[1]).astype(BF))
    kg = heads(mm(x, w_global[1]).astype(BF))
    vg = heads((mm(x, w_global[2]) + bias[3]).astype(BF))
    places = jnp.arange(length, dtype=jnp.int32)
    select = positions[:, None] == places[None, :]
    select_low = select.astype(BF)
    select_full = select.astype(F32)
    is_glob = jnp.sum(select_full, axis=0)
    keep_local = 1.0 - is_glob
    rows_glob = mm(select_low, x).astype(BF)
    qg = heads(((mm(rows_glob, w_global[0]) + bias[2]) * scale).astype(BF))
    block = 256
    offsets = list(range(0, length, block))

    def block_scores(offset):
        qb = q[offset : offset + block]
        row_places = offset + jnp.arange(block, dtype=jnp.int32)
        in_band = jnp.abs(row_places[:, None] - places[None, :]) <= WIN
        allowed = in_band | (is_glob[None, :] > 0.5)
        raw = jnp.einsum("ihe,jhe->hij", qb, k, preferred_element_type=F32)
        return (qb, jnp.where(allowed[None], raw, MASKED_SCORE))

    kept = []
    contexts = []
    for offset in offsets:
        qb, masked = block_scores(offset)
        top = jnp.max(masked, axis=-1, keepdims=True)
        powers = jnp.exp(masked - top)
        total = jnp.sum(powers, axis=-1, keepdims=True)
        low = (powers / total).astype(BF)
        contexts.append(jnp.einsum("hij,jhe->ihe", low, v, preferred_element_type=F32))
        kept.append((top, total))
    context_loc = jnp.concatenate(contexts, axis=0)
    glob_scores = jnp.einsum("ghe,jhe->hgj", qg, kg, preferred_element_type=F32)
    glob_probs = jax.nn.softmax(glob_scores, axis=-1)
    glob_low = glob_probs.astype(BF)
    context_glob = jnp.einsum("hgj,jhe->ghe", glob_low, vg, preferred_element_type=F32)
    context = context_loc * keep_local[:, None, None] + jnp.einsum(
        "gl,ghe->lhe", select_full, context_glob, precision=HIGHEST
    )
    merged = context.astype(BF).reshape(length, width)
    attended = mm(merged, w_out) + bias[4]
    normed_one, inverse_one = normalize(x.astype(F32) + attended)
    first_norm = normed_one * gain[0] + shift[0]
    first_low = first_norm.astype(BF)
    inner = mm(first_low, w_in) + c_in.astype(F32)
    act, slope = gelu_pair(inner)
    active = act.astype(BF)
    normed_two, inverse_two = normalize(first_norm + (mm(active, w_back) + bias[5]))
    result = normed_two * gain[1] + shift[1]
    upstream = upstream_low.astype(F32)
    grad_gain_two = jnp.sum(upstream * normed_two, axis=0)
    grad_shift_two = jnp.sum(upstream, axis=0)
    grad_second = norm_back(upstream * gain[1], normed_two, inverse_two)
    branch_grad = grad_second.astype(BF)
    grad_back_w = mm_tn(active, branch_grad)
    grad_out_bias = jnp.sum(branch_grad.astype(F32), axis=0)
    inner_grad = (mm_nt(branch_grad, w_back) * slope).astype(BF)
    grad_in_w = mm_tn(first_low, inner_grad)
    grad_in_bias = jnp.sum(inner_grad.astype(F32), axis=0)
    grad_first = grad_second + mm_nt(inner_grad, w_in)
    grad_gain_one = jnp.sum(grad_first * normed_one, axis=0)
    grad_shift_one = jnp.sum(grad_first, axis=0)
    grad_sum_one = norm_back(grad_first * gain[0], normed_one, inverse_one)
    attn_grad = grad_sum_one.astype(BF)
    grad_out_w = mm_tn(merged, attn_grad)
    grad_att_bias = jnp.sum(attn_grad.astype(F32), axis=0)
    ctx_grad = heads(mm_nt(attn_grad, w_out).astype(BF))
    local_grad = (ctx_grad.astype(F32) * keep_local[:, None, None]).astype(BF)
    glob_ctx_grad = jnp.einsum(
        "gl,lhe->ghe", select_low, ctx_grad, preferred_element_type=F32
    ).astype(BF)
    key_grad = jnp.zeros(k.shape, F32)
    value_grad = jnp.zeros(v.shape, F32)
    query_parts = []
    for index, offset in enumerate(offsets):
        qb, masked = block_scores(offset)
        probs = jnp.exp(masked - kept[index][0]) / kept[index][1]
        low = probs.astype(BF)
        gb = local_grad[offset : offset + block]
        grad_probs = jnp.einsum("ihe,jhe->hij", gb, v, preferred_element_type=F32)
        dot = jnp.sum(probs * grad_probs, axis=-1, keepdims=True)
        score_grad = (probs * (grad_probs - dot)).astype(BF)
        query_parts.append(jnp.einsum("hij,jhe->ihe", score_grad, k, preferred_element_type=F32))
        key_grad = key_grad + jnp.einsum(
            "hij,ihe->jhe", score_grad, qb, preferred_element_type=F32
        )
        value_grad = value_grad + jnp.einsum("hij,ihe->jhe", low, gb, preferred_element_type=F32)
    dq = jnp.concatenate(query_parts, axis=0).astype(BF)
    glob_grad_probs = jnp.einsum("ghe,jhe->hgj", glob_ctx_grad, vg, preferred_element_type=F32)
    glob_dot = jnp.sum(glob_probs * glob_grad_probs, axis=-1, keepdims=True)
    glob_score_grad = (glob_probs * (glob_grad_probs - glob_dot)).astype(BF)
    dqg = jnp.einsum("hgj,jhe->ghe", glob_score_grad, kg, preferred_element_type=F32).astype(BF)
    dkg = jnp.einsum("hgj,ghe->jhe", glob_score_grad, qg, preferred_element_type=F32).astype(BF)
    dvg = jnp.einsum("hgj,ghe->jhe", glob_low, glob_ctx_grad, preferred_element_type=F32).astype(BF)

    def flat(value):
        return value.astype(BF).reshape(value.shape[0], width)

    dq, dk, dv, dkg, dvg = (flat(value) for value in (dq, key_grad, value_grad, dkg, dvg))
    pre_query = dq * scale
    glob_pre = flat(dqg) * scale
    token_grad = (
        grad_sum_one
        + mm_nt(pre_query, w_local[0])
        + mm_nt(dk, w_local[1])
        + mm_nt(dv, w_local[2])
        + mm_nt(dkg, w_global[1])
        + mm_nt(dvg, w_global[2])
    )
    token_grad = token_grad + jnp.einsum(
        "gr,gd->rd", select_full, mm_nt(glob_pre, w_global[0]), precision=HIGHEST
    )
    grad_local = jnp.stack([mm_tn(x, pre_query), mm_tn(x, dk), mm_tn(x, dv)])
    grad_global = jnp.stack([mm_tn(rows_glob, glob_pre), mm_tn(x, dkg), mm_tn(x, dvg)])

    def total_of(value):
        return jnp.sum(value.astype(F32), axis=0)

    grad_bias = jnp.stack(
        [
            total_of(pre_query),
            total_of(dv),
            total_of(glob_pre),
            total_of(dvg),
            grad_att_bias,
            grad_out_bias,
        ]
    )
    grad_gain = jnp.stack([grad_gain_one, grad_gain_two])
    grad_shift = jnp.stack([grad_shift_one, grad_shift_two])
    return (
        result.astype(BF),
        token_grad.astype(BF),
        (
            grad_local,
            grad_global,
            grad_out_w,
            grad_bias,
            grad_gain,
            grad_shift,
            grad_in_w,
            grad_in_bias,
            grad_back_w,
        ),
    )


def per_device(
    inputs,
    global_pos,
    w_local,
    w_global,
    w_out,
    b_proj,
    gains,
    shifts,
    w_in,
    c_in,
    w_back,
    cotangent,
):
    sp_count = lax.axis_size("sp")
    fsdp_count = lax.axis_size("fsdp")
    sp_index = lax.axis_index("sp")
    own_seqs = inputs.shape[0] // sp_count
    shard = w_out.shape[0]
    width = w_out.shape[1]
    ff_shard = w_back.shape[0]
    pieces = w_in.shape[1] // width

    def to_sequence(value):
        return lax.all_to_all(value, "sp", split_axis=0, concat_axis=1, tiled=True)

    def to_tokens(value):
        return lax.all_to_all(value, "sp", split_axis=1, concat_axis=0, tiled=True)

    x_all = to_sequence(inputs)
    up_all = to_sequence(cotangent)
    own_pos = lax.dynamic_slice_in_dim(global_pos, sp_index * own_seqs, own_seqs, 0)

    small = jnp.concatenate(
        [b_proj.reshape(-1), gains.reshape(-1), shifts.reshape(-1), c_in.reshape(-1)]
    )
    small_rows = -(-small.shape[0] // width)
    small = jnp.pad(small, (0, small_rows * width - small.shape[0])).reshape(small_rows, width)
    pack_one = jnp.concatenate(
        [w_local.reshape(-1, width), w_global.reshape(-1, width), w_out, small], axis=0
    )
    pack_two = jnp.concatenate(
        [w_in.reshape(shard, pieces, width).transpose(1, 0, 2).reshape(-1, width), w_back], axis=0
    )
    all_one = lax.all_gather(pack_one, "fsdp")
    all_two = lax.all_gather(pack_two, "fsdp")

    def part(packed, start):
        return packed[:, start : start + shard].reshape(fsdp_count * shard, width)

    full_local = [part(all_one, index * shard) for index in range(3)]
    full_global = [part(all_one, (3 + index) * shard) for index in range(3)]
    full_out = part(all_one, 6 * shard)
    small_all = all_one[:, 7 * shard :].reshape(fsdp_count, -1)

    def vectors(start, count):
        taken = small_all[:, start : start + count * shard].reshape(fsdp_count, count, shard)
        return taken.transpose(1, 0, 2).reshape(count, fsdp_count * shard)

    full_bias = vectors(0, 6)
    full_gain = vectors(6 * shard, 2)
    full_shift = vectors(8 * shard, 2)
    full_c = small_all[:, 10 * shard : 10 * shard + ff_shard].reshape(-1)
    full_in = jnp.concatenate([part(all_two, index * shard) for index in range(pieces)], axis=1)
    full_back = all_two[:, pieces * shard :].reshape(-1, width)
    weights = (
        full_local,
        full_global,
        full_out,
        full_bias,
        full_gain,
        full_shift,
        full_in,
        full_c,
        full_back,
    )
    results = []
    token_grads = []
    totals = None
    for index in range(own_seqs):
        result, token_grad, grads = sequence_step(
            x_all[index], own_pos[index], up_all[index], weights
        )
        results.append(result)
        token_grads.append(token_grad)
        totals = grads if totals is None else tuple(a + b for a, b in zip(totals, grads))
    out = to_tokens(jnp.stack(results))
    grad_inputs = to_tokens(jnp.stack(token_grads))
    g_local, g_global, g_out, g_bias, g_gain, g_shift, g_in, g_c, g_back = totals

    def rows(value):
        return value.astype(BF).reshape(-1, fsdp_count, shard, width).transpose(1, 0, 2, 3)

    def cols(value):
        return value.reshape(-1, fsdp_count, shard).transpose(1, 0, 2).reshape(fsdp_count, -1)

    g_small = jnp.concatenate(
        [cols(g_bias), cols(g_gain), cols(g_shift), g_c.reshape(fsdp_count, ff_shard)], axis=1
    ).astype(BF)
    g_small = jnp.pad(g_small, ((0, 0), (0, small_rows * width - g_small.shape[1])))
    first = jnp.concatenate(
        [
            rows(g_in.reshape(width, pieces, width).transpose(1, 0, 2)).reshape(
                fsdp_count, -1, width
            ),
            g_back.astype(BF).reshape(fsdp_count, ff_shard, width),
        ],
        axis=1,
    )
    second = jnp.concatenate(
        [
            rows(g_local).reshape(fsdp_count, -1, width),
            rows(g_global).reshape(fsdp_count, -1, width),
            rows(g_out).reshape(fsdp_count, -1, width),
            g_small.reshape(fsdp_count, small_rows, width),
        ],
        axis=1,
    )

    def reduce(value):
        mine = lax.psum_scatter(value, "fsdp", scatter_dimension=0, tiled=False)
        return lax.psum(mine, "sp").astype(F32)

    first = reduce(first)
    second = reduce(second)
    small_sum = second[7 * shard :].reshape(-1)
    return (
        out,
        grad_inputs,
        second[: 3 * shard].reshape(3, shard, width),
        second[3 * shard : 6 * shard].reshape(3, shard, width),
        second[6 * shard : 7 * shard],
        small_sum[: 6 * shard].reshape(6, shard),
        small_sum[6 * shard : 8 * shard].reshape(2, shard),
        small_sum[8 * shard : 10 * shard].reshape(2, shard),
        first[: pieces * shard]
        .reshape(pieces, shard, width)
        .transpose(1, 0, 2)
        .reshape(shard, pieces * width),
        small_sum[10 * shard : 10 * shard + ff_shard],
        first[pieces * shard :],
    )


def solution(mesh):
    rows = P("fsdp", None)
    tokens = P("fsdp", "sp", None)
    columns = P(None, "fsdp")
    stacked = P(None, "fsdp", None)
    return jax.shard_map(
        per_device,
        mesh=mesh,
        in_specs=(
            tokens,
            rows,
            stacked,
            stacked,
            rows,
            columns,
            columns,
            columns,
            rows,
            P("fsdp"),
            rows,
            tokens,
        ),
        out_specs=(
            tokens,
            tokens,
            stacked,
            stacked,
            rows,
            columns,
            columns,
            columns,
            rows,
            P("fsdp"),
            rows,
        ),
        check_vma=False,
    )
```

time: 1300 us -> 709 us (0.55)
  waiting for transfers between devices: 343 us -> 155 us
  blocking collectives: 178 us -> 43.1 us
  local copies, waits for them, and re-layouts: 246 us -> 129 us
  matrix products: 335 us -> 269 us
  other arithmetic: 125 us -> 77.2 us
  starting transfers between devices: 38.8 us -> 13.4 us
    all_to_all x8 -> x3, waiting for transfers between devices: 164 us -> 28 us  [the longest x1 28 us: to_sequence(): return lax.all_to_all(value, 'sp', split_axis=0, concat_axis=1, tiled=True)]
    psum x3 -> x0, blocking collectives: 117 us -> none  [the longest x1 87.2 us: micro_step(): rows_glob = lax.psum(rows_part.astype(jnp.bfloat16), 'sp')]
    dot_general x94 -> x57, matrix products: 298 us -> 226 us  [the longest x9 38.9 us: mm_tn(): lax.dot_general(a, b, (((0,), (0,)), ((), ())), preferred_element_type=F32)]
    convert_element_type x21 -> x8, other arithmetic: 79.7 us -> 24.4 us  [the longest x4 23.8 us: sequence_step(): score_grad = (probs * (grad_probs - dot)).astype(BF)]
    all_gather x5 -> x2, waiting for transfers between devices: 46 us -> 0.04 us  [the longest x1 0.02 us: per_device(): all_one = lax.all_gather(pack_one, 'fsdp')]
    all_to_all x12 -> x0, local copies, waits for them, and re-layouts: 44 us -> none  [the longest x2 28.8 us: micro_step(): lax.all_to_all(heads_grad, 'sp', split_axis=2, concat_axis=3, tiled=True)]
    all_to_all x0 -> x1, blocking collectives: none -> 43.1 us  [to_sequence(): return lax.all_to_all(value, 'sp', split_axis=0, concat_axis=1, tiled=True)]
    reduce_scatter x3 -> x2, waiting for transfers between devices: 0.02 us -> 41.6 us  [reduce(): mine = lax.psum_scatter(value, 'fsdp', scatter_dimension=0, tiled=False)]
  transfers between devices with their start and end apart: 22 -> 8, of which waited for: 10 -> 3; matrix products, arithmetic and copies ran while one was open for 49% -> 31% of each run, Pallas kernels for 0% -> 0%
where the time goes in v1:
time: 709 us; the launch traced here: 703 us
  matrix products  269 us (38%)
  waiting for transfers between devices  155 us (22%)
  local copies, waits for them, and re-layouts  129 us (18%)
  other arithmetic  77.2 us (11%)
  blocking collectives  43.1 us (6%)
  between operations  15.4 us (2%)
  starting transfers between devices  13.4 us (2%)
    psum x1, waiting for transfers between devices, reduce(): return lax.psum(mine, 'sp').astype(F32)  85.1 us
    sub x4, matrix products, sequence_step(): powers = jnp.exp(masked - top)  43.7 us
    all_to_all x1, blocking collectives, to_sequence(): return lax.all_to_all(value, 'sp', split_axis=0, concat_axis=1, tiled=True)  43.1 us
    unnamed x271, local copies, waits for them, and re-layouts  42.3 us
    reduce_scatter x2, waiting for transfers between devices, reduce(): mine = lax.psum_scatter(value, 'fsdp', scatter_dimension=0, tiled=False)  41.6 us
    dot_general x9, matrix products, mm_tn(): lax.dot_general(a, b, (((0,), (0,)), ((), ())), preferred_element_type=F32)  38.9 us
    dot_general x10, matrix products, mm(): return jnp.dot(a, b, preferred_element_type=F32)  38.8 us
    dot_general x9, matrix products, mm_nt(): lax.dot_general(a, b, (((1,), (1,)), ((), ())), preferred_element_type=F32)  33.3 us
  transfers between devices with their start and end apart: 8, of which 3 were waited for; matrix products, arithmetic and copies ran while one was open for 31% of the time, Pallas kernels for 0%

profile of v1, /device:TPU:0, one launch (start us, length us, event | category | flops | bytes accessed | tf_op | source)
XLA Modules:
  0.0 702.7 jit_solution(2198869074152670844)
XLA Ops:
  12.7 43.1 %all_to_all.42 = bf16[4,256,768]{2,1,0:T(8,128)(2,1)S(1)} all-to-all(bf16[4,256,768]{2,1,0:T(8,128)(2,1)S(1)} %copy-done.35), channel_id=1, replica_groups=mesh['fsdp'=8,'sp'=4] {'sp'}, dimensions={0} | all-to-all | bytes 3145728 | tf_op jit(solution)/shard_map/all_to_all | solution.py:234
  55.8 3.6 all-to-all-start.2
  67.4 28.0 %all-to-all-done.2 = bf16[4,256,768]{2,1,0:T(8,128)(2,1)S(1)} async-done(((bf16[4,256,768]{2,1,0:T(8,128)(2,1)}), bf16[4,256,768]{2,1,0:T(8,128)(2,1)S(1)}, u32[]{:S(2)}, u32[]{:S(2)}) %all-to-all-start.2) | async-done | bytes 1572896 | tf_op jit(solution)/shard_map/all_to_all | solution.py:234
  106.4 6.1 fusion.127
  113.9 3.4 convolution_convert_fusion.5
  119.6 2.6 add_convert_fusion.4
  122.3 2.6 convolution_bitcast_fusion
  124.9 3.3 fusion.52
  130.6 2.6 convolution_convert_fusion.6
  133.3 2.6 add_convert_fusion.5
  135.9 11.0 %fusion.132 = (f32[12,256]{1,0:T(8,128)}, f32[12,256,1024]{2,1,0:T(8,128)}) fusion(pred[256,1024]{1,0:T(8,128)(4,1)} %get-tuple-element.82, bf16[256,12,64]{0,2,1:T(8,128)(2,1)} %bitcast.334, bf16[1024,12,64]{0,2,1:T(8,128)(2,1)} %bitcast.255), kind=kOutput, calls=%fused_computation.236 | convolution fusion | flops 412091392 | bytes 14823424 | tf_op jit(solution)/shard_map/sub | solution.py:89
  146.9 10.7 %fusion.133 = (f32[12,256]{1,0:T(8,128)}, f32[12,256,1024]{2,1,0:T(8,128)}) fusion(pred[256,1024]{1,0:T(8,128)(4,1)} %get-tuple-element.81, bf16[256,12,64]{0,2,1:T(8,128)(2,1)} %bitcast.311, bf16[1024,12,64]{0,2,1:T(8,128)(2,1)} %bitcast.256), kind=kOutput, calls=%fused_computation.237 | convolution fusion | flops 412091392 | bytes 14823424 | tf_op jit(solution)/shard_map/sub | solution.py:89
  157.6 10.8 %fusion.134 = (f32[12,256]{1,0:T(8,128)}, f32[12,256,1024]{2,1,0:T(8,128)}) fusion(pred[256,1024]{1,0:T(8,128)(4,1)} %get-tuple-element.80, bf16[256,12,64]{0,2,1:T(8,128)(2,1)} %bitcast.309, bf16[1024,12,64]{0,2,1:T(8,128)(2,1)} %bitcast.257), kind=kOutput, calls=%fused_computation.238 | convolution fusion | flops 412091392 | bytes 14823424 | tf_op jit(solution)/shard_map/sub | solution.py:89
  168.5 11.1 %fusion.135 = (f32[12,256]{1,0:T(8,128)}, f32[12,256,1024]{2,1,0:T(8,128)}) fusion(pred[256,1024]{1,0:T(8,128)(4,1)} %get-tuple-element.79, bf16[256,12,64]{0,2,1:T(8,128)(2,1)S(1)} %bitcast.307, bf16[1024,12,64]{0,2,1:T(8,128)(2,1)} %bitcast.258), kind=kOutput, calls=%fused_computation.239 | convolution fusion | flops 412091392 | bytes 14823424 | tf_op jit(solution)/shard_map/sub | solution.py:89
  179.6 6.5 fusion.73
  186.1 6.0 fusion.70
  192.1 6.0 fusion.67
  198.2 2.8 fusion.64
  206.7 5.2 slice.245
  213.5 2.5 fusion.126
  217.1 14.2 %multiply_convert_fusion.4 = (bf16[1024,3072]{1,0:T(8,128)(2,1)}, f32[1024,3072]{1,0:T(8,128)}) fusion(f32[3072]{0:T(1024)S(1)} %copy-done.85, bf16[768,768]{1,0:T(8,128)(2,1)} %bitcast.351, bf16[768,768]{1,0:T(8,128)(2,1)} %bitcast.353, bf16[768,768]{1,0:T(8,128)(2,1)} %bitcast.355, bf16[768,768]{1,0:T(8,128)(2,1)} %bitcast.349, ...), kind=kOutput, calls=%fused_computation.20 | convolution fusion | flops 4873519104 | bytes 26765312 | tf_op jit(solution)/shard_map/dot_general | solution.py:32
  231.4 7.7 %fusion.138 = (f32[1024]{0:T(1024)S(1)}, f32[1024,768]{0,1:T(8,128)S(1)}) fusion(f32[768]{0:T(1024)S(1)} %copy-done.96, bf16[1024,3072]{1,0:T(8,128)(2,1)} %get-tuple-element.95, bf16[3072,768]{1,0:T(8,128)(2,1)S(1)} %bitcast.303, f32[768]{0:T(1024)S(1)} %copy-done.94, f32[768]{0:T(1024)S(1)} %mul.222, f32[1024]{0:T(1024)S(1)} %add_rsqrt_fusion.1, ...), kind=kOutput, calls=%fused_computation.242 | convolution fusion | flops 4837342208 | bytes 17323008 | tf_op jit(solution)/shard_map/dot_general | solution.py:32
  239.7 3.0 multiply_reduce_fusion.4
  244.4 15.1 %fusion.140 = (bf16[3072]{0:T(1024)(128)(2,1)}, bf16[1024,3072]{1,0:T(8,128)(2,1)}) fusion(f32[1024,3072]{1,0:T(8,128)} %get-tuple-element.96, f32[3072]{0:T(1024)S(1)} %copy-done.85, bf16[3072,768]{1,0:T(8,128)(2,1)S(1)} %bitcast.304, f32[1024,768]{0,1:T(8,128)S(1)} %get-tuple-element.52), kind=kOutput, calls=%fused_computation.244 | convolution fusion | flops 4870370304 | bytes 26757120 | tf_op jit(solution)/shard_map/dot_general | solution.py:36
  259.6 9.4 %multiply_reduce_fusion.5 = (bf16[768]{0:T(1024)(128)(2,1)}, f32[1024]{0:T(1024)S(1)}, f32[1024]{0:T(1024)S(1)}, bf16[768]{0:T(1024)(128)(2,1)}, f32[1024,768]{0,1:T(8,128)S(1)}) fusion(f32[1024,768]{0,1:T(8,128)S(1)} %copy-done.14, f32[1024]{0:T(1024)S(1)} %add_rsqrt_fusion.1, f32[1024]{0:T(1024)S(1)} %broadcast_multiply_fusion.4, f32[768]{0:T(1024)S(1)} %mul.222, ...), kind=kOutput, calls=%fused_computation.57 | convolution fusion | flops 4858572800 | bytes 20469760 | tf_op jit(solution)/shard_map/dot_general | solution.py:36
  282.7 8.0 %fusion.41 = f32[12,64,1024]{2,1,0:T(8,128)} fusion(bf16[1024,12,64]{0,2,1:T(8,128)(2,1)S(1)} %multiply_convert_fusion.5, f32[12,256,1024]{2,1,0:T(8,128)} %get-tuple-element.88, f32[12,256]{1,0:T(8,128)S(1)} %copy-done.80), kind=kOutput, calls=%fused_computation.82 | convolution fusion | flops 408944640 | bytes 16138240 | tf_op jit(solution)/shard_map/hij,ihe->jhe/dot_general | solution.py:149
  290.7 8.4 %fusion.37 = f32[12,64,1024]{2,1,0:T(8,128)} fusion(bf16[1024,12,64]{0,2,1:T(8,128)(2,1)S(1)} %multiply_convert_fusion.5, f32[12,256,1024]{2,1,0:T(8,128)} %get-tuple-element.86, f32[12,256]{1,0:T(8,128)S(1)} %copy-done.82), kind=kOutput, calls=%fused_computation.78 | convolution fusion | flops 408944640 | bytes 16138240 | tf_op jit(solution)/shard_map/hij,ihe->jhe/dot_general | solution.py:149
  299.1 3.3 fusion.33
  302.4 8.2 %multiply_reduce_fusion = (f32[12,256]{1,0:T(8,128)}, f32[12,256,1024]{2,1,0:T(8,128)}) fusion(f32[12,256,1024]{2,1,0:T(8,128)S(1)} %bitcast.286, f32[12,256]{1,0:T(8,128)S(1)} %copy-done.78, bf16[1024,12,64]{0,2,1:T(8,128)(2,1)} %bitcast.382, bf16[1024,12,64]{0,2,1:T(8,128)(2,1)S(1)} %multiply_convert_fusion.5), kind=kOutput, calls=%fused_computation.13 | convolution fusion | flops 412087296 | bytes 27160576 | tf_op jit(solution)/shard_map/ihe,jhe->hij/dot_general | solution.py:142
  310.6 7.4 %multiply_reduce_fusion.1 = (f32[12,256]{1,0:T(8,128)S(1)}, f32[12,256,1024]{2,1,0:T(8,128)}) fusion(f32[12,256,1024]{2,1,0:T(8,128)S(1)} %bitcast.292, f32[12,256]{1,0:T(8,128)S(1)} %copy-done.82, bf16[1024,12,64]{0,2,1:T(8,128)(2,1)} %bitcast.383, bf16[1024,12,64]{0,2,1:T(8,128)(2,1)S(1)} %multiply_convert_fusion.5), kind=kOutput, calls=%fused_computation.15 | convolution fusion | flops 412087296 | bytes 27160576 | tf_op jit(solution)/shard_map/ihe,jhe->hij/dot_general | solution.py:142
  318.0 6.1 multiply_convert_fusion.1
  329.4 7.4 %multiply_reduce_fusion.2 = (f32[12,256]{1,0:T(8,128)S(1)}, f32[12,256,1024]{2,1,0:T(8,128)}) fusion(f32[12,256,1024]{2,1,0:T(8,128)S(1)} %bitcast.290, f32[12,256]{1,0:T(8,128)S(1)} %copy-done.81, bf16[1024,12,64]{0,2,1:T(8,128)(2,1)} %bitcast.384, bf16[1024,12,64]{0,2,1:T(8,128)(2,1)S(1)} %copy-done.40), kind=kOutput, calls=%fused_computation.17 | convolution fusion | flops 412087296 | bytes 27160576 | tf_op jit(solution)/shard_map/ihe,jhe->hij/dot_general | solution.py:142
  336.8 5.9 multiply_convert_fusion.2
  344.8 2.8 fusion.142
  348.9 7.6 %multiply_reduce_fusion.3 = (f32[12,256]{1,0:T(8,128)S(1)}, f32[12,256,1024]{2,1,0:T(8,128)}) fusion(f32[12,256,1024]{2,1,0:T(8,128)S(1)} %bitcast.282, f32[12,256]{1,0:T(8,128)S(1)} %copy-done.76, bf16[1024,12,64]{0,2,1:T(8,128)(2,1)} %bitcast.385, bf16[1024,12,64]{0,2,1:T(8,128)(2,1)S(1)} %copy-done.40), kind=kOutput, calls=%fused_computation.19 | convolution fusion | flops 412087296 | bytes 27160576 | tf_op jit(solution)/shard_map/ihe,jhe->hij/dot_general | solution.py:142
  356.4 5.9 multiply_convert_fusion.3
  364.5 2.9 fusion.141
  368.5 5.9 multiply_convert_fusion
  378.0 2.5 convolution_convert_fusion.13
  391.0 4.3 convolution_convert_fusion.10
  396.7 3.5 convolution_convert_fusion.9
  406.6 6.3 bitcast_reduce_fusion.1
  413.5 4.3 convolution_convert_fusion.11
  426.8 6.4 add_convert_fusion.2
  438.1 3.7 pad_maximum_fusion.1
  443.7 10.5 %convolution_convert_fusion.1 = bf16[768,3072]{1,0:T(8,128)(2,1)} fusion(bf16[1024,3072]{1,0:T(8,128)(2,1)} %get-tuple-element.117, f32[1024,768]{0,1:T(8,128)S(1)} %copy-done.15, f32[768]{0:T(1024)S(1)} %copy-done.95, f32[768]{0:T(1024)S(1)} %copy-done.72, f32[1024]{0:T(1024)S(1)} %copy-done.74, f32[1024]{0:T(1024)S(1)} %copy-done.67), kind=kOutput, calls=%fused_computation.49 | convolution fusion | flops 4838129664 | bytes 14170112 | tf_op jit(solution)/shard_map/dot_general | solution.py:40
  454.2 9.9 %convert_element_type.322 = bf16[768,4,768]{2,1,0:T(4,128)(2,1)} reshape(bf16[768,3072]{1,0:T(8,128)(2,1)} %convolution_convert_fusion.1) | data formatting | bytes 9437184 | tf_op jit(solution)/shard_map/convert_element_type | solution.py:301
  464.1 3.9 copy.112
  468.1 8.6 %convolution_convert_fusion = bf16[3072,768]{1,0:T(8,128)(2,1)S(1)} fusion(bf16[1024,3072]{1,0:T(8,128)(2,1)} %get-tuple-element.95, f32[1024,768]{0,1:T(8,128)S(1)} %copy-done.22), kind=kOutput, calls=%fused_computation.48 | convolution fusion | flops 4834983936 | bytes 14155776 | tf_op jit(solution)/shard_map/dot_general | solution.py:40
  476.7 4.0 pad_maximum_fusion
  481.5 7.6 %copy.94 = bf16[1,1024,768]{2,0,1:T(2,128)(2,1)S(1)} copy(bf16[1,1024,768]{1,2,0:T(8,128)(2,1)} %get-tuple-element.66) | data formatting | bytes 3145728 | tf_op jit(solution)/shard_map/stack | solution.py:296
  489.7 11.8 %reduce.65 = bf16[1024,768]{1,0:T(8,128)(2,1)} reduce(bf16[1024,1,768]{2,1,0:T(2,128)(2,1)S(1)} %bitcast.293, bf16[]{:T(256)} %broadcast.289), dimensions={1}, to_apply=%bitcast.153.reduce_sub_computation | reduce | bytes 3145730
  501.5 3.9 reshape.661
  505.3 4.5 all-to-all-start.1
  519.1 3.7 fusion.51
  522.8 7.6 %copy.105 = bf16[1,1024,768]{2,0,1:T(2,128)(2,1)S(1)} copy(bf16[1,1024,768]{1,2,0:T(8,128)(2,1)} %fusion.51) | data formatting | bytes 3145728 | tf_op jit(solution)/shard_map/stack | solution.py:297
  530.4 11.8 %reduce.66 = bf16[1024,768]{1,0:T(8,128)(2,1)} reduce(bf16[1024,1,768]{2,1,0:T(2,128)(2,1)S(1)} %bitcast.294, bf16[]{:T(256)} %broadcast.289), dimensions={1}, to_apply=%bitcast.155.reduce_sub_computation | reduce | bytes 3145730
  542.2 3.8 reshape.663
  546.0 5.1 all-to-all-start.3
  551.1 41.6 %reduce-scatter.5.cloned.1.call-done = bf16[1,768,768]{2,1,0:T(8,128)(2,1)} async-done(((bf16[8,768,768]{2,1,0:T(8,128)(2,1)}), bf16[1,768,768]{2,1,0:T(8,128)(2,1)}) %reduce-scatter.5.cloned.1.call-update) | async-done | bytes 1179664 | tf_op jit(solution)/shard_map/reduce_scatter | solution.py:330
  592.8 3.1 reshape.662
  597.2 3.1 reshape.664
  601.7 85.1 %all-reduce.5.cloned.1.call-done = (bf16[674,768]{1,0:T(8,128)(2,1)}, bf16[768,768]{1,0:T(8,128)(2,1)}) async-done(((bf16[674,768]{1,0:T(8,128)(2,1)}, bf16[768,768]{1,0:T(8,128)(2,1)}), (bf16[674,768]{1,0:T(8,128)(2,1)}, bf16[768,768]{1,0:T(8,128)(2,1)})) %all-reduce.5.cloned.1.call-update) | async-done | bytes 2214928 | tf_op jit(solution)/shard_map/psum | solution.py:331
  690.5 2.5 fusion.130
  (410 shorter events, 124.6 us)
Async XLA Ops:
  7.2 55.6 %copy-start = (s32[4,4]{1,0:T(4,128)S(1)}, s32[4,4]{1,0:T(4,128)}, u32[]{:S(2)}) copy-start(s32[4,4]{1,0:T(4,128)} %param.13) | copy-start | bytes 196
  7.2 5.5 copy-start.35
  7.2 91.1 %all-gather.8.cloned.1.call-start = ((), (), s32[]{:S(2)}) async-start(), calls=%async_computation.9 | async-start | bytes 9400320 | tf_op jit(solution)/shard_map/all_gather | solution.py:254
  55.8 10.6 %copy-start.6 = (bf16[4,256,768]{2,1,0:T(8,128)(2,1)}, bf16[4,256,768]{2,1,0:T(8,128)(2,1)S(1)}, u32[]{:S(2)}) copy-start(bf16[4,256,768]{2,1,0:T(8,128)(2,1)S(1)} %all_to_all.42) | copy-start | bytes 4718596
  55.8 39.7 %all-to-all-start.2 = ((bf16[4,256,768]{2,1,0:T(8,128)(2,1)}), bf16[4,256,768]{2,1,0:T(8,128)(2,1)S(1)}, u32[]{:S(2)}, u32[]{:S(2)}) async-start(bf16[4,256,768]{2,1,0:T(8,128)(2,1)} %param.23), calls=%async_computation.2 | async-start | bytes 3145728 | tf_op jit(solution)/shard_map/all_to_all | solution.py:234
  59.4 147.3 %all-gather.6.cloned.1.call-start = ((), (), s32[]{:S(2)}) async-start(), calls=%async_computation.8 | async-start | bytes 10616832 | tf_op jit(solution)/shard_map/all_gather | solution.py:255
  62.7 488.4 %reduce-scatter.3.cloned.1.call-start = ((), (), s32[]{:S(2)}) async-start(), calls=%async_computation.6 | async-start | bytes 9400320 | tf_op jit(solution)/shard_map/reduce_scatter | solution.py:330
  62.8 33.0 %copy-start.86 = (s32[4]{0:T(128)}, s32[4]{0:T(128)S(1)}, u32[]{:S(2)}) copy-start(s32[4]{0:T(128)S(1)} %dynamic-slice_bitcast_fusion) | copy-start | bytes 52
  101.0 168.0 %copy-start.71 = (f32[768]{0:T(1024)}, f32[768]{0:T(1024)S(1)}, u32[]{:S(2)}) copy-start(f32[768]{0:T(1024)S(1)} %mul.222) | copy-start | bytes 9220
  113.9 5.7 copy-start.7
  113.9 5.7 copy-start.47
  129.3 39.1 %copy-start.23 = (bf16[256,768]{0,1:T(8,128)(2,1)}, bf16[256,768]{0,1:T(8,128)(2,1)S(1)}, u32[]{:S(2)}) copy-start(bf16[256,768]{0,1:T(8,128)(2,1)S(1)} %get-tuple-element.67) | copy-start | bytes 1179652
  179.6 6.5 copy-start.82
  179.6 6.5 copy-start.100
  186.1 6.0 copy-start.80
  186.1 12.0 %slice-start = ((s8[12582912]{0:T(1024)(128)(4,1)}), s8[4194304]{0:T(1024)(128)(4,1)S(1)}, s32[]{:S(2)}) async-start(s8[12582912]{0:T(1024)(128)(4,1)} %bitcast.279), calls=%async_computation.11 | async-start | bytes 8388608
  186.1 12.0 %slice-start.1 = ((s8[12582912]{0:T(1024)(128)(4,1)}), s8[4194304]{0:T(1024)(128)(4,1)S(1)}, s32[]{:S(2)}) async-start(s8[12582912]{0:T(1024)(128)(4,1)} %bitcast.279), calls=%async_computation.12 | async-start | bytes 8388608
  192.1 6.1 slice-start.2
  192.1 6.1 copy-start.75
  204.5 64.4 %copy-start.66 = (f32[1024]{0:T(1024)}, f32[1024]{0:T(1024)S(1)}, u32[]{:S(2)}) copy-start(f32[1024]{0:T(1024)S(1)} %broadcast_multiply_fusion.4) | copy-start | bytes 12292
  206.7 62.3 %copy-start.73 = (f32[1024]{0:T(1024)}, f32[1024]{0:T(1024)S(1)}, u32[]{:S(2)}) copy-start(f32[1024]{0:T(1024)S(1)} %add_rsqrt_fusion.1) | copy-start | bytes 12292
  206.7 6.8 copy-start.18
  217.1 14.3 %copy-start.19 = (bf16[8,384,768]{2,1,0:T(8,128)(2,1)S(1)}, bf16[8,384,768]{2,1,0:T(8,128)(2,1)}, u32[]{:S(2)}) copy-start(bf16[8,384,768]{2,1,0:T(8,128)(2,1)} %slice.245) | copy-start | bytes 14155780
  217.1 14.3 %copy-start.96 = (f32[768]{0:T(1024)S(1)}, f32[768]{0:T(1024)}, u32[]{:S(2)}) copy-start(f32[768]{0:T(1024)} %add.238) | copy-start | bytes 9220
  244.4 15.1 %copy-start.21 = (f32[1024,768]{0,1:T(8,128)}, f32[1024,768]{0,1:T(8,128)S(1)}, u32[]{:S(2)}) copy-start(f32[1024,768]{0,1:T(8,128)S(1)} %get-tuple-element.52) | copy-start | bytes 9437188
  244.4 15.1 %copy-start.53 = (bf16[8,96,768]{2,1,0:T(8,128)(2,1)S(1)}, bf16[8,96,768]{2,1,0:T(8,128)(2,1)}, u32[]{:S(2)}) copy-start(bf16[8,96,768]{2,1,0:T(8,128)(2,1)} %get-tuple-element.55) | copy-start | bytes 3538948
  244.4 15.1 %copy-start.54 = (bf16[8,96,768]{2,1,0:T(8,128)(2,1)S(1)}, bf16[8,96,768]{2,1,0:T(8,128)(2,1)}, u32[]{:S(2)}) copy-start(bf16[8,96,768]{2,1,0:T(8,128)(2,1)} %get-tuple-element.56) | copy-start | bytes 3538948
  244.4 15.1 %copy-start.55 = (bf16[8,96,768]{2,1,0:T(8,128)(2,1)S(1)}, bf16[8,96,768]{2,1,0:T(8,128)(2,1)}, u32[]{:S(2)}) copy-start(bf16[8,96,768]{2,1,0:T(8,128)(2,1)} %get-tuple-element.57) | copy-start | bytes 3538948
  244.4 15.1 %copy-start.56 = (bf16[8,96,768]{2,1,0:T(8,128)(2,1)S(1)}, bf16[8,96,768]{2,1,0:T(8,128)(2,1)}, u32[]{:S(2)}) copy-start(bf16[8,96,768]{2,1,0:T(8,128)(2,1)} %get-tuple-element.58) | copy-start | bytes 3538948
  275.8 34.8 %copy-start.39 = (bf16[1024,12,64]{0,2,1:T(8,128)(2,1)}, bf16[1024,12,64]{0,2,1:T(8,128)(2,1)S(1)}, u32[]{:S(2)}) copy-start(bf16[1024,12,64]{0,2,1:T(8,128)(2,1)S(1)} %multiply_convert_fusion.5) | copy-start | bytes 4718596
  276.1 4.1 copy-start.60
  282.7 16.4 %slice-start.9 = ((s8[12582912]{0:T(1024)(128)(4,1)}), s8[4194304]{0:T(1024)(128)(4,1)S(1)}, s32[]{:S(2)}) async-start(s8[12582912]{0:T(1024)(128)(4,1)} %bitcast.285), calls=%async_computation.20 | async-start | bytes 8388608
  282.7 16.4 %slice-start.10 = ((s8[12582912]{0:T(1024)(128)(4,1)}), s8[4194304]{0:T(1024)(128)(4,1)S(1)}, s32[]{:S(2)}) async-start(s8[12582912]{0:T(1024)(128)(4,1)} %bitcast.285), calls=%async_computation.21 | async-start | bytes 8388608
  290.7 8.4 %slice-start.11 = ((s8[12582912]{0:T(1024)(128)(4,1)}), s8[4194304]{0:T(1024)(128)(4,1)S(1)}, s32[]{:S(2)}) async-start(s8[12582912]{0:T(1024)(128)(4,1)} %bitcast.285), calls=%async_computation.22 | async-start | bytes 8388608
  290.7 8.4 %copy-start.78 = (f32[12,256]{1,0:T(8,128)S(1)}, f32[12,256]{1,0:T(8,128)}, u32[]{:S(2)}) copy-start(f32[12,256]{1,0:T(8,128)} %get-tuple-element.83) | copy-start | bytes 36868
  299.1 11.5 %slice-start.18 = ((s8[12582912]{0:T(1024)(128)(4,1)}), s8[4194304]{0:T(1024)(128)(4,1)S(1)}, s32[]{:S(2)}) async-start(s8[12582912]{0:T(1024)(128)(4,1)} %bitcast.291), calls=%async_computation.29 | async-start | bytes 8388608
  299.1 11.5 %slice-start.19 = ((s8[12582912]{0:T(1024)(128)(4,1)}), s8[4194304]{0:T(1024)(128)(4,1)S(1)}, s32[]{:S(2)}) async-start(s8[12582912]{0:T(1024)(128)(4,1)} %bitcast.291), calls=%async_computation.30 | async-start | bytes 8388608
  302.4 8.2 %slice-start.20 = ((s8[12582912]{0:T(1024)(128)(4,1)}), s8[4194304]{0:T(1024)(128)(4,1)S(1)}, s32[]{:S(2)}) async-start(s8[12582912]{0:T(1024)(128)(4,1)} %bitcast.291), calls=%async_computation.31 | async-start | bytes 8388608
  318.0 6.1 copy-start.4
  318.0 8.1 %copy-start.26 = (bf16[256,768]{0,1:T(8,128)(2,1)S(1)}, bf16[256,768]{0,1:T(8,128)(2,1)}, u32[]{:S(2)}) copy-start(bf16[256,768]{0,1:T(8,128)(2,1)} %get-tuple-element.69) | copy-start | bytes 1179652
  336.8 8.0 %copy-start.25 = (bf16[256,768]{0,1:T(8,128)(2,1)S(1)}, bf16[256,768]{0,1:T(8,128)(2,1)}, u32[]{:S(2)}) copy-start(bf16[256,768]{0,1:T(8,128)(2,1)} %get-tuple-element.70) | copy-start | bytes 1179652
  342.7 4.9 slice-start.3
  342.7 4.9 slice-start.4
  344.8 33.2 %copy-start.27 = (bf16[12,64,256]{2,1,0:T(8,128)(2,1)}, bf16[12,64,256]{2,1,0:T(8,128)(2,1)S(1)}, u32[]{:S(2)}) copy-start(bf16[12,64,256]{2,1,0:T(8,128)(2,1)S(1)} %convolution_convert_fusion.16) | copy-start | bytes 1179652
  356.4 8.0 %copy-start.24 = (bf16[256,768]{0,1:T(8,128)(2,1)S(1)}, bf16[256,768]{0,1:T(8,128)(2,1)}, u32[]{:S(2)}) copy-start(bf16[256,768]{0,1:T(8,128)(2,1)} %copy-done.23) | copy-start | bytes 1179652
  362.4 5.0 slice-start.12
  362.4 5.0 slice-start.13
  364.4 13.6 %copy-start.29 = (bf16[12,64,256]{2,1,0:T(8,128)(2,1)}, bf16[12,64,256]{2,1,0:T(8,128)(2,1)S(1)}, u32[]{:S(2)}) copy-start(bf16[12,64,256]{2,1,0:T(8,128)(2,1)S(1)} %convolution_convert_fusion.17) | copy-start | bytes 1179652
  364.4 4.0 slice-start.14
  378.0 6.0 copy-start.89
  378.0 8.8 %copy-start.90 = (bf16[768]{0:T(1024)(128)(2,1)S(1)}, bf16[768]{0:T(1024)(128)(2,1)}, u32[]{:S(2)}) copy-start(bf16[768]{0:T(1024)(128)(2,1)} %get-tuple-element.53) | copy-start | bytes 4612
  391.0 9.2 %copy-start.70 = (bf16[8,96,4]{1,0,2:T(8,128)(2,1)S(1)}, bf16[8,96,4]{1,0,2:T(8,128)(2,1)}, u32[]{:S(2)}) copy-start(bf16[8,96,4]{1,0,2:T(8,128)(2,1)} %reshape.581) | copy-start | bytes 18436
  396.7 8.7 %slice-start.6 = ((s8[12582912]{0:T(1024)(128)(4,1)}), s8[4194304]{0:T(1024)(128)(4,1)S(1)}, s32[]{:S(2)}) async-start(s8[12582912]{0:T(1024)(128)(4,1)} %bitcast.283), calls=%async_computation.17 | async-start | bytes 8388608
  396.7 8.7 %slice-start.7 = ((s8[12582912]{0:T(1024)(128)(4,1)}), s8[4194304]{0:T(1024)(128)(4,1)S(1)}, s32[]{:S(2)}) async-start(s8[12582912]{0:T(1024)(128)(4,1)} %bitcast.283), calls=%async_computation.18 | async-start | bytes 8388608
  413.5 4.3 copy-start.91
  413.5 6.4 copy-start.92
  426.8 6.4 copy-start.10
  441.9 150.9 %reduce-scatter.5.cloned.1.call-start = ((), (), s32[]{:S(2)}) async-start(), calls=%async_computation.7 | async-start | bytes 10616832 | tf_op jit(solution)/shard_map/reduce_scatter | solution.py:330
  501.5 8.4 %copy-start.41 = (bf16[12,64,1024]{2,1,0:T(8,128)(2,1)S(1)}, bf16[12,64,1024]{2,1,0:T(8,128)(2,1)}, u32[]{:S(2)}) copy-start(bf16[12,64,1024]{2,1,0:T(8,128)(2,1)} %convolution_convert_fusion.3) | copy-start | bytes 4718596
  501.5 8.4 %copy-start.49 = (bf16[8,96,768]{2,1,0:T(8,128)(2,1)S(1)}, bf16[8,96,768]{2,1,0:T(8,128)(2,1)}, u32[]{:S(2)}) copy-start(bf16[8,96,768]{2,1,0:T(8,128)(2,1)} %get-tuple-element.60) | copy-start | bytes 3538948
  505.3 40.7 %all-to-all-start.1 = ((bf16[4,2,98304]{2,1,0:T(2,128)(2,1)}), bf16[4,2,98304]{2,1,0:T(2,128)(2,1)}, u32[]{:S(2)}, u32[]{:S(2)}) async-start(bf16[4,2,98304]{2,1,0:T(2,128)(2,1)} %reshape.661), calls=%async_computation.1 | async-start | bytes 3145728 | tf_op jit(solution)/shard_map/all_to_all | solution.py:237
  546.0 51.2 %all-to-all-start.3 = ((bf16[4,2,98304]{2,1,0:T(2,128)(2,1)}), bf16[4,2,98304]{2,1,0:T(2,128)(2,1)}, u32[]{:S(2)}, u32[]{:S(2)}) async-start(bf16[4,2,98304]{2,1,0:T(2,128)(2,1)} %reshape.663), calls=%async_computation.3 | async-start | bytes 3145728 | tf_op jit(solution)/shard_map/all_to_all | solution.py:237
  551.1 135.7 %all-reduce.5.cloned.1.call-start = ((), (), s32[]{:S(2)}) async-start(), calls=%async_computation.10 | async-start | bytes 4448256 | tf_op jit(solution)/shard_map/psum | solution.py:331
  686.8 6.8 copy-start.20
  (72 other events, 167.4 us)
Sparse Core Ops, SparseCore 0:
  12.8 56.9 all-gather.7
  72.3 58.8 all-gather.5
  442.0 70.4 reduce-scatter.2
  516.3 76.4 reduce-scatter.4
  595.2 91.5 all-reduce.4

commit v2 on v1

--- a/solution.py
+++ b/solution.py
@@ -1,14 +1,17 @@
 import jax
 import jax.numpy as jnp
 from jax import lax
+from jax.experimental import pallas as pl
+from jax.experimental.pallas import tpu as pltpu
 from jax.sharding import PartitionSpec as P
 
 HEADS = 12
 HEAD_DIM = 64
 WIN = 256
+QB = 128
+NEG = -1e9
 
 HIGHEST = lax.Precision.HIGHEST
-MASKED_SCORE = -1000000000.0
 NORM_EPS = 1e-05
 BF = jnp.bfloat16
 F32 = jnp.float32
@@ -46,60 +49,189 @@
     return (inner * cdf, cdf + inner * pdf)
 
 
+def dot_nn(a,b): return jnp.dot(a,b,preferred_element_type=F32)
+def dot_nt(a,b): return lax.dot_general(a,b,(((1,),(1,)),((),())),preferred_element_type=F32)
+def dot_tn(a,b): return lax.dot_general(a,b,(((0,),(0,)),((),())),preferred_element_type=F32)
+
+def split_pair(block):
+    lane=lax.broadcasted_iota(jnp.int32,block.shape,1)
+    zero=jnp.zeros_like(block)
+    return jnp.concatenate([jnp.where(lane<HEAD_DIM,block,zero),jnp.where(lane<HEAD_DIM,zero,block)],axis=0)
+
+def far_mask(pos, start):
+    place=start+lax.broadcasted_iota(jnp.int32,(16,2*QB),1)%QB
+    return (pos>=0)&(jnp.abs(place-pos)>WIN)
+
+def edge_masks():
+    row=lax.broadcasted_iota(jnp.int32,(QB,2*QB),0)
+    col=lax.broadcasted_iota(jnp.int32,(QB,2*QB),1)%QB
+    return row>=col, row<=col
+
+def key_range(start,length):
+    return max(0,start-WIN), min(length,start+QB+WIN)
+
+def pick_head(both):
+    row=lax.broadcasted_iota(jnp.int32,(2*HEAD_DIM,QB),0)
+    return jnp.where(row<HEAD_DIM,both[:,:QB],both[:,QB:])
+
+def masked_scores(raw,start,length,low_ok,high_ok):
+    lo,hi=key_range(start,length)
+    parts=[]
+    for first in range(lo,hi,QB):
+        chunk=raw[first-lo:first-lo+QB]
+        if first==start-WIN: chunk=jnp.where(low_ok,chunk,NEG)
+        elif first==start+WIN: chunk=jnp.where(high_ok,chunk,NEG)
+        parts.append(chunk)
+    return parts
+
+def fwd_kernel(pos_ref,q_ref,k_ref,v_ref,ctx_ref,lse_ref):
+    length=q_ref.shape[0]
+    pos=pos_ref[...]
+    token=lax.broadcasted_iota(jnp.int32,(16,length),1)
+    sel=jnp.where(token==pos,1.0,0.0).astype(BF)
+    key_far=dot_nn(sel,k_ref[...]).astype(BF)
+    val_far_t=dot_nn(sel,v_ref[...]).astype(BF).T
+    val_t=v_ref[...].T
+    low_ok,high_ok=edge_masks()
+    for start in range(0,length,QB):
+        lo,hi=key_range(start,length)
+        qq=split_pair(q_ref[start:start+QB,:])
+        raw=dot_nt(k_ref[lo:hi,:],qq)
+        parts=masked_scores(raw,start,length,low_ok,high_ok)
+        far=jnp.where(far_mask(pos,start),dot_nt(key_far,qq),NEG)
+        top=jnp.max(far,axis=0,keepdims=True)
+        for part in parts: top=jnp.maximum(top,jnp.max(part,axis=0,keepdims=True))
+        far_p=jnp.exp(far-top)
+        total=jnp.sum(far_p,axis=0,keepdims=True)
+        probs=[]
+        for part in parts:
+            p=jnp.exp(part-top)
+            total=total+jnp.sum(p,axis=0,keepdims=True)
+            probs.append(p.astype(BF))
+        both=dot_nn(val_t[:,lo:hi],jnp.concatenate(probs,axis=0))+dot_nn(val_far_t,far_p.astype(BF))
+        both=both*(1.0/total)
+        ctx_ref[start:start+QB,:]=pick_head(both).T.astype(BF)
+        lse=top+jnp.log(total)
+        lse_ref[0,0:1,start:start+QB]=lse[:,:QB]
+        lse_ref[0,1:2,start:start+QB]=lse[:,QB:]
+
+def attn_fwd(pos,q,k,v):
+    length,width=q.shape
+    pairs=width//128
+    col=pl.BlockSpec((length,128),lambda i:(0,i))
+    return pl.pallas_call(fwd_kernel,grid=(pairs,),
+        in_specs=[pl.BlockSpec((16,1),lambda i:(0,0)),col,col,col],
+        out_specs=[col,pl.BlockSpec((1,8,length),lambda i:(i,0,0))],
+        out_shape=[jax.ShapeDtypeStruct((length,width),BF),jax.ShapeDtypeStruct((pairs,8,length),F32)],
+        compiler_params=pltpu.CompilerParams(vmem_limit_bytes=32<<20),
+        cost_estimate=pl.CostEstimate(flops=int(20e9),bytes_accessed=8<<20,transcendentals=8<<20),
+        name="attend")(pos,q,k,v)
+
+def bwd_kernel(pos_ref,q_ref,k_ref,v_ref,g_ref,ctx_ref,lse_ref,dq_ref,dk_ref,dv_ref,dk_acc,dv_acc,grad_scr):
+    length=q_ref.shape[0]
+    pos=pos_ref[...]
+    token=lax.broadcasted_iota(jnp.int32,(16,length),1)
+    sel_bool=token==pos
+    sel=jnp.where(sel_bool,1.0,0.0).astype(BF)
+    sel_full=jnp.where(sel_bool,1.0,0.0)
+    key_far=dot_nn(sel,k_ref[...]).astype(BF)
+    val_far=dot_nn(sel,v_ref[...]).astype(BF)
+    key_far_t=key_far.T
+    key_t=k_ref[...].T
+    ones=jnp.ones((16,128),F32)
+    is_glob=lax.dot_general(sel_full,ones,(((0,),(0,)),((),())),preferred_element_type=F32)
+    grad_scr[...]=jnp.where(is_glob>0.5,0.0,g_ref[...].astype(F32)).astype(BF)
+    prod=grad_scr[...].astype(F32)*ctx_ref[...].astype(F32)
+    hrow=lax.broadcasted_iota(jnp.int32,(16,128),0)
+    hlane=lax.broadcasted_iota(jnp.int32,(16,128),1)//HEAD_DIM
+    hsel=jnp.where(hrow==hlane,1.0,0.0)
+    delta_all=lax.dot_general(hsel,prod,(((1,),(1,)),((),())),preferred_element_type=F32,precision=lax.Precision.HIGHEST)
+    dk_acc[...]=jnp.zeros_like(dk_acc)
+    dv_acc[...]=jnp.zeros_like(dv_acc)
+    dk_far=jnp.zeros((16,128),F32); dv_far=jnp.zeros((16,128),F32)
+    low_ok,high_ok=edge_masks()
+    for start in range(0,length,QB):
+        lo,hi=key_range(start,length)
+        qq=split_pair(q_ref[start:start+QB,:])
+        gg=split_pair(grad_scr[start:start+QB,:])
+        lse=jnp.concatenate([lse_ref[0,0:1,start:start+QB],lse_ref[0,1:2,start:start+QB]],axis=1)
+        delta=jnp.concatenate([delta_all[0:1,start:start+QB],delta_all[1:2,start:start+QB]],axis=1)
+        dq_t=jnp.zeros((128,2*QB),F32)
+        def one(scores,vals):
+            p=jnp.exp(scores-lse)
+            dp=dot_nt(vals,gg)
+            return p.astype(BF),(p*(dp-delta)).astype(BF)
+        far=jnp.where(far_mask(pos,start),dot_nt(key_far,qq),NEG)
+        p,ds=one(far,val_far)
+        dv_far=dv_far+dot_nn(p,gg); dk_far=dk_far+dot_nn(ds,qq)
+        dq_t=dq_t+dot_nn(key_far_t,ds)
+        parts=masked_scores(dot_nt(k_ref[lo:hi,:],qq),start,length,low_ok,high_ok)
+        plist=[];dlist=[]
+        for n,part in enumerate(parts):
+            a=lo+n*QB
+            p,ds=one(part,v_ref[a:a+QB,:])
+            plist.append(p);dlist.append(ds)
+        p=jnp.concatenate(plist,axis=0); ds=jnp.concatenate(dlist,axis=0)
+        dv_acc[lo:hi,:]+=dot_nn(p,gg)
+        dk_acc[lo:hi,:]+=dot_nn(ds,qq)
+        dq_t=dq_t+dot_nn(key_t[:,lo:hi],ds)
+        dq_ref[start:start+QB,:]=pick_head(dq_t).T.astype(BF)
+    dk_ref[...]=(dk_acc[...]+lax.dot_general(sel_full,dk_far,(((0,),(0,)),((),())),preferred_element_type=F32,precision=lax.Precision.HIGHEST)).astype(BF)
+    dv_ref[...]=(dv_acc[...]+lax.dot_general(sel_full,dv_far,(((0,),(0,)),((),())),preferred_element_type=F32,precision=lax.Precision.HIGHEST)).astype(BF)
+
+def attn_bwd(pos,q,k,v,grad,ctx,lse):
+    length,width=q.shape
+    pairs=width//128
+    col=pl.BlockSpec((length,128),lambda i:(0,i))
+    out=jax.ShapeDtypeStruct((length,width),BF)
+    return pl.pallas_call(bwd_kernel,grid=(pairs,),
+        in_specs=[pl.BlockSpec((16,1),lambda i:(0,0)),col,col,col,col,col,pl.BlockSpec((1,8,length),lambda i:(i,0,0))],
+        out_specs=[col,col,col],
+        out_shape=[out,out,out],
+        scratch_shapes=[pltpu.VMEM((length,128),F32),pltpu.VMEM((length,128),F32),pltpu.VMEM((length,128),BF)],
+        compiler_params=pltpu.CompilerParams(vmem_limit_bytes=32<<20),
+        cost_estimate=pl.CostEstimate(flops=int(40e9),bytes_accessed=12<<20,transcendentals=8<<20),
+        name="attend_back")(pos,q,k,v,grad,ctx,lse)
+
+
 def sequence_step(x, positions, upstream_low, weights):
     w_local, w_global, w_out, b_proj, gains, shifts, w_in, c_in, w_back = weights
     length, width = x.shape
+    glob_count = positions.shape[0]
     scale = HEAD_DIM ** (-0.5)
     bias = b_proj.astype(F32)
     gain = gains.astype(F32)
     shift = shifts.astype(F32)
-
-    def heads(value):
-        return value.reshape(value.shape[0], HEADS, HEAD_DIM)
-
-    q = heads(((mm(x, w_local[0]) + bias[0]) * scale).astype(BF))
-    k = heads(mm(x, w_local[1]).astype(BF))
-    v = heads((mm(x, w_local[2]) + bias[1]).astype(BF))
-    kg = heads(mm(x, w_global[1]).astype(BF))
-    vg = heads((mm(x, w_global[2]) + bias[3]).astype(BF))
+    pos16 = jnp.full((16, 1), -1, jnp.int32).at[:glob_count, 0].set(positions)
+    q = ((mm(x, w_local[0]) + bias[0]) * scale).astype(BF)
+    k = mm(x, w_local[1]).astype(BF)
+    v = (mm(x, w_local[2]) + bias[1]).astype(BF)
+    ctx_loc, lse = attn_fwd(pos16, q, k, v)
     places = jnp.arange(length, dtype=jnp.int32)
     select = positions[:, None] == places[None, :]
     select_low = select.astype(BF)
-    select_full = select.astype(F32)
-    is_glob = jnp.sum(select_full, axis=0)
-    keep_local = 1.0 - is_glob
+    is_glob = jnp.any(select, axis=0)[:, None]
     rows_glob = mm(select_low, x).astype(BF)
-    qg = heads(((mm(rows_glob, w_global[0]) + bias[2]) * scale).astype(BF))
-    block = 256
-    offsets = list(range(0, length, block))
-
-    def block_scores(offset):
-        qb = q[offset : offset + block]
-        row_places = offset + jnp.arange(block, dtype=jnp.int32)
-        in_band = jnp.abs(row_places[:, None] - places[None, :]) <= WIN
-        allowed = in_band | (is_glob[None, :] > 0.5)
-        raw = jnp.einsum("ihe,jhe->hij", qb, k, preferred_element_type=F32)
-        return (qb, jnp.where(allowed[None], raw, MASKED_SCORE))
-
-    kept = []
-    contexts = []
-    for offset in offsets:
-        qb, masked = block_scores(offset)
-        top = jnp.max(masked, axis=-1, keepdims=True)
-        powers = jnp.exp(masked - top)
-        total = jnp.sum(powers, axis=-1, keepdims=True)
-        low = (powers / total).astype(BF)
-        contexts.append(jnp.einsum("hij,jhe->ihe", low, v, preferred_element_type=F32))
-        kept.append((top, total))
-    context_loc = jnp.concatenate(contexts, axis=0)
-    glob_scores = jnp.einsum("ghe,jhe->hgj", qg, kg, preferred_element_type=F32)
-    glob_probs = jax.nn.softmax(glob_scores, axis=-1)
+    head_of = jnp.arange(width, dtype=jnp.int32) // HEAD_DIM
+    own = head_of[None, :] == jnp.arange(16, dtype=jnp.int32)[:, None]
+
+    def spread(rows):
+        return jnp.where(own[None], rows[:, None, :], 0).reshape(-1, width)
+
+    def gather(rows):
+        return jnp.sum(jnp.where(own[None], rows.reshape(glob_count, 16, width), 0), axis=1)
+
+    qg = ((mm(rows_glob, w_global[0]) + bias[2]) * scale).astype(BF)
+    q_spread = spread(qg)
+    key_map = mm_nt(w_global[1], q_spread).astype(BF)
+    glob_scores = mm(x, key_map)
+    glob_probs = jax.nn.softmax(glob_scores, axis=0)
     glob_low = glob_probs.astype(BF)
-    context_glob = jnp.einsum("hgj,jhe->ghe", glob_low, vg, preferred_element_type=F32)
-    context = context_loc * keep_local[:, None, None] + jnp.einsum(
-        "gl,ghe->lhe", select_full, context_glob, precision=HIGHEST
-    )
-    merged = context.astype(BF).reshape(length, width)
+    mixed = mm_tn(glob_low, x)
+    glob_mass = jnp.sum(glob_low.astype(F32), axis=0)
+    ctx_glob = gather(mm(mixed.astype(BF), w_global[2]) + glob_mass[:, None] * bias[3])
+    ctx_glob = ctx_glob.astype(BF)
+    merged = jnp.where(is_glob, mm_tn(select_low, ctx_glob).astype(BF), ctx_loc)
     attended = mm(merged, w_out) + bias[4]
     normed_one, inverse_one = normalize(x.astype(F32) + attended)
     first_norm = normed_one * gain[0] + shift[0]
@@ -126,54 +258,36 @@
     attn_grad = grad_sum_one.astype(BF)
     grad_out_w = mm_tn(merged, attn_grad)
     grad_att_bias = jnp.sum(attn_grad.astype(F32), axis=0)
-    ctx_grad = heads(mm_nt(attn_grad, w_out).astype(BF))
-    local_grad = (ctx_grad.astype(F32) * keep_local[:, None, None]).astype(BF)
-    glob_ctx_grad = jnp.einsum(
-        "gl,lhe->ghe", select_low, ctx_grad, preferred_element_type=F32
-    ).astype(BF)
-    key_grad = jnp.zeros(k.shape, F32)
-    value_grad = jnp.zeros(v.shape, F32)
-    query_parts = []
-    for index, offset in enumerate(offsets):
-        qb, masked = block_scores(offset)
-        probs = jnp.exp(masked - kept[index][0]) / kept[index][1]
-        low = probs.astype(BF)
-        gb = local_grad[offset : offset + block]
-        grad_probs = jnp.einsum("ihe,jhe->hij", gb, v, preferred_element_type=F32)
-        dot = jnp.sum(probs * grad_probs, axis=-1, keepdims=True)
-        score_grad = (probs * (grad_probs - dot)).astype(BF)
-        query_parts.append(jnp.einsum("hij,jhe->ihe", score_grad, k, preferred_element_type=F32))
-        key_grad = key_grad + jnp.einsum(
-            "hij,ihe->jhe", score_grad, qb, preferred_element_type=F32
-        )
-        value_grad = value_grad + jnp.einsum("hij,ihe->jhe", low, gb, preferred_element_type=F32)
-    dq = jnp.concatenate(query_parts, axis=0).astype(BF)
-    glob_grad_probs = jnp.einsum("ghe,jhe->hgj", glob_ctx_grad, vg, preferred_element_type=F32)
-    glob_dot = jnp.sum(glob_probs * glob_grad_probs, axis=-1, keepdims=True)
-    glob_score_grad = (glob_probs * (glob_grad_probs - glob_dot)).astype(BF)
-    dqg = jnp.einsum("hgj,jhe->ghe", glob_score_grad, kg, preferred_element_type=F32).astype(BF)
-    dkg = jnp.einsum("hgj,ghe->jhe", glob_score_grad, qg, preferred_element_type=F32).astype(BF)
-    dvg = jnp.einsum("hgj,ghe->jhe", glob_low, glob_ctx_grad, preferred_element_type=F32).astype(BF)
-
-    def flat(value):
-        return value.astype(BF).reshape(value.shape[0], width)
-
-    dq, dk, dv, dkg, dvg = (flat(value) for value in (dq, key_grad, value_grad, dkg, dvg))
+    ctx_grad = mm_nt(attn_grad, w_out).astype(BF)
+    dq, dk, dv = attn_bwd(pos16, q, k, v, ctx_grad, merged, lse)
     pre_query = dq * scale
-    glob_pre = flat(dqg) * scale
+    glob_ctx_grad = mm(select_low, ctx_grad).astype(BF)
+    c_spread = spread(glob_ctx_grad)
+    value_map = mm_nt(w_global[2], c_spread).astype(BF)
+    glob_grad_probs = mm(x, value_map) + mm_nt(bias[3:4].astype(BF), c_spread)
+    glob_dot = jnp.sum(glob_probs * glob_grad_probs, axis=0, keepdims=True)
+    glob_ds = (glob_probs * (glob_grad_probs - glob_dot)).astype(BF)
+    key_mixed = mm_tn(glob_ds, x)
+    dqg = gather(mm(key_mixed.astype(BF), w_global[1])).astype(BF)
+    glob_pre = dqg * scale
     token_grad = (
         grad_sum_one
         + mm_nt(pre_query, w_local[0])
         + mm_nt(dk, w_local[1])
         + mm_nt(dv, w_local[2])
-        + mm_nt(dkg, w_global[1])
-        + mm_nt(dvg, w_global[2])
-    )
-    token_grad = token_grad + jnp.einsum(
-        "gr,gd->rd", select_full, mm_nt(glob_pre, w_global[0]), precision=HIGHEST
-    )
+        + mm_nt(glob_ds, key_map)
+        + mm_nt(glob_low, value_map)
+    )
+    rows_grad = mm_nt(glob_pre, w_global[0])
+    token_grad = token_grad + mm_tn(select.astype(F32), rows_grad)
     grad_local = jnp.stack([mm_tn(x, pre_query), mm_tn(x, dk), mm_tn(x, dv)])
-    grad_global = jnp.stack([mm_tn(rows_glob, glob_pre), mm_tn(x, dkg), mm_tn(x, dvg)])
+    grad_global = jnp.stack(
+        [
+            mm_tn(rows_glob, glob_pre),
+            mm_tn(key_mixed.astype(BF), q_spread),
+            mm_tn(mixed.astype(BF), c_spread),
+        ]
+    )
 
     def total_of(value):
         return jnp.sum(value.astype(F32), axis=0)
@@ -183,7 +297,7 @@
             total_of(pre_query),
             total_of(dv),
             total_of(glob_pre),
-            total_of(dvg),
+            jnp.sum(glob_mass[:, None] * c_spread.astype(F32), axis=0),
             grad_att_bias,
             grad_out_bias,
         ]

time: 709 us -> 560 us (0.79)
  matrix products: 269 us -> 121 us
  Pallas kernels: 0 us -> 60.4 us
  other arithmetic: 77.2 us -> 42.8 us
  local copies, waits for them, and re-layouts: 129 us -> 96.1 us
    dot_general x29 -> x0, matrix products: 115 us -> none  [the longest x4 30.6 us: sequence_step(): grad_probs = jnp.einsum('ihe,jhe->hij', gb, v, preferred_element_type=F32)]
    pallas_call x0 -> x2, Pallas kernels: none -> 60.4 us  [the longest x1 35.4 us: attn_bwd(): pl.pallas_call(bwd_kernel, grid=(pairs,), in_specs=[pl.BlockSpec((16, 1),...]
    sub x4 -> x0, matrix products: 43.7 us -> none  [sequence_step(): powers = jnp.exp(masked - top)]
    all_to_all x2, waiting for transfers between devices: 0.01 us -> 34.5 us  [to_tokens(): return lax.all_to_all(value, 'sp', split_axis=1, concat_axis=0, tiled=True)]
    convert_element_type x5 -> x0, other arithmetic: 24.2 us -> none  [the longest x4 23.8 us: sequence_step(): score_grad = (probs * (grad_probs - dot)).astype(BF)]
    reduce_scatter x2, waiting for transfers between devices: 41.6 us -> 22.4 us  [reduce(): mine = lax.psum_scatter(value, 'fsdp', scatter_dimension=0, tiled=False)]
    psum x1, waiting for transfers between devices: 85.1 us -> 66.5 us  [reduce(): return lax.psum(mine, 'sp').astype(F32)]
    unnamed x271 -> x145, local copies, waits for them, and re-layouts: 42.3 us -> 31 us
  transfers between devices with their start and end apart: 8 -> 8, of which waited for: 3 -> 5; matrix products, arithmetic and copies ran while one was open for 31% -> 27% of each run, Pallas kernels for 0% -> 5%
where the time goes in v2:
time: 560 us; the launch traced here: 549 us
  waiting for transfers between devices  158 us (28%)
  matrix products  121 us (22%)
  local copies, waits for them, and re-layouts  96.1 us (17%)
  Pallas kernels  60.4 us (11%)
  blocking collectives  43.3 us (8%)
  other arithmetic  42.8 us (8%)
  between operations  14.9 us (3%)
  starting transfers between devices  12.8 us (2%)
    psum x1, waiting for transfers between devices, reduce(): return lax.psum(mine, 'sp').astype(F32)  66.5 us
    dot_general x13, matrix products, mm_tn(): lax.dot_general(a, b, (((0,), (0,)), ((), ())), preferred_element_type=F32)  45.5 us
    all_to_all x1, blocking collectives, to_sequence(): return lax.all_to_all(value, 'sp', split_axis=0, concat_axis=1, tiled=True)  43.3 us
    dot_general x11, matrix products, mm_nt(): lax.dot_general(a, b, (((1,), (1,)), ((), ())), preferred_element_type=F32)  40.7 us
    pallas_call x1, Pallas kernels, attn_bwd(): pl.pallas_call(bwd_kernel, grid=(pairs,), in_specs=[pl.BlockSpec((16, 1),...  35.4 us
    dot_general x13, matrix products, mm(): return jnp.dot(a, b, preferred_element_type=F32)  35.1 us
    all_to_all x2, waiting for transfers between devices, to_tokens(): return lax.all_to_all(value, 'sp', split_axis=1, concat_axis=0, tiled=True)  34.5 us
    all_to_all x1, waiting for transfers between devices, to_sequence(): return lax.all_to_all(value, 'sp', split_axis=0, concat_axis=1, tiled=True)  34.2 us
  transfers between devices with their start and end apart: 8, of which 5 were waited for; matrix products, arithmetic and copies ran while one was open for 27% of the time, Pallas kernels for 5%

profile of v2, /device:TPU:0, one launch (start us, length us, event | category | flops | bytes accessed | tf_op | source)
XLA Modules:
  0.0 549.5 jit_solution(2724951818376031502)
XLA Ops:
  10.4 2.3 maximum_bitcast_fusion.2
  13.9 43.3 %all_to_all.42 = bf16[4,256,768]{2,1,0:T(8,128)(2,1)S(1)} all-to-all(bf16[4,256,768]{2,1,0:T(8,128)(2,1)} %param.25), channel_id=1, replica_groups=mesh['fsdp'=8,'sp'=4] {'sp'}, dimensions={0} | all-to-all | bytes 3145728 | tf_op jit(solution)/shard_map/all_to_all | solution.py:348
  57.2 3.6 all-to-all-start
  62.7 34.2 %all-to-all-done = bf16[4,256,768]{2,1,0:T(8,128)(2,1)S(1)} async-done(((bf16[4,256,768]{2,1,0:T(8,128)(2,1)}), bf16[4,256,768]{2,1,0:T(8,128)(2,1)S(1)}, u32[]{:S(2)}, u32[]{:S(2)}) %all-to-all-start) | async-done | bytes 1572896 | tf_op jit(solution)/shard_map/all_to_all | solution.py:348
  96.9 1.7 copy.160
  98.5 2.2 copy.161
  104.4 5.7 %fusion.61 = (bf16[8,96,768]{2,1,0:T(8,128)(2,1)}, bf16[8,96,768]{2,1,0:T(8,128)(2,1)}, bf16[8,96,768]{2,1,0:T(8,128)(2,1)}, bf16[8,96,768]{2,1,0:T(8,128)(2,1)}...) fusion(bf16[8,674,768]{2,1,0:T(8,128)(2,1)} %all-gather.8.cloned.1.call-done), kind=kLoop, calls=%fused_computation.161 | loop fusion | bytes 16515072 | tf_op jit(solution)/shard_map/slice | solution.py:372
  115.7 1.6 select_reduce_fusion
  117.3 2.8 fusion.9.k_ref
  120.1 3.4 fusion.10.q_ref
  123.6 1.4 fusion.11.v_ref
  125.0 25.0 %attend.1 = (bf16[1024,768]{1,0:T(8,128)(2,1)S(1)}, f32[6,8,1024]{2,1,0:T(8,128)S(1)}) custom-call(s32[16,1]{1,0:T(8,128)S(1)} %scatter.4.pos_ref, bf16[1024,768]{1,0:T(8,128)(2,1)S(1)} %fusion.10.q_ref, bf16[1024,768]{1,0:T(8,128)(2,1)S(1)} %fusion.9.k_ref, bf16[1024,768]{1,0:T(8,128)(2,1)S(1)} %fusion.11.v_ref), custom_call_target="tpu_custom_call" | custom-call | flops 20000000000 | bytes 8388608 | tf_op jit(solution)/shard_map/attend/pallas_call | solution.py:122
  151.8 1.7 fusion.66
  153.5 1.6 copy-done.16
  155.6 5.2 slice.206
  160.8 1.6 copy-done.24
  162.4 1.9 fusion.60
  164.3 1.3 copy-done.17
  165.6 13.8 %multiply_convert_fusion = (bf16[1024,3072]{1,0:T(8,128)(2,1)}, f32[1024,3072]{1,0:T(8,128)}) fusion(f32[3072]{0:T(1024)S(1)} %reshape.492, bf16[768,768]{1,0:T(8,128)(2,1)} %bitcast.234, bf16[768,768]{1,0:T(8,128)(2,1)} %bitcast.236, bf16[768,768]{1,0:T(8,128)(2,1)} %bitcast.238, bf16[768,768]{1,0:T(8,128)(2,1)S(1)} %bitcast.232, ...), kind=kOutput, calls=%fused_computation.7 | convolution fusion | flops 4873519104 | bytes 26765312 | tf_op jit(solution)/shard_map/dot_general | solution.py:35
  179.4 7.7 %fusion.67 = (f32[1024]{0:T(1024)S(1)}, f32[1024,768]{0,1:T(8,128)S(1)}) fusion(f32[768]{0:T(1024)S(1)} %add.193, bf16[1024,3072]{1,0:T(8,128)(2,1)} %get-tuple-element.103, bf16[3072,768]{1,0:T(8,128)(2,1)S(1)} %bitcast.216, f32[768]{0:T(1024)S(1)} %add.186, f32[768]{0:T(1024)S(1)} %mul.204, f32[1024]{0:T(1024)S(1)} %add_rsqrt_fusion.1, ...), kind=kOutput, calls=%fused_computation.167 | convolution fusion | flops 4837342208 | bytes 17323008 | tf_op jit(solution)/shard_map/dot_general | solution.py:35
  187.5 1.5 copy-done.11
  189.0 2.8 multiply_reduce_fusion
  192.9 14.8 %fusion.68 = (bf16[3072]{0:T(1024)(128)(2,1)}, bf16[1024,3072]{1,0:T(8,128)(2,1)}) fusion(f32[1024,3072]{1,0:T(8,128)} %get-tuple-element.104, f32[3072]{0:T(1024)S(1)} %reshape.492, bf16[3072,768]{1,0:T(8,128)(2,1)S(1)} %bitcast.217, f32[1024,768]{0,1:T(8,128)S(1)} %get-tuple-element.74), kind=kOutput, calls=%fused_computation.168 | convolution fusion | flops 4870370304 | bytes 26757120 | tf_op jit(solution)/shard_map/dot_general | solution.py:39
  207.7 9.4 %multiply_reduce_fusion.1 = (bf16[768]{0:T(1024)(128)(2,1)}, f32[1024]{0:T(1024)S(1)}, f32[1024]{0:T(1024)S(1)}, bf16[768]{0:T(1024)(128)(2,1)S(1)}, f32[1024,768]{0,1:T(8,128)S(1)}) fusion(f32[1024,768]{0,1:T(8,128)S(1)} %copy-done.17, f32[1024]{0:T(1024)S(1)} %add_rsqrt_fusion.1, f32[1024]{0:T(1024)S(1)} %broadcast_multiply_fusion.4, f32[768]{0:T(1024)S(1)} %mul.204, ...), kind=kOutput, calls=%fused_computation.17 | convolution fusion | flops 4858572800 | bytes 20469760 | tf_op jit(solution)/shard_map/dot_general | solution.py:39
  218.4 1.5 convolution_convert_fusion.3.g_ref
  219.9 2.5 convolution_convert_fusion.8
  225.4 1.5 convolution_convert_fusion.11
  227.0 35.4 %attend_back.1 = (bf16[1024,768]{1,0:T(8,128)(2,1)S(1)}, bf16[1024,768]{1,0:T(8,128)(2,1)S(1)}, bf16[1024,768]{1,0:T(8,128)(2,1)S(1)}) custom-call(s32[16,1]{1,0:T(8,128)S(1)} %scatter.4.pos_ref, bf16[1024,768]{1,0:T(8,128)(2,1)S(1)} %copy-done.8, bf16[1024,768]{1,0:T(8,128)(2,1)S(1)} %copy-done.6, bf16[1024,768]{1,0:T(8,128)(2,1)S(1)} %copy-done.10, ...), custom_call_target="tpu_custom_call" | custom-call | flops 40000000000 | bytes 12582912 | tf_op jit(solution)/shard_map/attend_back/pallas_call | solution.py:187
  262.8 2.5 convolution_convert_fusion.7
  265.7 4.0 convolution_convert_fusion.5
  272.6 1.5 fusion.12
  274.1 1.4 fusion.13
  277.8 1.5 convolution_convert_fusion.6
  281.4 3.6 pad_maximum_fusion.1
  285.1 9.8 %convolution_convert_fusion.1 = bf16[768,3072]{1,0:T(8,128)(2,1)} fusion(bf16[1024,3072]{1,0:T(8,128)(2,1)} %get-tuple-element.111, f32[1024,768]{0,1:T(8,128)} %copy-done.16, f32[768]{0:T(1024)S(1)} %add.186, f32[768]{0:T(1024)S(1)} %mul.204, f32[1024]{0:T(1024)S(1)} %add_rsqrt_fusion.1, f32[1024]{0:T(1024)S(1)} %broadcast_multiply_fusion.4), kind=kOutput, calls=%fused_computation.12 | convolution fusion | flops 4838129664 | bytes 14170112 | tf_op jit(solution)/shard_map/dot_general | solution.py:43
  294.9 10.1 %convert_element_type.261 = bf16[768,4,768]{2,1,0:T(4,128)(2,1)} reshape(bf16[768,3072]{1,0:T(8,128)(2,1)} %convolution_convert_fusion.1) | data formatting | bytes 9437184 | tf_op jit(solution)/shard_map/convert_element_type | solution.py:415
  304.9 3.4 copy.147
  308.3 9.2 %convolution_convert_fusion = bf16[3072,768]{1,0:T(8,128)(2,1)S(1)} fusion(bf16[1024,3072]{1,0:T(8,128)(2,1)} %get-tuple-element.103, f32[1024,768]{0,1:T(8,128)S(1)} %copy-done.32), kind=kOutput, calls=%fused_computation.11 | convolution fusion | flops 4834983936 | bytes 14155776 | tf_op jit(solution)/shard_map/dot_general | solution.py:43
  317.6 3.9 pad_maximum_fusion
  322.5 2.3 fusion.43
  324.8 2.3 fusion.56
  327.1 3.1 fusion.69
  330.2 3.2 fusion.70
  333.4 3.1 fusion.15
  336.5 9.9 %fusion.8 = bf16[1,1024,768]{1,2,0:T(8,128)(2,1)} fusion(f32[1024,768]{0,1:T(8,128)} %fusion.43, f32[1024,768]{0,1:T(8,128)} %fusion.56, f32[1024,768]{0,1:T(8,128)} %fusion.70, f32[1024,768]{0,1:T(8,128)} %fusion.69, f32[1024,768]{0,1:T(8,128)} %copy-done.18, f32[1024,768]{0,1:T(8,128)} %fusion.15, bf16[768,768]{1,0:T(8,128)(2,1)S(1)} %bitcast.212, ...), kind=kOutput, calls=%fused_computation.49 | convolution fusion | flops 16531456 | bytes 21633040 | tf_op jit(solution)/shard_map/dot_general | solution.py:43
  346.3 7.6 %copy.139 = bf16[1,1024,768]{2,0,1:T(2,128)(2,1)S(1)} copy(bf16[1,1024,768]{1,2,0:T(8,128)(2,1)} %fusion.8) | data formatting | bytes 3145728 | tf_op jit(solution)/shard_map/stack | solution.py:411
  354.5 11.4 %reduce.67 = bf16[1024,768]{1,0:T(8,128)(2,1)} reduce(bf16[1024,1,768]{2,1,0:T(2,128)(2,1)S(1)} %bitcast.203, bf16[]{:T(256)} %broadcast.253), dimensions={1}, to_apply=%bitcast.130.reduce_sub_computation | reduce | bytes 3145730
  365.9 3.8 reshape.563
  369.7 4.7 all-to-all-start.3
  374.4 7.3 %copy.130 = bf16[1,1024,768]{2,0,1:T(2,128)(2,1)S(1)} copy(bf16[1,1024,768]{1,2,0:T(8,128)(2,1)} %get-tuple-element.88) | data formatting | bytes 3145728 | tf_op jit(solution)/shard_map/stack | solution.py:410
  381.7 11.4 %reduce.66 = bf16[1024,768]{1,0:T(8,128)(2,1)} reduce(bf16[1024,1,768]{2,1,0:T(2,128)(2,1)S(1)} %bitcast.204, bf16[]{:T(256)} %broadcast.253), dimensions={1}, to_apply=%bitcast.128.reduce_sub_computation | reduce | bytes 3145730
  393.0 3.7 reshape.561
  396.8 13.0 %all-to-all-done.3 = bf16[4,2,98304]{2,1,0:T(2,128)(2,1)} async-done(((bf16[4,2,98304]{2,1,0:T(2,128)(2,1)}), bf16[4,2,98304]{2,1,0:T(2,128)(2,1)}, u32[]{:S(2)}, u32[]{:S(2)}) %all-to-all-start.3) | async-done | bytes 1572896 | tf_op jit(solution)/shard_map/all_to_all | solution.py:351
  409.8 4.4 all-to-all-start.1
  414.3 22.4 %reduce-scatter.5.cloned.1.call-done = bf16[1,768,768]{2,1,0:T(8,128)(2,1)} async-done(((bf16[8,768,768]{2,1,0:T(8,128)(2,1)}), bf16[1,768,768]{2,1,0:T(8,128)(2,1)}) %reduce-scatter.5.cloned.1.call-update) | async-done | bytes 1179664 | tf_op jit(solution)/shard_map/reduce_scatter | solution.py:444
  436.7 3.1 reshape.564
  439.8 1.4 copy.163
  441.2 21.4 %all-to-all-done.1 = bf16[4,2,98304]{2,1,0:T(2,128)(2,1)} async-done(((bf16[4,2,98304]{2,1,0:T(2,128)(2,1)}), bf16[4,2,98304]{2,1,0:T(2,128)(2,1)}, u32[]{:S(2)}, u32[]{:S(2)}) %all-to-all-start.1) | async-done | bytes 1572896 | tf_op jit(solution)/shard_map/all_to_all | solution.py:351
  462.6 3.1 reshape.562
  465.7 1.4 copy.162
  467.1 66.5 %all-reduce.6.cloned.1.call-done = (bf16[674,768]{1,0:T(8,128)(2,1)}, bf16[768,768]{1,0:T(8,128)(2,1)}) async-done(((bf16[674,768]{1,0:T(8,128)(2,1)}, bf16[768,768]{1,0:T(8,128)(2,1)}), (bf16[674,768]{1,0:T(8,128)(2,1)}, bf16[768,768]{1,0:T(8,128)(2,1)})) %all-reduce.6.cloned.1.call-update) | async-done | bytes 2214928 | tf_op jit(solution)/shard_map/psum | solution.py:445
  535.7 1.6 slice.212
  537.3 2.5 fusion.63
  540.4 1.2 fusion.62
  (254 shorter events, 36.8 us)
Async XLA Ops:
  7.2 5.5 %copy-start.51 = (bf16[96,3072]{1,0:T(8,128)(2,1)S(1)}, bf16[96,3072]{1,0:T(8,128)(2,1)}, u32[]{:S(2)}) copy-start(bf16[96,3072]{1,0:T(8,128)(2,1)} %param.22) | copy-start | bytes 1769476
  7.2 5.6 %copy-start.52 = (bf16[384,768]{1,0:T(8,128)(2,1)S(1)}, bf16[384,768]{1,0:T(8,128)(2,1)}, u32[]{:S(2)}) copy-start(bf16[384,768]{1,0:T(8,128)(2,1)} %param.24) | copy-start | bytes 1769476
  7.2 93.8 %all-gather.8.cloned.1.call-start = ((), (), s32[]{:S(2)}) async-start(), calls=%async_computation.9 | async-start | bytes 9400320 | tf_op jit(solution)/shard_map/all_gather | solution.py:368
  12.7 142.9 %all-gather.6.cloned.1.call-start = ((), (), s32[]{:S(2)}) async-start(), calls=%async_computation.8 | async-start | bytes 10616832 | tf_op jit(solution)/shard_map/all_gather | solution.py:369
  57.2 39.7 %all-to-all-start = ((bf16[4,256,768]{2,1,0:T(8,128)(2,1)}), bf16[4,256,768]{2,1,0:T(8,128)(2,1)S(1)}, u32[]{:S(2)}, u32[]{:S(2)}) async-start(bf16[4,256,768]{2,1,0:T(8,128)(2,1)} %param.14), calls=%async_computation | async-start | bytes 3145728 | tf_op jit(solution)/shard_map/all_to_all | solution.py:348
  60.8 353.5 %reduce-scatter.3.cloned.1.call-start = ((), (), s32[]{:S(2)}) async-start(), calls=%async_computation.6 | async-start | bytes 9400320 | tf_op jit(solution)/shard_map/reduce_scatter | solution.py:444
  96.9 20.4 %copy-start.12 = (bf16[4,256,768]{2,1,0:T(8,128)(2,1)}, bf16[4,256,768]{2,1,0:T(8,128)(2,1)S(1)}, u32[]{:S(2)}) copy-start(bf16[4,256,768]{2,1,0:T(8,128)(2,1)S(1)} %all-to-all-done) | copy-start | bytes 4718596
  110.1 4.8 copy-start.19
  112.6 4.7 copy-start.47
  113.3 4.0 copy-start.25
  117.3 2.8 copy-start.34
  120.1 4.9 copy-start.5
  120.1 3.4 copy-start.13
  120.1 3.4 copy-start.36
  123.6 1.4 copy-start.7
  125.0 25.1 %copy-start.9 = (bf16[1024,768]{1,0:T(8,128)(2,1)}, bf16[1024,768]{1,0:T(8,128)(2,1)S(1)}, u32[]{:S(2)}) copy-start(bf16[1024,768]{1,0:T(8,128)(2,1)S(1)} %fusion.11.v_ref) | copy-start | bytes 4718596
  150.1 1.4 copy-start.33
  150.1 1.7 copy-start.40
  151.0 68.9 %copy-start = (bf16[1024,768]{1,0:T(8,128)(2,1)}, bf16[1024,768]{1,0:T(8,128)(2,1)S(1)}, u32[]{:S(2)}) copy-start(bf16[1024,768]{1,0:T(8,128)(2,1)S(1)} %broadcast_select_fusion.ctx_ref) | copy-start | bytes 4718596
  153.5 1.6 copy-start.16
  155.6 6.8 %copy-start.24 = (bf16[6144,768]{1,0:T(8,128)(2,1)S(1)}, bf16[6144,768]{1,0:T(8,128)(2,1)}, u32[]{:S(2)}) copy-start(bf16[6144,768]{1,0:T(8,128)(2,1)} %all-gather.6.cloned.1.call-done) | copy-start | bytes 28311556
  162.4 3.2 copy-start.17
  165.6 13.8 %copy-start.29 = (bf16[8,384,768]{2,1,0:T(8,128)(2,1)S(1)}, bf16[8,384,768]{2,1,0:T(8,128)(2,1)}, u32[]{:S(2)}) copy-start(bf16[8,384,768]{2,1,0:T(8,128)(2,1)} %slice.206) | copy-start | bytes 14155780
  187.1 1.9 copy-start.11
  192.9 14.8 %copy-start.31 = (f32[1024,768]{0,1:T(8,128)}, f32[1024,768]{0,1:T(8,128)S(1)}, u32[]{:S(2)}) copy-start(f32[1024,768]{0,1:T(8,128)S(1)} %get-tuple-element.74) | copy-start | bytes 9437188
  192.9 14.8 %copy-start.42 = (bf16[8,96,768]{2,1,0:T(8,128)(2,1)S(1)}, bf16[8,96,768]{2,1,0:T(8,128)(2,1)}, u32[]{:S(2)}) copy-start(bf16[8,96,768]{2,1,0:T(8,128)(2,1)} %get-tuple-element.78) | copy-start | bytes 3538948
  192.9 14.8 %copy-start.43 = (bf16[8,96,768]{2,1,0:T(8,128)(2,1)S(1)}, bf16[8,96,768]{2,1,0:T(8,128)(2,1)}, u32[]{:S(2)}) copy-start(bf16[8,96,768]{2,1,0:T(8,128)(2,1)} %get-tuple-element.79) | copy-start | bytes 3538948
  192.9 14.8 %copy-start.44 = (bf16[8,96,768]{2,1,0:T(8,128)(2,1)S(1)}, bf16[8,96,768]{2,1,0:T(8,128)(2,1)}, u32[]{:S(2)}) copy-start(bf16[8,96,768]{2,1,0:T(8,128)(2,1)} %get-tuple-element.80) | copy-start | bytes 3538948
  218.3 1.6 copy-start.18
  219.9 2.9 copy-start.21
  219.9 3.4 copy-start.61
  222.4 1.4 copy-start.26
  222.8 2.3 copy-start.20
  223.3 3.7 copy-start.53
  223.8 3.2 copy-start.1
  223.8 3.2 copy-start.6
  223.8 3.2 copy-start.8
  223.8 3.2 copy-start.10
  224.6 2.4 copy-start.57
  225.0 2.0 copy-start.55
  262.4 2.9 copy-start.2
  265.6 4.8 copy-start.62
  265.6 5.2 copy-start.59
  265.7 5.4 copy-start.60
  265.7 6.1 %copy-start.56 = (bf16[64,768]{1,0:T(8,128)(2,1)S(1)}, bf16[64,768]{1,0:T(8,128)(2,1)}, u32[]{:S(2)}) copy-start(bf16[64,768]{1,0:T(8,128)(2,1)} %copy-done.55) | copy-start | bytes 294916
  265.7 6.9 %copy-start.50 = (bf16[4,16,768]{2,1,0:T(8,128)(2,1)S(1)}, bf16[4,16,768]{2,1,0:T(8,128)(2,1)}, u32[]{:S(2)}) copy-start(bf16[4,16,768]{2,1,0:T(8,128)(2,1)} %copy-done.49) | copy-start | bytes 294916
  272.6 2.9 copy-start.28
  276.0 1.9 copy-start.15
  277.8 1.5 copy-start.45
  277.8 1.6 copy-start.46
  285.0 151.7 %reduce-scatter.5.cloned.1.call-start = ((), (), s32[]{:S(2)}) async-start(), calls=%async_computation.7 | async-start | bytes 10616832 | tf_op jit(solution)/shard_map/reduce_scatter | solution.py:444
  304.9 3.4 copy-start.32
  322.5 2.3 copy-start.48
  322.5 2.3 copy-start.58
  322.5 2.3 copy-start.64
  322.5 4.6 copy-start.4
  322.5 4.6 copy-start.38
  327.1 3.1 copy-start.37
  330.2 3.2 copy-start.35
  333.4 3.1 copy-start.23
  369.7 40.1 %all-to-all-start.3 = ((bf16[4,2,98304]{2,1,0:T(2,128)(2,1)}), bf16[4,2,98304]{2,1,0:T(2,128)(2,1)}, u32[]{:S(2)}, u32[]{:S(2)}) async-start(bf16[4,2,98304]{2,1,0:T(2,128)(2,1)} %reshape.563), calls=%async_computation.3 | async-start | bytes 3145728 | tf_op jit(solution)/shard_map/all_to_all | solution.py:351
  409.8 52.8 %all-to-all-start.1 = ((bf16[4,2,98304]{2,1,0:T(2,128)(2,1)}), bf16[4,2,98304]{2,1,0:T(2,128)(2,1)}, u32[]{:S(2)}, u32[]{:S(2)}) async-start(bf16[4,2,98304]{2,1,0:T(2,128)(2,1)} %reshape.561), calls=%async_computation.1 | async-start | bytes 3145728 | tf_op jit(solution)/shard_map/all_to_all | solution.py:351
  414.2 119.4 %all-reduce.6.cloned.1.call-start = ((), (), s32[]{:S(2)}) async-start(), calls=%async_computation.10 | async-start | bytes 4448256 | tf_op jit(solution)/shard_map/psum | solution.py:445
  533.6 6.8 %copy-start.30 = (bf16[768,768]{1,0:T(8,128)(2,1)S(1)}, bf16[768,768]{1,0:T(8,128)(2,1)}, u32[]{:S(2)}) copy-start(bf16[768,768]{1,0:T(8,128)(2,1)} %get-tuple-element.72) | copy-start | bytes 3538948
  (9 other events, 9.5 us)
Sparse Core Ops, SparseCore 0:
  12.8 56.9 all-gather.7
  72.2 58.8 all-gather.5
  285.1 71.2 reduce-scatter.2
  360.2 76.4 reduce-scatter.4
  439.1 94.4 all-reduce.5

commit v3 on v2

--- a/solution.py
+++ b/solution.py
@@ -321,6 +321,104 @@
     )
 
 
+def log2_of(count):
+    return count.bit_length() - 1
+
+
+def flip(value, axis, bit):
+    count = lax.axis_size(axis)
+    return lax.ppermute(value, axis, [(index, index ^ bit) for index in range(count)])
+
+
+def after(value, *others):
+    return lax.optimization_barrier((value,) + others)[0]
+
+
+def spread_slots(unit, order):
+    slots = {0: unit}
+    levels = []
+    for bit in order:
+        for slot in list(slots):
+            slots[slot | bit] = flip(slots[slot], "fsdp", bit)
+        levels.append(slots[bit])
+    return ([slots[slot] for slot in range(len(slots))], slots)
+
+
+def assemble(pieces, parts, axis="fsdp"):
+    count = len(pieces)
+    width = pieces[0].shape[-1]
+
+    def body(*refs):
+        ins = refs[:count]
+        outs = refs[count : count + len(parts)]
+        sems = refs[-1]
+        me = lax.axis_index(axis)
+        copies = []
+        for slot in range(count):
+            place = me ^ slot
+            for part, (first, planes, rows) in enumerate(parts):
+                for plane in range(planes):
+                    copies.append(
+                        pltpu.make_async_copy(
+                            ins[slot].at[pl.ds(first + plane * rows, rows)],
+                            outs[part].at[plane, pl.ds(pl.multiple_of(place * rows, rows), rows)],
+                            sems.at[len(copies)],
+                        )
+                    )
+        for copy in copies:
+            copy.start()
+        for copy in copies:
+            copy.wait()
+
+    total = count * sum(planes for _, planes, _ in parts)
+    size = sum(count * planes * rows for _, planes, rows in parts) * width * 2
+    return pl.pallas_call(
+        body,
+        in_specs=[pl.BlockSpec(memory_space=pl.ANY)] * count,
+        out_specs=[pl.BlockSpec(memory_space=pl.ANY)] * len(parts),
+        out_shape=[
+            jax.ShapeDtypeStruct((planes, count * rows, width), pieces[0].dtype)
+            for _, planes, rows in parts
+        ],
+        scratch_shapes=[pltpu.SemaphoreType.DMA((total,))],
+        cost_estimate=pl.CostEstimate(flops=0, bytes_accessed=2 * size, transcendentals=0),
+        name="assemble",
+    )(*pieces)
+
+
+def reduce_to_owner(grads, order):
+    count = lax.axis_size("fsdp")
+    bits = log2_of(count)
+    me = lax.axis_index("fsdp")
+    grads = grads.reshape((2,) * bits + grads.shape[1:])
+    alive = list(range(bits - 1, -1, -1))
+    for bit in order:
+        place = alive.index(log2_of(bit))
+        alive.pop(place)
+        mine = (me >> log2_of(bit)) & 1
+        send = lax.dynamic_index_in_dim(grads, 1 - mine, place, keepdims=False).astype(BF)
+        keep = lax.dynamic_index_in_dim(grads, mine, place, keepdims=False).astype(F32)
+        grads = keep + flip(send, "fsdp", bit).astype(F32)
+    return grads
+
+
+def sum_over_sp(value):
+    me = lax.axis_index("sp")
+    value = value.reshape((2, 2) + (value.shape[0] // 4,) + value.shape[1:])
+    low, high = me & 1, me >> 1
+    send = lax.dynamic_index_in_dim(value, 1 - low, 0, keepdims=False).astype(BF)
+    keep = lax.dynamic_index_in_dim(value, low, 0, keepdims=False)
+    value = keep + flip(send, "sp", 1).astype(F32)
+    send = lax.dynamic_index_in_dim(value, 1 - high, 0, keepdims=False).astype(BF)
+    keep = lax.dynamic_index_in_dim(value, high, 0, keepdims=False)
+    mine = (keep + flip(send, "sp", 2).astype(F32)).astype(BF)
+    other = flip(mine, "sp", 2)
+    pair = jnp.stack([jnp.where(high == 0, mine, other), jnp.where(high == 0, other, mine)])
+    there = flip(pair, "sp", 1)
+    both = jnp.stack([jnp.where(low == 0, pair, there), jnp.where(low == 0, there, pair)])
+    return both.reshape((-1,) + both.shape[3:]).astype(F32)
+
+
 def per_device(
     inputs,
     global_pos,
@@ -342,59 +440,68 @@
     shard = w_out.shape[0]
     width = w_out.shape[1]
     ff_shard = w_back.shape[0]
-    pieces = w_in.shape[1] // width
+    ff_width = w_in.shape[1]
+    tree = fsdp_count == 8 and sp_count == 4 and shard % 32 == 0
 
     def to_sequence(value):
+        if own_seqs == 1:
+            moved = lax.all_to_all(value, "sp", split_axis=0, concat_axis=0)
+            return moved.reshape(1, -1, width)
         return lax.all_to_all(value, "sp", split_axis=0, concat_axis=1, tiled=True)
 
-    def to_tokens(value):
-        return lax.all_to_all(value, "sp", split_axis=1, concat_axis=0, tiled=True)
-
-    x_all = to_sequence(inputs)
-    up_all = to_sequence(cotangent)
+    def to_tokens(values):
+        if own_seqs == 1:
+            return lax.all_to_all(
+                values[0].reshape(sp_count, -1, width), "sp", split_axis=0, concat_axis=0
+            )
+        return lax.all_to_all(jnp.stack(values), "sp", split_axis=1, concat_axis=0, tiled=True)
+
     own_pos = lax.dynamic_slice_in_dim(global_pos, sp_index * own_seqs, own_seqs, 0)
-
     small = jnp.concatenate(
         [b_proj.reshape(-1), gains.reshape(-1), shifts.reshape(-1), c_in.reshape(-1)]
     )
-    small_rows = -(-small.shape[0] // width)
+    small_rows = 16 * -(-small.shape[0] // (16 * width))
     small = jnp.pad(small, (0, small_rows * width - small.shape[0])).reshape(small_rows, width)
-    pack_one = jnp.concatenate(
-        [w_local.reshape(-1, width), w_global.reshape(-1, width), w_out, small], axis=0
-    )
-    pack_two = jnp.concatenate(
-        [w_in.reshape(shard, pieces, width).transpose(1, 0, 2).reshape(-1, width), w_back], axis=0
-    )
-    all_one = lax.all_gather(pack_one, "fsdp")
-    all_two = lax.all_gather(pack_two, "fsdp")
-
-    def part(packed, start):
-        return packed[:, start : start + shard].reshape(fsdp_count * shard, width)
-
-    full_local = [part(all_one, index * shard) for index in range(3)]
-    full_global = [part(all_one, (3 + index) * shard) for index in range(3)]
-    full_out = part(all_one, 6 * shard)
-    small_all = all_one[:, 7 * shard :].reshape(fsdp_count, -1)
+    x_all = to_sequence(inputs)
+    if tree:
+        first = w_local.reshape(-1, width)
+        second = jnp.concatenate([w_global.reshape(-1, width), w_out, small], axis=0)
+        slots_one, by_bit = spread_slots(first, (2, 4, 1))
+        slots_two, _ = spread_slots(second, (4, 2, 1))
+        mark = by_bit[4]
+        third, fourth, mark = lax.optimization_barrier((w_in, w_back, mark))
+        slots_three, _ = spread_slots(third, (2, 4, 1))
+        slots_four, _ = spread_slots(fourth, (4, 2, 1))
+        (full_local,) = assemble(slots_one, [(0, 3, shard)])
+        full_global, full_out, small_all = assemble(
+            slots_two, [(0, 3, shard), (3 * shard, 1, shard), (4 * shard, 1, small_rows)]
+        )
+        (full_in,) = assemble(slots_three, [(0, 1, shard)])
+        (full_back,) = assemble(slots_four, [(0, 1, ff_shard)])
+        full_out, full_in, full_back = full_out[0], full_in[0], full_back[0]
+    else:
+        full_local = lax.all_gather(w_local, "fsdp", axis=1, tiled=True)
+        full_global = lax.all_gather(w_global, "fsdp", axis=1, tiled=True)
+        full_out = lax.all_gather(w_out, "fsdp", axis=0, tiled=True)
+        full_in = lax.all_gather(w_in, "fsdp", axis=0, tiled=True)
+        full_back = lax.all_gather(w_back, "fsdp", axis=0, tiled=True)
+        small_all = lax.all_gather(small, "fsdp")
+    up_all = to_sequence(after(cotangent, x_all))
+    small_all = small_all.reshape(fsdp_count, -1)
 
     def vectors(start, count):
         taken = small_all[:, start : start + count * shard].reshape(fsdp_count, count, shard)
         return taken.transpose(1, 0, 2).reshape(count, fsdp_count * shard)
 
-    full_bias = vectors(0, 6)
-    full_gain = vectors(6 * shard, 2)
-    full_shift = vectors(8 * shard, 2)
-    full_c = small_all[:, 10 * shard : 10 * shard + ff_shard].reshape(-1)
-    full_in = jnp.concatenate([part(all_two, index * shard) for index in range(pieces)], axis=1)
-    full_back = all_two[:, pieces * shard :].reshape(-1, width)
     weights = (
         full_local,
         full_global,
         full_out,
-        full_bias,
-        full_gain,
-        full_shift,
+        vectors(0, 6),
+        vectors(6 * shard, 2),
+        vectors(8 * shard, 2),
         full_in,
-        full_c,
+        small_all[:, 10 * shard : 10 * shard + ff_shard].reshape(-1),
         full_back,
     )
     results = []
@@ -407,61 +514,60 @@
         results.append(result)
         token_grads.append(token_grad)
         totals = grads if totals is None else tuple(a + b for a, b in zip(totals, grads))
-    out = to_tokens(jnp.stack(results))
-    grad_inputs = to_tokens(jnp.stack(token_grads))
+    out = to_tokens(results)
+    grad_inputs = to_tokens(token_grads)
     g_local, g_global, g_out, g_bias, g_gain, g_shift, g_in, g_c, g_back = totals
-
-    def rows(value):
-        return value.astype(BF).reshape(-1, fsdp_count, shard, width).transpose(1, 0, 2, 3)
 
     def cols(value):
         return value.reshape(-1, fsdp_count, shard).transpose(1, 0, 2).reshape(fsdp_count, -1)
 
     g_small = jnp.concatenate(
         [cols(g_bias), cols(g_gain), cols(g_shift), g_c.reshape(fsdp_count, ff_shard)], axis=1
-    ).astype(BF)
+    )
     g_small = jnp.pad(g_small, ((0, 0), (0, small_rows * width - g_small.shape[1])))
-    first = jnp.concatenate(
-        [
-            rows(g_in.reshape(width, pieces, width).transpose(1, 0, 2)).reshape(
-                fsdp_count, -1, width
+
+    def owned(value):
+        planes, rows, columns = value.shape
+        split = value.reshape(planes, fsdp_count, rows // fsdp_count, columns)
+        return split.transpose(1, 0, 2, 3).reshape(fsdp_count, -1, columns)
+
+    units = [
+        (g_back.reshape(fsdp_count, ff_shard, width), (1, 2, 4)),
+        (g_in.reshape(fsdp_count, shard, ff_width), (1, 4, 2)),
+        (
+            jnp.concatenate(
+                [
+                    owned(g_global),
+                    g_out.reshape(fsdp_count, shard, width),
+                    g_small.reshape(fsdp_count, small_rows, width),
+                ],
+                axis=1,
             ),
-            g_back.astype(BF).reshape(fsdp_count, ff_shard, width),
-        ],
-        axis=1,
-    )
-    second = jnp.concatenate(
-        [
-            rows(g_local).reshape(fsdp_count, -1, width),
-            rows(g_global).reshape(fsdp_count, -1, width),
-            rows(g_out).reshape(fsdp_count, -1, width),
-            g_small.reshape(fsdp_count, small_rows, width),
-        ],
-        axis=1,
-    )
-
-    def reduce(value):
-        mine = lax.psum_scatter(value, "fsdp", scatter_dimension=0, tiled=False)
-        return lax.psum(mine, "sp").astype(F32)
-
-    first = reduce(first)
-    second = reduce(second)
-    small_sum = second[7 * shard :].reshape(-1)
+            (1, 2, 4),
+        ),
+        (owned(g_local), (1, 4, 2)),
+    ]
+    summed = []
+    for unit, order in units:
+        if tree:
+            summed.append(sum_over_sp(reduce_to_owner(unit, order)))
+        else:
+            mine = lax.psum_scatter(unit.astype(BF), "fsdp", scatter_dimension=0, tiled=False)
+            summed.append(lax.psum(mine, "sp").astype(F32))
+    s_back, s_in, s_mixed, s_local = summed
+    small_sum = s_mixed[4 * shard :].reshape(-1)
     return (
         out,
         grad_inputs,
-        second[: 3 * shard].reshape(3, shard, width),
-        second[3 * shard : 6 * shard].reshape(3, shard, width),
-        second[6 * shard : 7 * shard],
+        s_local.reshape(3, shard, width),
+        s_mixed[: 3 * shard].reshape(3, shard, width),
+        s_mixed[3 * shard : 4 * shard],
         small_sum[: 6 * shard].reshape(6, shard),
         small_sum[6 * shard : 8 * shard].reshape(2, shard),
         small_sum[8 * shard : 10 * shard].reshape(2, shard),
-        first[: pieces * shard]
-        .reshape(pieces, shard, width)
-        .transpose(1, 0, 2)
-        .reshape(shard, pieces * width),
+        s_in,
         small_sum[10 * shard : 10 * shard + ff_shard],
-        first[pieces * shard :],
+        s_back,
     )
 
 

time: 560 us -> 1050 us (1.88)
  Pallas kernels: 60.4 us -> 607 us
  starting transfers between devices: 12.8 us -> 68 us
  blocking collectives: 43.3 us -> 0 us
  local copies, waits for them, and re-layouts: 96.1 us -> 65.7 us
  between operations: 14.9 us -> 2.49 us
  waiting for transfers between devices: 158 us -> 146 us
    pallas_call x0 -> x4, Pallas kernels: none -> 547 us  [assemble(): pl.pallas_call(body, in_specs=[pl.BlockSpec(memory_space=pl.ANY)] * count...]
    ppermute x0 -> x56, waiting for transfers between devices: none -> 134 us  [flip(): lax.ppermute(value, axis, [(index, index ^ bit) for index in range(count)])]
    psum x1 -> x0, waiting for transfers between devices: 66.5 us -> none  [reduce(): return lax.psum(mine, 'sp').astype(F32)]
    all_to_all x3 -> x4, waiting for transfers between devices: 68.7 us -> 11.9 us  [the longest x2 11.9 us: to_tokens(): lax.all_to_all(values[0].reshape(sp_count, -1, width), 'sp', split_axis=0...]
    ppermute x0 -> x56, starting transfers between devices: none -> 47.7 us  [flip(): lax.ppermute(value, axis, [(index, index ^ bit) for index in range(count)])]
    all_to_all x1 -> x0, blocking collectives: 43.3 us -> none  [to_sequence(): return lax.all_to_all(value, 'sp', split_axis=0, concat_axis=1, tiled=True)]
    unnamed x4 -> x9, other arithmetic: 25 us -> 0.01 us
    reduce_scatter x2 -> x0, waiting for transfers between devices: 22.4 us -> none  [reduce(): mine = lax.psum_scatter(value, 'fsdp', scatter_dimension=0, tiled=False)]
  transfers between devices with their start and end apart: 8 -> 60, of which waited for: 5 -> 23; matrix products, arithmetic and copies ran while one was open for 27% -> 12% of each run, Pallas kernels for 5% -> 55%
where the time goes in v3:
time: 1050 us
  Pallas kernels  607 us (58%)
  waiting for transfers between devices  146 us (14%)
  matrix products  116 us (11%)
  starting transfers between devices  68 us (6%)
  local copies, waits for them, and re-layouts  65.7 us (6%)
  other arithmetic  43.6 us (4%)
    pallas_call x4, Pallas kernels, assemble(): pl.pallas_call(body, in_specs=[pl.BlockSpec(memory_space=pl.ANY)] * count...  547 us
    ppermute x56, waiting for transfers between devices, flip(): lax.ppermute(value, axis, [(index, index ^ bit) for index in range(count)])  134 us
    dot_general x13, matrix products, mm_tn(): lax.dot_general(a, b, (((0,), (0,)), ((), ())), preferred_element_type=F32)  48.2 us
    ppermute x56, starting transfers between devices, flip(): lax.ppermute(value, axis, [(index, index ^ bit) for index in range(count)])  47.7 us
    dot_general x11, matrix products, mm_nt(): lax.dot_general(a, b, (((1,), (1,)), ((), ())), preferred_element_type=F32)  38.2 us
    pallas_call x1, Pallas kernels, attn_bwd(): pl.pallas_call(bwd_kernel, grid=(pairs,), in_specs=[pl.BlockSpec((16, 1),...  35.4 us
    dot_general x13, matrix products, mm(): return jnp.dot(a, b, preferred_element_type=F32)  29.1 us
    pallas_call x1, Pallas kernels, attn_fwd(): pl.pallas_call(fwd_kernel, grid=(pairs,), in_specs=[pl.BlockSpec((16, 1),...  24.8 us
  transfers between devices with their start and end apart: 60, of which 23 were waited for; matrix products, arithmetic and copies ran while one was open for 12% of the time, Pallas kernels for 55%

profile of v3, /device:TPU:0, one launch (start us, length us, event | category | flops | bytes accessed | tf_op | source)
XLA Modules:
  0.0 1048.3 jit_solution(15392222841756111928)
XLA Ops:
  0.6 3.0 collective-permute-start.10
  10.0 4.9 collective-permute-done.10.refs_4_
  17.5 9.7 collective-permute-done.3.refs_4_
  34.6 4.9 all-to-all-start
  39.5 5.7 collective-permute-done.12.refs_6_
  45.8 9.8 collective-permute-done.15.refs_2_
  57.3 12.7 %collective-permute-done.24.refs_4_ = bf16[384,768]{1,0:T(8,128)(2,1)} collective-permute-done((bf16[384,768]{1,0:T(8,128)(2,1)}, bf16[384,768]{1,0:T(8,128)(2,1)}, u32[]{:S(2)}, u32[]{:S(2)}) %collective-permute-start.24) | collective-permute-done | bytes 589856 | tf_op jit(solution)/shard_map/ppermute | solution.py:330
  72.7 108.5 %assemble.5 = bf16[3,768,768]{2,1,0:T(8,128)(2,1)} custom-call(bf16[288,768]{1,0:T(8,128)(2,1)} %bitcast.408, bf16[288,768]{1,0:T(8,128)(2,1)} %copy-done.48, bf16[288,768]{1,0:T(8,128)(2,1)} %collective-permute-done.8.refs_2_, bf16[288,768]{1,0:T(8,128)(2,1)} %copy-done.49, bf16[288,768]{1,0:T(8,128)(2,1)} %copy-done.47, bf16[288,768]{1,0:T(8,128)(2,1)} %copy-done.50, ...), custom_call_target="tpu_custom_call" | custom-call | bytes 7077888 | tf_op jit(solution)/shard_map/assemble/pallas_call | solution.py:375
  181.3 150.4 %assemble.4 = (bf16[3,768,768]{2,1,0:T(8,128)(2,1)}, bf16[1,768,768]{2,1,0:T(8,128)(2,1)}, bf16[1,128,768]{2,1,0:T(8,128)(2,1)}) custom-call(bf16[400,768]{1,0:T(8,128)(2,1)} %copy-done.37, bf16[400,768]{1,0:T(8,128)(2,1)} %copy-done.43, bf16[400,768]{1,0:T(8,128)(2,1)} %copy-done.44, bf16[400,768]{1,0:T(8,128)(2,1)} %collective-permute-done.2.refs_3_, ...), custom_call_target="tpu_custom_call" | custom-call | bytes 9830400 | tf_op jit(solution)/shard_map/assemble/pallas_call | solution.py:375
  337.8 144.1 %assemble.6 = bf16[1,768,3072]{2,1,0:T(8,128)(2,1)} custom-call(bf16[96,3072]{1,0:T(8,128)(2,1)} %refs_0_, bf16[96,3072]{1,0:T(8,128)(2,1)} %collective-permute-done.14.refs_1_, bf16[96,3072]{1,0:T(8,128)(2,1)} %collective-permute-done.15.refs_2_, bf16[96,3072]{1,0:T(8,128)(2,1)} %collective-permute-done.16.refs_3_, ...), custom_call_target="tpu_custom_call" | custom-call | bytes 9437184 | tf_op jit(solution)/shard_map/assemble/pallas_call | solution.py:375
  483.0 144.1 %assemble.7 = bf16[1,3072,768]{2,1,0:T(8,128)(2,1)} custom-call(bf16[384,768]{1,0:T(8,128)(2,1)} %refs_0_.1, bf16[384,768]{1,0:T(8,128)(2,1)} %copy-done.45, bf16[384,768]{1,0:T(8,128)(2,1)} %collective-permute-done.22.refs_2_, bf16[384,768]{1,0:T(8,128)(2,1)} %collective-permute-done.23.refs_3_, bf16[384,768]{1,0:T(8,128)(2,1)} %collective-permute-done.24.refs_4_, ...), custom_call_target="tpu_custom_call" | custom-call | bytes 9437184 | tf_op jit(solution)/shard_map/assemble/pallas_call | solution.py:375
  627.1 5.1 all-to-all-start.2
  640.0 3.4 fusion.31.q_ref
  644.9 2.2 select_reduce_fusion
  647.1 24.8 %attend.1 = (bf16[1024,768]{1,0:T(8,128)(2,1)S(1)}, f32[6,8,1024]{2,1,0:T(8,128)S(1)}) custom-call(s32[16,1]{1,0:T(8,128)S(1)} %scatter.4.pos_ref, bf16[1024,768]{1,0:T(8,128)(2,1)S(1)} %fusion.31.q_ref, bf16[1024,768]{1,0:T(8,128)(2,1)S(1)} %fusion.30.k_ref, bf16[1024,768]{1,0:T(8,128)(2,1)S(1)} %fusion.32.v_ref), custom_call_target="tpu_custom_call" | custom-call | flops 20000000000 | bytes 8388608 | tf_op jit(solution)/shard_map/attend/pallas_call | solution.py:122
  675.6 9.7 multiply_convert_fusion
  685.4 5.4 fusion.151
  693.0 4.3 fusion.19
  697.3 2.8 convert_reduce_fusion.1
  700.1 3.6 convert_reduce_fusion.2
  703.7 13.7 %convert_reduce_fusion = (f32[3072]{0:T(1024)}, bf16[1024,3072]{1,0:T(8,128)(2,1)S(1)}) fusion(f32[1024,3072]{1,0:T(8,128)} %get-tuple-element.93, f32[3072]{0:T(1024)S(1)} %reshape.427, bf16[1,3072,768]{2,1,0:T(8,128)(2,1)} %assemble.7, f32[1024,768]{1,0:T(8,128)S(1)} %get-tuple-element.62), kind=kOutput, calls=%fused_computation.7 | convolution fusion | flops 4873516032 | bytes 26763264 | tf_op jit(solution)/shard_map/dot_general | solution.py:39
  717.5 6.6 multiply_reduce_fusion
  729.2 35.4 %attend_back.1 = (bf16[1024,768]{1,0:T(8,128)(2,1)S(1)}, bf16[1024,768]{1,0:T(8,128)(2,1)S(1)}, bf16[1024,768]{1,0:T(8,128)(2,1)S(1)}) custom-call(s32[16,1]{1,0:T(8,128)S(1)} %scatter.4.pos_ref, bf16[1024,768]{1,0:T(8,128)(2,1)S(1)} %copy-done.7, bf16[1024,768]{1,0:T(8,128)(2,1)S(1)} %copy-done.5, bf16[1024,768]{1,0:T(8,128)(2,1)S(1)} %copy-done.9, ...), custom_call_target="tpu_custom_call" | custom-call | flops 40000000000 | bytes 12582912 | tf_op jit(solution)/shard_map/attend_back/pallas_call | solution.py:187
  764.7 2.9 fusion.34
  768.0 2.8 fusion.153
  771.8 5.4 fusion.132
  782.1 10.9 %fusion.144 = f32[768,3072]{1,0:T(8,128)} fusion(bf16[1024,3072]{1,0:T(8,128)(2,1)} %copy-done.26, f32[1024,768]{1,0:T(8,128)S(1)} %copy-done.11, f32[768]{0:T(1024)S(1)} %add.323, f32[768]{0:T(1024)S(1)} %mul.203, f32[1024]{0:T(1024)S(1)} %add_rsqrt_fusion.1, f32[1024]{0:T(1024)S(1)} %broadcast_multiply_fusion.4), kind=kOutput, calls=%fused_computation.270 | convolution fusion | flops 4835770368 | bytes 18888704 | tf_op jit(solution)/shard_map/dot_general | solution.py:43
  793.0 7.6 fusion.135
  800.7 5.1 all-to-all-start.1
  805.8 3.5 fusion.152
  810.0 2.8 copy-done.15
  833.1 4.3 fusion.22
  839.0 2.3 fusion.142
  841.3 2.2 copy-done.33
  843.5 3.1 fusion.85
  846.6 3.1 fusion.84
  849.7 2.3 fusion.129
  853.7 3.1 fusion.36
  861.4 4.0 fusion.23
  865.9 8.4 add_convert_fusion
  874.3 5.3 all-to-all-start.3
  879.5 2.7 collective-permute-done.29
  885.8 4.4 bitcast_add_fusion.2
  893.2 3.0 collective-permute-done.30
  896.2 2.1 collective-permute-start.31
  898.4 2.4 bitcast_add_fusion.1
  904.8 11.9 %all-to-all-done.3 = bf16[4,256,768]{2,1,0:T(8,128)(2,1)S(1)} async-done(((bf16[4,256,768]{2,1,0:T(8,128)(2,1)}), bf16[4,256,768]{2,1,0:T(8,128)(2,1)S(1)}, u32[]{:S(2)}, u32[]{:S(2)}) %all-to-all-start.3) | async-done | bytes 1572896 | tf_op jit(solution)/shard_map/all_to_all | solution.py:454
  916.9 3.9 bitcast_add_fusion
  920.8 2.2 collective-permute-done.32
  925.3 5.4 collective-permute-done.33
  937.4 21.4 %collective-permute-done.36 = bf16[2,400,768]{2,1,0:T(8,128)(2,1)S(1)} collective-permute-done((bf16[2,400,768]{2,1,0:T(8,128)(2,1)S(1)}, bf16[2,400,768]{2,1,0:T(8,128)(2,1)S(1)}, u32[]{:S(2)}, u32[]{:S(2)}) %collective-permute-start.36) | collective-permute-done | bytes 1228832 | tf_op jit(solution)/shard_map/ppermute | solution.py:330
  961.8 7.1 collective-permute-done.44
  974.9 5.9 collective-permute-done.45
  982.9 7.4 collective-permute-done.52
  993.0 3.4 collective-permute-start.47
  996.4 10.3 collective-permute-done.53
  1007.0 3.0 collective-permute-start.39
  1011.0 9.2 collective-permute-done.39
  1020.4 2.6 collective-permute-start.55
  1023.1 4.8 collective-permute-done.40
  1029.3 3.4 collective-permute-done.55
  1033.9 2.6 collective-permute-done.41
  1037.8 2.1 slice.166
  1044.4 2.7 copy.61
  (449 shorter events, 127.9 us)
Async XLA Ops:
  0.6 14.2 %collective-permute-start.10 = (bf16[288,768]{1,0:T(8,128)(2,1)}, bf16[288,768]{1,0:T(8,128)(2,1)S(1)}, u32[]{:S(2)}, u32[]{:S(2)}) collective-permute-start(bf16[288,768]{1,0:T(8,128)(2,1)} %bitcast.405), channel_id=1, source_target_pairs={{0,16},{4,20},{8,24},{12,28},{16,0},{20,4},{24,8},{28,12},{1,17},{... | collective-permute-start | bytes 1327112 | tf_op jit(solution)/shard_map/ppermute | solution.py:330
  3.7 13.3 %collective-permute-start.7 = (bf16[288,768]{1,0:T(8,128)(2,1)}, bf16[288,768]{1,0:T(8,128)(2,1)S(1)}, u32[]{:S(2)}, u32[]{:S(2)}) collective-permute-start(bf16[288,768]{1,0:T(8,128)(2,1)} %bitcast.406), channel_id=1, source_target_pairs={{0,4},{4,0},{8,12},{12,8},{16,20},{20,16},{24,28},{28,24},{1,5},{5... | collective-permute-start | bytes 1327112 | tf_op jit(solution)/shard_map/ppermute | solution.py:330
  3.7 13.3 %collective-permute-start.8 = (bf16[288,768]{1,0:T(8,128)(2,1)}, bf16[288,768]{1,0:T(8,128)(2,1)}, u32[]{:S(2)}, u32[]{:S(2)}) collective-permute-start(bf16[288,768]{1,0:T(8,128)(2,1)} %bitcast.407), channel_id=1, source_target_pairs={{0,8},{4,12},{8,0},{12,4},{16,24},{20,28},{24,16},{28,20},{1,9},{5... | collective-permute-start | bytes 1327112 | tf_op jit(solution)/shard_map/ppermute | solution.py:330
  9.4 171.9 %copy-start.37 = (bf16[400,768]{1,0:T(8,128)(2,1)}, bf16[400,768]{1,0:T(8,128)(2,1)S(1)}, u32[]{:S(2)}) copy-start(bf16[400,768]{1,0:T(8,128)(2,1)S(1)} %pad_maximum_fusion.2.refs_0_) | copy-start | bytes 1843204
  9.4 17.8 %collective-permute-start.3 = (bf16[400,768]{1,0:T(8,128)(2,1)S(1)}, bf16[400,768]{1,0:T(8,128)(2,1)S(1)}, u32[]{:S(2)}, u32[]{:S(2)}) collective-permute-start(bf16[400,768]{1,0:T(8,128)(2,1)S(1)} %pad_maximum_fusion.2.refs_0_), channel_id=1, source_target_pairs={{0,16},{4,20},{8,24},{12,28},{16,0},{20,4},{24,8},{28,12},{1,17},{... | collective-permute-start | bytes 1843208 | tf_op jit(solution)/shard_map/ppermute | solution.py:330
  10.0 19.0 %collective-permute-start = (bf16[400,768]{1,0:T(8,128)(2,1)S(1)}, bf16[400,768]{1,0:T(8,128)(2,1)S(1)}, u32[]{:S(2)}, u32[]{:S(2)}) collective-permute-start(bf16[400,768]{1,0:T(8,128)(2,1)S(1)} %pad_maximum_fusion.2.refs_0_), channel_id=1, source_target_pairs={{0,4},{4,0},{8,12},{12,8},{16,20},{20,16},{24,28},{28,24},{1,5},{5... | collective-permute-start | bytes 1843208 | tf_op jit(solution)/shard_map/ppermute | solution.py:330
  14.9 15.2 %collective-permute-start.1 = (bf16[400,768]{1,0:T(8,128)(2,1)S(1)}, bf16[400,768]{1,0:T(8,128)(2,1)S(1)}, u32[]{:S(2)}, u32[]{:S(2)}) collective-permute-start(bf16[400,768]{1,0:T(8,128)(2,1)S(1)} %pad_maximum_fusion.2.refs_0_), channel_id=1, source_target_pairs={{0,8},{4,12},{8,0},{12,4},{16,24},{20,28},{24,16},{28,20},{1,9},{5... | collective-permute-start | bytes 1843208 | tf_op jit(solution)/shard_map/ppermute | solution.py:330
  17.0 14.7 %collective-permute-start.9 = (bf16[288,768]{1,0:T(8,128)(2,1)}, bf16[288,768]{1,0:T(8,128)(2,1)S(1)}, u32[]{:S(2)}, u32[]{:S(2)}) collective-permute-start(bf16[288,768]{1,0:T(8,128)(2,1)} %collective-permute-done.8.refs_2_), channel_id=1, source_target_pairs={{0,4},{4,0},{8,12},{12,8},{16,20},{20,16},{24,28},{28,24},{1,5},{5... | collective-permute-start | bytes 1327112 | tf_op jit(solution)/shard_map/ppermute | solution.py:330
  17.0 15.3 %collective-permute-start.11 = (bf16[288,768]{1,0:T(8,128)(2,1)S(1)}, bf16[288,768]{1,0:T(8,128)(2,1)S(1)}, u32[]{:S(2)}, u32[]{:S(2)}) collective-permute-start(bf16[288,768]{1,0:T(8,128)(2,1)S(1)} %collective-permute-done.10.refs_4_), channel_id=1, source_target_pairs={{0,4},{4,0},{8,12},{12,8},{16,20},{20,16},{24,28},{28,24},{1,5},{5... | collective-permute-start | bytes 1327112 | tf_op jit(solution)/shard_map/ppermute | solution.py:330
  27.2 154.1 %copy-start.42 = (bf16[400,768]{1,0:T(8,128)(2,1)}, bf16[400,768]{1,0:T(8,128)(2,1)S(1)}, u32[]{:S(2)}) copy-start(bf16[400,768]{1,0:T(8,128)(2,1)S(1)} %collective-permute-done.3.refs_4_) | copy-start | bytes 1843204
  27.2 18.5 %collective-permute-start.5 = (bf16[400,768]{1,0:T(8,128)(2,1)S(1)}, bf16[400,768]{1,0:T(8,128)(2,1)}, u32[]{:S(2)}, u32[]{:S(2)}) collective-permute-start(bf16[400,768]{1,0:T(8,128)(2,1)S(1)} %collective-permute-done.3.refs_4_), channel_id=1, source_target_pairs={{0,8},{4,12},{8,0},{12,4},{16,24},{20,28},{24,16},{28,20},{1,9},{5... | collective-permute-start | bytes 1843208 | tf_op jit(solution)/shard_map/ppermute | solution.py:330
  28.9 16.3 %collective-permute-start.14 = (bf16[96,3072]{1,0:T(8,128)(2,1)}, bf16[96,3072]{1,0:T(8,128)(2,1)}, u32[]{:S(2)}, u32[]{:S(2)}) collective-permute-start(bf16[96,3072]{1,0:T(8,128)(2,1)} %refs_0_), channel_id=1, source_target_pairs={{0,4},{4,0},{8,12},{12,8},{16,20},{20,16},{24,28},{28,24},{1,5},{5... | collective-permute-start | bytes 1769480 | tf_op jit(solution)/shard_map/ppermute | solution.py:330
  30.1 25.4 %collective-permute-start.15 = (bf16[96,3072]{1,0:T(8,128)(2,1)}, bf16[96,3072]{1,0:T(8,128)(2,1)}, u32[]{:S(2)}, u32[]{:S(2)}) collective-permute-start(bf16[96,3072]{1,0:T(8,128)(2,1)} %refs_0_), channel_id=1, source_target_pairs={{0,8},{4,12},{8,0},{12,4},{16,24},{20,28},{24,16},{28,20},{1,9},{5... | collective-permute-start | bytes 1769480 | tf_op jit(solution)/shard_map/ppermute | solution.py:330
  31.7 13.5 %collective-permute-start.12 = (bf16[288,768]{1,0:T(8,128)(2,1)}, bf16[288,768]{1,0:T(8,128)(2,1)}, u32[]{:S(2)}, u32[]{:S(2)}) collective-permute-start(bf16[288,768]{1,0:T(8,128)(2,1)} %collective-permute-done.8.refs_2_), channel_id=1, source_target_pairs={{0,16},{4,20},{8,24},{12,28},{16,0},{20,4},{24,8},{28,12},{1,17},{... | collective-permute-start | bytes 1327112 | tf_op jit(solution)/shard_map/ppermute | solution.py:330
  33.3 23.3 %collective-permute-start.17 = (bf16[96,3072]{1,0:T(8,128)(2,1)}, bf16[96,3072]{1,0:T(8,128)(2,1)}, u32[]{:S(2)}, u32[]{:S(2)}) collective-permute-start(bf16[96,3072]{1,0:T(8,128)(2,1)} %refs_0_), channel_id=1, source_target_pairs={{0,16},{4,20},{8,24},{12,28},{16,0},{20,4},{24,8},{28,12},{1,17},{... | collective-permute-start | bytes 1769480 | tf_op jit(solution)/shard_map/ppermute | solution.py:330
  34.6 592.5 %all-to-all-start = ((bf16[4,256,768]{2,1,0:T(8,128)(2,1)}), bf16[4,256,768]{2,1,0:T(8,128)(2,1)S(1)}, u32[]{:S(2)}, u32[]{:S(2)}) async-start(bf16[4,256,768]{2,1,0:T(8,128)(2,1)} %param.14), calls=%async_computation | async-start | bytes 3145728 | tf_op jit(solution)/shard_map/all_to_all | solution.py:448
  45.2 26.1 %collective-permute-start.2 = (bf16[400,768]{1,0:T(8,128)(2,1)}, bf16[400,768]{1,0:T(8,128)(2,1)}, u32[]{:S(2)}, u32[]{:S(2)}) collective-permute-start(bf16[400,768]{1,0:T(8,128)(2,1)} %copy-done.44), channel_id=1, source_target_pairs={{0,4},{4,0},{8,12},{12,8},{16,20},{20,16},{24,28},{28,24},{1,5},{5... | collective-permute-start | bytes 1843208 | tf_op jit(solution)/shard_map/ppermute | solution.py:330
  45.2 26.1 %collective-permute-start.4 = (bf16[400,768]{1,0:T(8,128)(2,1)S(1)}, bf16[400,768]{1,0:T(8,128)(2,1)}, u32[]{:S(2)}, u32[]{:S(2)}) collective-permute-start(bf16[400,768]{1,0:T(8,128)(2,1)S(1)} %collective-permute-done.3.refs_4_), channel_id=1, source_target_pairs={{0,4},{4,0},{8,12},{12,8},{16,20},{20,16},{24,28},{28,24},{1,5},{5... | collective-permute-start | bytes 1843208 | tf_op jit(solution)/shard_map/ppermute | solution.py:330
  45.7 26.3 %collective-permute-start.6 = (bf16[400,768]{1,0:T(8,128)(2,1)}, bf16[400,768]{1,0:T(8,128)(2,1)}, u32[]{:S(2)}, u32[]{:S(2)}) collective-permute-start(bf16[400,768]{1,0:T(8,128)(2,1)} %collective-permute-done.5.refs_6_), channel_id=1, source_target_pairs={{0,4},{4,0},{8,12},{12,8},{16,20},{20,16},{24,28},{28,24},{1,5},{5... | collective-permute-start | bytes 1843208 | tf_op jit(solution)/shard_map/ppermute | solution.py:330
  55.5 14.4 %collective-permute-start.24 = (bf16[384,768]{1,0:T(8,128)(2,1)}, bf16[384,768]{1,0:T(8,128)(2,1)}, u32[]{:S(2)}, u32[]{:S(2)}) collective-permute-start(bf16[384,768]{1,0:T(8,128)(2,1)} %refs_0_.1), channel_id=1, source_target_pairs={{0,16},{4,20},{8,24},{12,28},{16,0},{20,4},{24,8},{28,12},{1,17},{... | collective-permute-start | bytes 1769480 | tf_op jit(solution)/shard_map/ppermute | solution.py:330
  56.5 15.3 %collective-permute-start.13 = (bf16[288,768]{1,0:T(8,128)(2,1)}, bf16[288,768]{1,0:T(8,128)(2,1)}, u32[]{:S(2)}, u32[]{:S(2)}) collective-permute-start(bf16[288,768]{1,0:T(8,128)(2,1)} %collective-permute-done.12.refs_6_), channel_id=1, source_target_pairs={{0,4},{4,0},{8,12},{12,8},{16,20},{20,16},{24,28},{28,24},{1,5},{5... | collective-permute-start | bytes 1327112 | tf_op jit(solution)/shard_map/ppermute | solution.py:330
  57.2 669.6 %copy-start.66 = (s32[4]{0:T(128)}, s32[4]{0:T(128)S(1)}, u32[]{:S(2)}) copy-start(s32[4]{0:T(128)S(1)} %get-tuple-element.86) | copy-start | bytes 52
  70.0 263.0 %collective-permute-start.22 = (bf16[384,768]{1,0:T(8,128)(2,1)}, bf16[384,768]{1,0:T(8,128)(2,1)}, u32[]{:S(2)}, u32[]{:S(2)}) collective-permute-start(bf16[384,768]{1,0:T(8,128)(2,1)} %refs_0_.1), channel_id=1, source_target_pairs={{0,8},{4,12},{8,0},{12,4},{16,24},{20,28},{24,16},{28,20},{1,9},{5... | collective-permute-start | bytes 1769480 | tf_op jit(solution)/shard_map/ppermute | solution.py:330
  71.3 261.7 %collective-permute-start.16 = (bf16[96,3072]{1,0:T(8,128)(2,1)}, bf16[96,3072]{1,0:T(8,128)(2,1)}, u32[]{:S(2)}, u32[]{:S(2)}) collective-permute-start(bf16[96,3072]{1,0:T(8,128)(2,1)} %collective-permute-done.15.refs_2_), channel_id=1, source_target_pairs={{0,4},{4,0},{8,12},{12,8},{16,20},{20,16},{24,28},{28,24},{1,5},{5... | collective-permute-start | bytes 1769480 | tf_op jit(solution)/shard_map/ppermute | solution.py:330
  71.3 262.3 %collective-permute-start.19 = (bf16[96,3072]{1,0:T(8,128)(2,1)}, bf16[96,3072]{1,0:T(8,128)(2,1)}, u32[]{:S(2)}, u32[]{:S(2)}) collective-permute-start(bf16[96,3072]{1,0:T(8,128)(2,1)} %collective-permute-done.15.refs_2_), channel_id=1, source_target_pairs={{0,16},{4,20},{8,24},{12,28},{16,0},{20,4},{24,8},{28,12},{1,17},{... | collective-permute-start | bytes 1769480 | tf_op jit(solution)/shard_map/ppermute | solution.py:330
  71.8 261.7 %collective-permute-start.18 = (bf16[96,3072]{1,0:T(8,128)(2,1)}, bf16[96,3072]{1,0:T(8,128)(2,1)}, u32[]{:S(2)}, u32[]{:S(2)}) collective-permute-start(bf16[96,3072]{1,0:T(8,128)(2,1)} %collective-permute-done.17.refs_4_), channel_id=1, source_target_pairs={{0,4},{4,0},{8,12},{12,8},{16,20},{20,16},{24,28},{28,24},{1,5},{5... | collective-permute-start | bytes 1769480 | tf_op jit(solution)/shard_map/ppermute | solution.py:330
  72.0 262.0 %collective-permute-start.26 = (bf16[384,768]{1,0:T(8,128)(2,1)}, bf16[384,768]{1,0:T(8,128)(2,1)}, u32[]{:S(2)}, u32[]{:S(2)}) collective-permute-start(bf16[384,768]{1,0:T(8,128)(2,1)} %collective-permute-done.24.refs_4_), channel_id=1, source_target_pairs={{0,8},{4,12},{8,0},{12,4},{16,24},{20,28},{24,16},{28,20},{1,9},{5... | collective-permute-start | bytes 1769480 | tf_op jit(solution)/shard_map/ppermute | solution.py:330
  332.9 149.0 %collective-permute-start.21 = (bf16[384,768]{1,0:T(8,128)(2,1)}, bf16[384,768]{1,0:T(8,128)(2,1)S(1)}, u32[]{:S(2)}, u32[]{:S(2)}) collective-permute-start(bf16[384,768]{1,0:T(8,128)(2,1)} %refs_0_.1), channel_id=1, source_target_pairs={{0,4},{4,0},{8,12},{12,8},{16,20},{20,16},{24,28},{28,24},{1,5},{5... | collective-permute-start | bytes 1769480 | tf_op jit(solution)/shard_map/ppermute | solution.py:330
  333.0 149.0 %collective-permute-start.25 = (bf16[384,768]{1,0:T(8,128)(2,1)}, bf16[384,768]{1,0:T(8,128)(2,1)S(1)}, u32[]{:S(2)}, u32[]{:S(2)}) collective-permute-start(bf16[384,768]{1,0:T(8,128)(2,1)} %collective-permute-done.24.refs_4_), channel_id=1, source_target_pairs={{0,4},{4,0},{8,12},{12,8},{16,20},{20,16},{24,28},{28,24},{1,5},{5... | collective-permute-start | bytes 1769480 | tf_op jit(solution)/shard_map/ppermute | solution.py:330
  333.5 148.5 %collective-permute-start.23 = (bf16[384,768]{1,0:T(8,128)(2,1)}, bf16[384,768]{1,0:T(8,128)(2,1)}, u32[]{:S(2)}, u32[]{:S(2)}) collective-permute-start(bf16[384,768]{1,0:T(8,128)(2,1)} %collective-permute-done.22.refs_2_), channel_id=1, source_target_pairs={{0,4},{4,0},{8,12},{12,8},{16,20},{20,16},{24,28},{28,24},{1,5},{5... | collective-permute-start | bytes 1769480 | tf_op jit(solution)/shard_map/ppermute | solution.py:330
  333.6 4.3 collective-permute-start.20
  334.0 148.0 %collective-permute-start.27 = (bf16[384,768]{1,0:T(8,128)(2,1)}, bf16[384,768]{1,0:T(8,128)(2,1)}, u32[]{:S(2)}, u32[]{:S(2)}) collective-permute-start(bf16[384,768]{1,0:T(8,128)(2,1)} %collective-permute-done.26.refs_6_), channel_id=1, source_target_pairs={{0,4},{4,0},{8,12},{12,8},{16,20},{20,16},{24,28},{28,24},{1,5},{5... | collective-permute-start | bytes 1769480 | tf_op jit(solution)/shard_map/ppermute | solution.py:330
  627.1 65.9 %all-to-all-start.2 = ((bf16[4,256,768]{2,1,0:T(8,128)(2,1)}), bf16[4,256,768]{2,1,0:T(8,128)(2,1)}, u32[]{:S(2)}, u32[]{:S(2)}) async-start(bf16[4,256,768]{2,1,0:T(8,128)(2,1)} %param.25), calls=%async_computation.2 | async-start | bytes 3145728 | tf_op jit(solution)/shard_map/all_to_all | solution.py:448
  637.4 141.3 %copy-start.64 = (f32[64]{0:T(128)}, f32[64]{0:T(128)S(1)}, u32[]{:S(2)}) copy-start(f32[64]{0:T(128)S(1)} %get-tuple-element.88) | copy-start | bytes 772
  800.7 73.6 %all-to-all-start.1 = ((bf16[4,256,768]{2,1,0:T(8,128)(2,1)}), bf16[4,256,768]{2,1,0:T(8,128)(2,1)}, u32[]{:S(2)}, u32[]{:S(2)}) async-start(bf16[4,256,768]{2,1,0:T(8,128)(2,1)} %bitcast.379), calls=%async_computation.1 | async-start | bytes 3145728 | tf_op jit(solution)/shard_map/all_to_all | solution.py:454
  814.2 42.6 %collective-permute-start.28 = (bf16[2,2,288,768]{3,2,1,0:T(8,128)(2,1)}, bf16[2,2,288,768]{3,2,1,0:T(8,128)(2,1)}, u32[]{:S(2)}, u32[]{:S(2)}) collective-permute-start(bf16[2,2,288,768]{3,2,1,0:T(8,128)(2,1)} %fusion.24), channel_id=1, source_target_pairs={{0,4},{4,0},{8,12},{12,8},{16,20},{20,16},{24,28},{28,24},{1,5},{5... | collective-permute-start | bytes 5308424 | tf_op jit(solution)/shard_map/ppermute | solution.py:330
  837.4 48.4 %collective-permute-start.42 = (bf16[2,2,96,3072]{3,2,1,0:T(8,128)(2,1)}, bf16[2,2,96,3072]{3,2,1,0:T(8,128)(2,1)}, u32[]{:S(2)}, u32[]{:S(2)}) collective-permute-start(bf16[2,2,96,3072]{3,2,1,0:T(8,128)(2,1)} %fusion.22), channel_id=1, source_target_pairs={{0,4},{4,0},{8,12},{12,8},{16,20},{20,16},{24,28},{28,24},{1,5},{5... | collective-permute-start | bytes 7077896 | tf_op jit(solution)/shard_map/ppermute | solution.py:330
  853.7 63.2 %collective-permute-start.35 = (bf16[2,2,400,768]{3,2,1,0:T(8,128)(2,1)}, bf16[2,2,400,768]{3,2,1,0:T(8,128)(2,1)}, u32[]{:S(2)}, u32[]{:S(2)}) collective-permute-start(bf16[2,2,400,768]{3,2,1,0:T(8,128)(2,1)} %fusion.21), channel_id=1, source_target_pairs={{0,4},{4,0},{8,12},{12,8},{16,20},{20,16},{24,28},{28,24},{1,5},{5... | collective-permute-start | bytes 7372808 | tf_op jit(solution)/shard_map/ppermute | solution.py:330
  859.9 22.4 %collective-permute-start.29 = (bf16[2,288,768]{2,1,0:T(8,128)(2,1)}, bf16[2,288,768]{2,1,0:T(8,128)(2,1)}, u32[]{:S(2)}, u32[]{:S(2)}) collective-permute-start(bf16[2,288,768]{2,1,0:T(8,128)(2,1)} %fusion.93), channel_id=1, source_target_pairs={{0,16},{4,20},{8,24},{12,28},{16,0},{20,4},{24,8},{28,12},{1,17},{... | collective-permute-start | bytes 2654216 | tf_op jit(solution)/shard_map/ppermute | solution.py:330
  865.4 32.9 %collective-permute-start.49 = (bf16[2,2,384,768]{3,2,1,0:T(8,128)(2,1)}, bf16[2,2,384,768]{3,2,1,0:T(8,128)(2,1)}, u32[]{:S(2)}, u32[]{:S(2)}) collective-permute-start(bf16[2,2,384,768]{3,2,1,0:T(8,128)(2,1)} %fusion.23), channel_id=1, source_target_pairs={{0,4},{4,0},{8,12},{12,8},{16,20},{20,16},{24,28},{28,24},{1,5},{5... | collective-permute-start | bytes 7077896 | tf_op jit(solution)/shard_map/ppermute | solution.py:330
  874.3 42.4 %all-to-all-start.3 = ((bf16[4,256,768]{2,1,0:T(8,128)(2,1)}), bf16[4,256,768]{2,1,0:T(8,128)(2,1)S(1)}, u32[]{:S(2)}, u32[]{:S(2)}) async-start(bf16[4,256,768]{2,1,0:T(8,128)(2,1)} %bitcast.380), calls=%async_computation.3 | async-start | bytes 3145728 | tf_op jit(solution)/shard_map/all_to_all | solution.py:454
  884.3 11.9 %collective-permute-start.30 = (bf16[288,768]{1,0:T(8,128)(2,1)S(1)}, bf16[288,768]{1,0:T(8,128)(2,1)S(1)}, u32[]{:S(2)}, u32[]{:S(2)}) collective-permute-start(bf16[288,768]{1,0:T(8,128)(2,1)S(1)} %fusion.99), channel_id=1, source_target_pairs={{0,8},{4,12},{8,0},{12,4},{16,24},{20,28},{24,16},{28,20},{1,9},{5... | collective-permute-start | bytes 1327112 | tf_op jit(solution)/shard_map/ppermute | solution.py:330
  891.6 39.3 %collective-permute-start.43 = (bf16[2,96,3072]{2,1,0:T(8,128)(2,1)}, bf16[2,96,3072]{2,1,0:T(8,128)(2,1)}, u32[]{:S(2)}, u32[]{:S(2)}) collective-permute-start(bf16[2,96,3072]{2,1,0:T(8,128)(2,1)} %fusion.38), channel_id=1, source_target_pairs={{0,16},{4,20},{8,24},{12,28},{16,0},{20,4},{24,8},{28,12},{1,17},{... | collective-permute-start | bytes 3538952 | tf_op jit(solution)/shard_map/ppermute | solution.py:330
  896.2 20.5 %collective-permute-start.31 = (bf16[2,72,768]{2,1,0:T(8,128)(2,1)S(1)}, bf16[2,72,768]{2,1,0:T(8,128)(2,1)S(1)}, u32[]{:S(2)}, u32[]{:S(2)}) collective-permute-start(bf16[2,72,768]{2,1,0:T(8,128)(2,1)S(1)} %fusion.110), channel_id=1, source_target_pairs={{0,1},{1,0},{2,3},{3,2},{4,5},{5,4},{6,7},{7,6},{8,9},{9,8},{10,11... | collective-permute-start | bytes 663560 | tf_op jit(solution)/shard_map/ppermute | solution.py:330
  903.3 30.8 %collective-permute-start.50 = (bf16[2,384,768]{2,1,0:T(8,128)(2,1)}, bf16[2,384,768]{2,1,0:T(8,128)(2,1)}, u32[]{:S(2)}, u32[]{:S(2)}) collective-permute-start(bf16[2,384,768]{2,1,0:T(8,128)(2,1)} %fusion.39), channel_id=1, source_target_pairs={{0,8},{4,12},{8,0},{12,4},{16,24},{20,28},{24,16},{28,20},{1,9},{5... | collective-permute-start | bytes 3538952 | tf_op jit(solution)/shard_map/ppermute | solution.py:330
  916.8 6.2 collective-permute-start.32
  923.1 7.7 collective-permute-start.33
  923.8 35.0 %collective-permute-start.36 = (bf16[2,400,768]{2,1,0:T(8,128)(2,1)S(1)}, bf16[2,400,768]{2,1,0:T(8,128)(2,1)S(1)}, u32[]{:S(2)}, u32[]{:S(2)}) collective-permute-start(bf16[2,400,768]{2,1,0:T(8,128)(2,1)S(1)} %fusion.33), channel_id=1, source_target_pairs={{0,8},{4,12},{8,0},{12,4},{16,24},{20,28},{24,16},{28,20},{1,9},{5... | collective-permute-start | bytes 3686408 | tf_op jit(solution)/shard_map/ppermute | solution.py:330
  930.8 29.9 %collective-permute-start.34 = (bf16[2,72,768]{2,1,0:T(8,128)(2,1)S(1)}, bf16[2,72,768]{2,1,0:T(8,128)(2,1)S(1)}, u32[]{:S(2)}, u32[]{:S(2)}) collective-permute-start(bf16[2,72,768]{2,1,0:T(8,128)(2,1)S(1)} %pad_maximum_fusion.9), channel_id=1, source_target_pairs={{0,1},{1,0},{2,3},{3,2},{4,5},{5,4},{6,7},{7,6},{8,9},{9,8},{10,11... | collective-permute-start | bytes 663560 | tf_op jit(solution)/shard_map/ppermute | solution.py:330
  932.5 36.4 %collective-permute-start.44 = (bf16[96,3072]{1,0:T(8,128)(2,1)S(1)}, bf16[96,3072]{1,0:T(8,128)(2,1)S(1)}, u32[]{:S(2)}, u32[]{:S(2)}) collective-permute-start(bf16[96,3072]{1,0:T(8,128)(2,1)S(1)} %fusion.97), channel_id=1, source_target_pairs={{0,8},{4,12},{8,0},{12,4},{16,24},{20,28},{24,16},{28,20},{1,9},{5... | collective-permute-start | bytes 1769480 | tf_op jit(solution)/shard_map/ppermute | solution.py:330
  935.8 33.7 %collective-permute-start.51 = (bf16[384,768]{1,0:T(8,128)(2,1)S(1)}, bf16[384,768]{1,0:T(8,128)(2,1)S(1)}, u32[]{:S(2)}, u32[]{:S(2)}) collective-permute-start(bf16[384,768]{1,0:T(8,128)(2,1)S(1)} %fusion.98), channel_id=1, source_target_pairs={{0,16},{4,20},{8,24},{12,28},{16,0},{20,4},{24,8},{28,12},{1,17},{... | collective-permute-start | bytes 1769480 | tf_op jit(solution)/shard_map/ppermute | solution.py:330
  959.1 12.4 %collective-permute-start.37 = (bf16[400,768]{1,0:T(8,128)(2,1)S(1)}, bf16[400,768]{1,0:T(8,128)(2,1)S(1)}, u32[]{:S(2)}, u32[]{:S(2)}) collective-permute-start(bf16[400,768]{1,0:T(8,128)(2,1)S(1)} %fusion.96), channel_id=1, source_target_pairs={{0,16},{4,20},{8,24},{12,28},{16,0},{20,4},{24,8},{28,12},{1,17},{... | collective-permute-start | bytes 1843208 | tf_op jit(solution)/shard_map/ppermute | solution.py:330
  969.1 11.7 %collective-permute-start.45 = (bf16[2,24,3072]{2,1,0:T(8,128)(2,1)S(1)}, bf16[2,24,3072]{2,1,0:T(8,128)(2,1)}, u32[]{:S(2)}, u32[]{:S(2)}) collective-permute-start(bf16[2,24,3072]{2,1,0:T(8,128)(2,1)S(1)} %fusion.102), channel_id=1, source_target_pairs={{0,1},{1,0},{2,3},{3,2},{4,5},{5,4},{6,7},{7,6},{8,9},{9,8},{10,11... | collective-permute-start | bytes 884744 | tf_op jit(solution)/shard_map/ppermute | solution.py:330
  969.7 20.6 %collective-permute-start.52 = (bf16[2,96,768]{2,1,0:T(8,128)(2,1)S(1)}, bf16[2,96,768]{2,1,0:T(8,128)(2,1)}, u32[]{:S(2)}, u32[]{:S(2)}) collective-permute-start(bf16[2,96,768]{2,1,0:T(8,128)(2,1)S(1)} %fusion.103), channel_id=1, source_target_pairs={{0,1},{1,0},{2,3},{3,2},{4,5},{5,4},{6,7},{7,6},{8,9},{9,8},{10,11... | collective-permute-start | bytes 884744 | tf_op jit(solution)/shard_map/ppermute | solution.py:330
  974.0 32.9 %collective-permute-start.38 = (bf16[2,100,768]{2,1,0:T(8,128)(2,1)S(1)}, bf16[2,100,768]{2,1,0:T(8,128)(2,1)S(1)}, u32[]{:S(2)}, u32[]{:S(2)}) collective-permute-start(bf16[2,100,768]{2,1,0:T(8,128)(2,1)S(1)} %fusion.100), channel_id=1, source_target_pairs={{0,1},{1,0},{2,3},{3,2},{4,5},{5,4},{6,7},{7,6},{8,9},{9,8},{10,11... | collective-permute-start | bytes 921608 | tf_op jit(solution)/shard_map/ppermute | solution.py:330
  982.0 10.9 %collective-permute-start.46 = (bf16[24,3072]{1,0:T(8,128)(2,1)S(1)}, bf16[24,3072]{1,0:T(8,128)(2,1)S(1)}, u32[]{:S(2)}, u32[]{:S(2)}) collective-permute-start(bf16[24,3072]{1,0:T(8,128)(2,1)S(1)} %fusion.113), channel_id=1, source_target_pairs={{0,2},{1,3},{2,0},{3,1},{4,6},{5,7},{6,4},{7,5},{8,10},{9,11},{10,... | collective-permute-start | bytes 442376 | tf_op jit(solution)/shard_map/ppermute | solution.py:330
  991.5 15.2 %collective-permute-start.53 = (bf16[96,768]{1,0:T(8,128)(2,1)S(1)}, bf16[96,768]{1,0:T(8,128)(2,1)S(1)}, u32[]{:S(2)}, u32[]{:S(2)}) collective-permute-start(bf16[96,768]{1,0:T(8,128)(2,1)S(1)} %fusion.114), channel_id=1, source_target_pairs={{0,2},{1,3},{2,0},{3,1},{4,6},{5,7},{6,4},{7,5},{8,10},{9,11},{10,... | collective-permute-start | bytes 442376 | tf_op jit(solution)/shard_map/ppermute | solution.py:330
  993.0 17.9 %collective-permute-start.47 = (bf16[24,3072]{1,0:T(8,128)(2,1)S(1)}, bf16[24,3072]{1,0:T(8,128)(2,1)S(1)}, u32[]{:S(2)}, u32[]{:S(2)}) collective-permute-start(bf16[24,3072]{1,0:T(8,128)(2,1)S(1)} %fusion.105), channel_id=1, source_target_pairs={{0,2},{1,3},{2,0},{3,1},{4,6},{5,7},{6,4},{7,5},{8,10},{9,11},{10,... | collective-permute-start | bytes 442376 | tf_op jit(solution)/shard_map/ppermute | solution.py:330
  1006.8 13.5 %collective-permute-start.54 = (bf16[96,768]{1,0:T(8,128)(2,1)S(1)}, bf16[96,768]{1,0:T(8,128)(2,1)S(1)}, u32[]{:S(2)}, u32[]{:S(2)}) collective-permute-start(bf16[96,768]{1,0:T(8,128)(2,1)S(1)} %fusion.104), channel_id=1, source_target_pairs={{0,2},{1,3},{2,0},{3,1},{4,6},{5,7},{6,4},{7,5},{8,10},{9,11},{10,... | collective-permute-start | bytes 442376 | tf_op jit(solution)/shard_map/ppermute | solution.py:330
  1007.0 13.2 %collective-permute-start.39 = (bf16[100,768]{1,0:T(8,128)(2,1)S(1)}, bf16[100,768]{1,0:T(8,128)(2,1)S(1)}, u32[]{:S(2)}, u32[]{:S(2)}) collective-permute-start(bf16[100,768]{1,0:T(8,128)(2,1)S(1)} %fusion.112), channel_id=1, source_target_pairs={{0,2},{1,3},{2,0},{3,1},{4,6},{5,7},{6,4},{7,5},{8,10},{9,11},{10,... | collective-permute-start | bytes 460808 | tf_op jit(solution)/shard_map/ppermute | solution.py:330
  1011.0 17.0 %collective-permute-start.48 = (bf16[2,24,3072]{2,1,0:T(8,128)(2,1)S(1)}, bf16[2,24,3072]{2,1,0:T(8,128)(2,1)S(1)}, u32[]{:S(2)}, u32[]{:S(2)}) collective-permute-start(bf16[2,24,3072]{2,1,0:T(8,128)(2,1)S(1)} %pad_maximum_fusion.7), channel_id=1, source_target_pairs={{0,1},{1,0},{2,3},{3,2},{4,5},{5,4},{6,7},{7,6},{8,9},{9,8},{10,11... | collective-permute-start | bytes 884744 | tf_op jit(solution)/shard_map/ppermute | solution.py:330
  1020.3 7.6 collective-permute-start.40
  1020.4 12.3 %collective-permute-start.55 = (bf16[2,96,768]{2,1,0:T(8,128)(2,1)S(1)}, bf16[2,96,768]{2,1,0:T(8,128)(2,1)S(1)}, u32[]{:S(2)}, u32[]{:S(2)}) collective-permute-start(bf16[2,96,768]{2,1,0:T(8,128)(2,1)S(1)} %pad_maximum_fusion.8), channel_id=1, source_target_pairs={{0,1},{1,0},{2,3},{3,2},{4,5},{5,4},{6,7},{7,6},{8,9},{9,8},{10,11... | collective-permute-start | bytes 884744 | tf_op jit(solution)/shard_map/ppermute | solution.py:330
  1027.9 8.6 collective-permute-start.41
  (89 other events, 791.7 us)
